TPU v7x, 32 devices: a whole 2x2x4 slice. The times are simulated.
32 devices in a mesh: grp: 4 (over y, x), fsdp: 8 (over z, core).
Axes of the slice: x: 2, y: 2, z: 4, core: 2. Of those that a mesh axis runs over, the one named last changes fastest.
Arguments:
- tokens: bfloat16 [64, 4096], P(('grp', 'fsdp')), may hold values from -128 to 128
- norm_gain: float32 [4096], replicated, may hold values from 0.25 to 1.75
- routes: int32 [64, 8], P(('grp', 'fsdp')), may hold values from 0 to 31, all different within a row; in each aligned block of 16 rows (0 to 15, 16 to 31, ...) at most 8 rows name the same one
- gate_probs: bfloat16 [64, 8], P(('grp', 'fsdp')), may hold values from 0.019897461 to 1
- w_gate_up: bfloat16 [32, 4096, 2048], P(('grp', 'fsdp')), may hold values from -0.09375 to 0.09375
- w_down: bfloat16 [32, 1024, 4096], P(('grp', 'fsdp')), may hold values from -0.1875 to 0.1875
Outputs:
- moe_out: bfloat16 [64, 4096], P(('grp', 'fsdp'))
Inputs may be any that keep to these rules, and one draw needn't show every extreme that they name: `routes`: each row names 8 different experts. In every aligned block of 16 rows no expert is named by more than 8 rows, a bound that some block reaches.
All inputs are finite; a program needn't handle non-finite values.
Results may differ from a plain program's by a relative error of at most 0.0095.
Values may be sent and summed in bfloat16 or wider, within the bound.
No kernel may reach another device: no remote copies, remote signals or barrier semaphores. Data moves between devices by JAX's collectives and lax.ppermute only.
A program may use at most 64 MiB of HBM per device.

v0:
```python
import jax
import jax.numpy as jnp
from jax import lax
from jax.sharding import PartitionSpec as P

FF = 1024


def local(tokens, norm_gain, routes, gate_probs, w_gate_up, w_down):
    group_count = lax.axis_size("grp")
    shard_count = lax.axis_size("fsdp")
    shard_index = lax.axis_index("fsdp")
    hidden_dev = w_down.shape[1]
    split_count = FF // hidden_dev
    expert_count = group_count * shard_count // split_count
    rows_dev = tokens.shape[0]
    top_count = routes.shape[1]
    block_rows = rows_dev * shard_count
    capacity = 2 * rows_dev * shard_count * top_count // expert_count
    width = tokens.shape[1]
    as_float = tokens.astype(jnp.float32)
    mean_square = jnp.mean(as_float * as_float, axis=-1, keepdims=True)
    normed = (as_float * lax.rsqrt(mean_square + 1e-06) * norm_gain).astype(jnp.bfloat16)
    rows_all, probs_all = (
        lax.all_gather(normed, "fsdp", axis=0, tiled=True),
        lax.all_gather(gate_probs, "fsdp", axis=0, tiled=True),
    )
    routes_all = lax.all_gather(routes, "fsdp", axis=0, tiled=True)
    probs = probs_all.astype(jnp.float32)
    combine = probs / jnp.sum(probs, axis=-1, keepdims=True)
    targets = (
        jnp.arange(group_count, dtype=jnp.int32) * (shard_count // split_count)
        + shard_index // split_count
    )
    matched = routes_all[None, :, :] == targets[:, None, None]
    is_routed = jnp.any(matched, axis=-1)
    row_weight = jnp.sum(jnp.where(matched, combine[None, :, :], 0.0), axis=-1)
    slot_index = jnp.cumsum(is_routed.astype(jnp.int32), axis=1) - 1
    select = (
        slot_index[:, None, :] == jnp.arange(capacity, dtype=jnp.int32)[None, :, None]
    ) & is_routed[:, None, :]
    outgoing = jnp.einsum(
        "gcb,bd->gcd", select.astype(jnp.bfloat16), rows_all, preferred_element_type=jnp.float32
    ).astype(jnp.bfloat16)
    incoming = lax.all_to_all(outgoing, "grp", split_axis=0, concat_axis=0, tiled=True)
    flattened = incoming.reshape(-1, width)
    projected = jnp.dot(flattened, w_gate_up[0], preferred_element_type=jnp.float32)
    hidden = (jax.nn.silu(projected[:, :hidden_dev]) * projected[:, hidden_dev:]).astype(
        jnp.bfloat16
    )
    result = jnp.dot(hidden, w_down[0], preferred_element_type=jnp.float32).astype(jnp.bfloat16)
    returned = lax.all_to_all(
        result.reshape(incoming.shape), "grp", split_axis=0, concat_axis=0, tiled=True
    )
    mix_matrix = (select.astype(jnp.float32) * row_weight[:, None, :]).reshape(-1, block_rows)
    row_partial = jnp.dot(
        mix_matrix.T,
        returned.reshape(-1, width),
        precision=lax.Precision.HIGHEST,
        preferred_element_type=jnp.float32,
    )
    summed = lax.psum_scatter(row_partial, "fsdp", scatter_dimension=0, tiled=True)
    return summed.astype(jnp.bfloat16)


def solution(mesh):
    return jax.shard_map(
        local,
        mesh=mesh,
        in_specs=(
            P(("grp", "fsdp"), None),
            P(),
            P(("grp", "fsdp"), None),
            P(("grp", "fsdp"), None),
            P(("grp", "fsdp"), None, None),
            P(("grp", "fsdp"), None, None),
        ),
        out_specs=P(("grp", "fsdp"), None),
        check_vma=False,
    )
```

profile of v0, /device:TPU:0, one launch (start us, length us, event | category | flops | bytes accessed | tf_op | source)
XLA Modules:
  0.0 94.8 jit_solution(7591240734302826050)
XLA Ops:
  0.0 0.9 fusion.14
  0.9 13.7 %all-gather = s32[8,2,8]{2,1,0:T(2,128)S(1)} all-gather(s32[1,2,8]{2,1,0:T(2,128)} %bitcast.29), channel_id=1, replica_groups=mesh['grp'=4,'fsdp'=8] {'fsdp'}, dimensions={0}, use_global_device_ids=true | all-gather | bytes 576 | tf_op jit(solution)/shard_map/all_gather | solution.py:28
  14.6 0.1 copy.7
  14.6 0.1 compare_reduce_fusion
  14.7 0.2 reduce_window_sum.11
  14.9 0.8 fusion.19
  15.7 14.0 %all-gather.2 = bf16[8,2,4096]{2,1,0:T(2,128)(2,1)S(1)} all-gather(bf16[1,2,4096]{2,1,0:T(2,128)(2,1)S(1)} %fusion.19), channel_id=1, replica_groups=mesh['grp'=4,'fsdp'=8] {'fsdp'}, dimensions={0}, use_global_device_ids=true | all-gather | bytes 147456 | tf_op jit(solution)/shard_map/all_gather | solution.py:25
  29.7 0.1 reshape.46
  29.8 0.9 convolution_convert_fusion
  30.7 3.7 %all-to-all-start = ((bf16[4,8,4096]{2,1,0:T(8,128)(2,1)}), bf16[4,8,4096]{2,1,0:T(8,128)(2,1)S(1)}, u32[]{:S(2)}, u32[]{:S(2)}) async-start(bf16[4,8,4096]{2,1,0:T(8,128)(2,1)} %convolution_convert_fusion), calls=%async_computation | async-start | bytes 524288 | tf_op jit(solution)/shard_map/all_to_all | solution.py:45
  34.4 8.8 %all-gather.1 = bf16[8,2,8]{2,1,0:T(2,128)(2,1)S(1)} all-gather(bf16[1,2,8]{2,1,0:T(2,128)(2,1)} %bitcast.30), channel_id=1, replica_groups=mesh['grp'=4,'fsdp'=8] {'fsdp'}, dimensions={0}, use_global_device_ids=true | all-gather | bytes 288 | tf_op jit(solution)/shard_map/all_gather | solution.py:26
  43.2 0.1 convert_reduce_fusion
  43.3 0.1 reshape.45
  43.4 8.9 %fusion = f32[32,2048]{1,0:T(8,128)S(1)} fusion(bf16[1,4096,2048]{2,1,0:T(8,128)(2,1)} %param.10, bf16[4,8,4096]{2,1,0:T(8,128)(2,1)S(1)} %all-to-all-done), kind=kOutput, calls=%fused_computation | convolution fusion | flops 536870912 | bytes 17301504 | tf_op jit(solution)/shard_map/dot_general | solution.py:47
  52.3 2.2 %fusion.7 = bf16[4,8,4096]{2,1,0:T(8,128)(2,1)} fusion(bf16[1,1024,4096]{2,1,0:T(8,128)(2,1)S(1)} %copy-done, f32[32,2048]{1,0:T(8,128)S(1)} %fusion), kind=kOutput, calls=%fused_computation.6 | convolution fusion | flops 268763136 | bytes 8912896 | tf_op jit(solution)/shard_map/dot_general | solution.py:51
  54.5 4.2 %all-to-all-start.1 = ((bf16[4,8,4096]{2,1,0:T(8,128)(2,1)}), bf16[4,8,4096]{2,1,0:T(8,128)(2,1)S(1)}, u32[]{:S(2)}, u32[]{:S(2)}) async-start(bf16[4,8,4096]{2,1,0:T(8,128)(2,1)} %fusion.7), calls=%async_computation.1 | async-start | bytes 524288 | tf_op jit(solution)/shard_map/all_to_all | solution.py:52
  58.7 0.1 broadcast_divide_fusion
  58.8 0.1 copy.8
  58.9 0.6 dynamic-slice
  60.1 0.1 fusion.17
  60.2 4.4 %all-to-all-done.1 = bf16[4,8,4096]{2,1,0:T(8,128)(2,1)S(1)} async-done(((bf16[4,8,4096]{2,1,0:T(8,128)(2,1)}), bf16[4,8,4096]{2,1,0:T(8,128)(2,1)S(1)}, u32[]{:S(2)}, u32[]{:S(2)}) %all-to-all-start.1) | async-done | bytes 262176 | tf_op jit(solution)/shard_map/all_to_all | solution.py:52
  64.6 0.3 convolution_bitcast_fusion
  64.9 29.2 %all-reduce.2 = bf16[16,4096]{1,0:T(8,128)(2,1)S(1)} all-reduce(f32[16,4096]{1,0:T(8,128)S(1)} %convolution_bitcast_fusion), channel_id=2, replica_groups=mesh['grp'=4,'fsdp'=8] {'fsdp'}, use_global_device_ids=true, to_apply=%region_5.6.clone | all-reduce | flops 65536 | bytes 393216
  94.1 0.6 dynamic-slice_convert_fusion
  (9 shorter events, 0.0 us)
Async XLA Ops:
  30.7 12.7 %all-to-all-start = ((bf16[4,8,4096]{2,1,0:T(8,128)(2,1)}), bf16[4,8,4096]{2,1,0:T(8,128)(2,1)S(1)}, u32[]{:S(2)}, u32[]{:S(2)}) async-start(bf16[4,8,4096]{2,1,0:T(8,128)(2,1)} %convolution_convert_fusion), calls=%async_computation | async-start | bytes 524288 | tf_op jit(solution)/shard_map/all_to_all | solution.py:45
  43.4 15.5 %copy-start.1 = (u32[32]{0:T(128)S(1)}, u32[32]{0:T(128)}, u32[]{:S(2)}) copy-start(u32[32]{0:T(128)} %constant.44) | copy-start | bytes 388
  43.4 8.9 %copy-start = (bf16[1,1024,4096]{2,1,0:T(8,128)(2,1)S(1)}, bf16[1,1024,4096]{2,1,0:T(8,128)(2,1)}, u32[]{:S(2)}) copy-start(bf16[1,1024,4096]{2,1,0:T(8,128)(2,1)} %param.11) | copy-start | bytes 25165828
  54.5 10.0 %all-to-all-start.1 = ((bf16[4,8,4096]{2,1,0:T(8,128)(2,1)}), bf16[4,8,4096]{2,1,0:T(8,128)(2,1)S(1)}, u32[]{:S(2)}, u32[]{:S(2)}) async-start(bf16[4,8,4096]{2,1,0:T(8,128)(2,1)} %fusion.7), calls=%async_computation.1 | async-start | bytes 524288 | tf_op jit(solution)/shard_map/all_to_all | solution.py:52
where the time goes:
time: 95.3 us; the launch traced here: 94.8 us
  blocking collectives  65.7 us (69%)
  matrix products  12.4 us (13%)
  starting transfers between devices  7.91 us (8%)
  waiting for transfers between devices  4.35 us (5%)
  other arithmetic  2.24 us (2%)
  local copies, waits for them, and re-layouts  1.5 us (2%)
    unnamed x1, blocking collectives  29.2 us
    all_gather x1, blocking collectives, local(): lax.all_gather(normed, 'fsdp', axis=0, tiled=True)  14 us
    all_gather x1, blocking collectives, local(): routes_all = lax.all_gather(routes, 'fsdp', axis=0, tiled=True)  13.7 us
    dot_general x1, matrix products, local(): jnp.dot(flattened, w_gate_up[0], preferred_element_type=jnp.float32)  8.9 us
    all_gather x1, blocking collectives, local(): lax.all_gather(gate_probs, 'fsdp', axis=0, tiled=True)  8.82 us
    all_to_all x1, waiting for transfers between devices, local(): lax.all_to_all(result.reshape(incoming.shape), 'grp', split_axis=0, conca...  4.35 us
    all_to_all x1, starting transfers between devices, local(): lax.all_to_all(result.reshape(incoming.shape), 'grp', split_axis=0, conca...  4.19 us
    all_to_all x1, starting transfers between devices, local(): lax.all_to_all(outgoing, 'grp', split_axis=0, concat_axis=0, tiled=True)  3.71 us
  transfers between devices with their start and end apart: 2, of which 1 were waited for; matrix products, arithmetic and copies ran while one was open for 1% of the time, Pallas kernels for 0%

commit v1 on v0

v1 whole, which is shorter than its diff:
```python
import jax
import jax.numpy as jnp
from jax import lax
from jax.sharding import PartitionSpec as P

FF = 1024
LANES = 128
AXES = ("grp", "fsdp")


def rms_normed(tokens, norm_gain):
    as_float = tokens.astype(jnp.float32)
    mean_square = jnp.mean(as_float * as_float, axis=-1, keepdims=True)
    return (as_float * lax.rsqrt(mean_square + 1e-06) * norm_gain).astype(jnp.bfloat16)


def expert_mlp(rows, w_gate_up, w_down):
    hidden_dev = w_down.shape[1]
    projected = jnp.dot(rows, w_gate_up[0], preferred_element_type=jnp.float32)
    hidden = (jax.nn.silu(projected[:, :hidden_dev]) * projected[:, hidden_dev:]).astype(
        jnp.bfloat16
    )
    return jnp.dot(hidden, w_down[0], preferred_element_type=jnp.float32).astype(jnp.bfloat16)


def every_row(tokens, norm_gain, routes, gate_probs, w_gate_up, w_down):
    device_count = lax.axis_size(AXES)
    pair_count = device_count // 2
    me = lax.axis_index(AXES)
    my_expert = me // (FF // w_down.shape[1])
    rows_dev, width = tokens.shape
    top_count = routes.shape[1]
    same_core = [[d for d in range(device_count) if d % 2 == k] for k in range(2)]
    partner = [(d, d ^ 1) for d in range(device_count)]

    normed = rms_normed(tokens, norm_gain)
    padding = jnp.zeros((rows_dev, -2 * top_count % LANES), jnp.bfloat16)
    payload = jnp.concatenate(
        [normed, routes.astype(jnp.bfloat16), gate_probs, padding], axis=1
    )
    outgoing = jnp.broadcast_to(payload[None], (pair_count,) + payload.shape)
    own = lax.all_to_all(outgoing, AXES, 0, 0, axis_index_groups=same_core, tiled=True)
    other = lax.ppermute(own, AXES, partner)
    rows = jnp.concatenate([own, other]).reshape(-1, payload.shape[1])

    sent_routes = rows[:, width : width + top_count].astype(jnp.int32)
    probs = rows[:, width + top_count : width + 2 * top_count].astype(jnp.float32)
    combine = probs / jnp.sum(probs, axis=-1, keepdims=True)
    row_weight = jnp.sum(jnp.where(sent_routes == my_expert, combine, 0.0), axis=-1)

    part = expert_mlp(rows[:, :width], w_gate_up, w_down)
    weighted = (part.astype(jnp.float32) * row_weight[:, None]).reshape(
        2, pair_count, rows_dev, width
    )
    from_partner = lax.ppermute(weighted[1].astype(jnp.bfloat16), AXES, partner)
    chip_sum = (weighted[0] + from_partner.astype(jnp.float32)).astype(jnp.bfloat16)
    returned = lax.all_to_all(chip_sum, AXES, 0, 0, axis_index_groups=same_core, tiled=True)
    return jnp.sum(returned.astype(jnp.float32), axis=0).astype(jnp.bfloat16)


def routed_rows(tokens, norm_gain, routes, gate_probs, w_gate_up, w_down):
    group_count = lax.axis_size("grp")
    shard_count = lax.axis_size("fsdp")
    shard_index = lax.axis_index("fsdp")
    split_count = FF // w_down.shape[1]
    rows_dev, width = tokens.shape
    block_rows = rows_dev * shard_count
    capacity = slot_capacity(tokens, routes, w_down)
    normed = rms_normed(tokens, norm_gain)
    rows_all = lax.all_gather(normed, "fsdp", axis=0, tiled=True)
    probs_all = lax.all_gather(gate_probs, "fsdp", axis=0, tiled=True)
    routes_all = lax.all_gather(routes, "fsdp", axis=0, tiled=True)
    probs = probs_all.astype(jnp.float32)
    combine = probs / jnp.sum(probs, axis=-1, keepdims=True)
    targets = (
        jnp.arange(group_count, dtype=jnp.int32) * (shard_count // split_count)
        + shard_index // split_count
    )
    matched = routes_all[None, :, :] == targets[:, None, None]
    is_routed = jnp.any(matched, axis=-1)
    row_weight = jnp.sum(jnp.where(matched, combine[None, :, :], 0.0), axis=-1)
    row_ids = jnp.arange(block_rows, dtype=jnp.int32)
    earlier = row_ids[:, None] >= row_ids[None, :]
    slot_index = jnp.sum(is_routed[:, None, :] & earlier[None], axis=-1, dtype=jnp.int32) - 1
    select = (
        slot_index[:, None, :] == jnp.arange(capacity, dtype=jnp.int32)[None, :, None]
    ) & is_routed[:, None, :]
    outgoing = jnp.einsum(
        "gcb,bd->gcd", select.astype(jnp.bfloat16), rows_all, preferred_element_type=jnp.float32
    ).astype(jnp.bfloat16)
    incoming = lax.all_to_all(outgoing, "grp", split_axis=0, concat_axis=0, tiled=True)
    result = expert_mlp(incoming.reshape(-1, width), w_gate_up, w_down)
    returned = lax.all_to_all(
        result.reshape(incoming.shape), "grp", split_axis=0, concat_axis=0, tiled=True
    )
    mix_matrix = (select.astype(jnp.float32) * row_weight[:, None, :]).reshape(-1, block_rows)
    row_partial = jnp.dot(
        mix_matrix.T,
        returned.reshape(-1, width),
        precision=lax.Precision.HIGHEST,
        preferred_element_type=jnp.float32,
    )
    summed = lax.psum_scatter(row_partial, "fsdp", scatter_dimension=0, tiled=True)
    return summed.astype(jnp.bfloat16)


def slot_capacity(tokens, routes, w_down):
    block_rows = tokens.shape[0] * lax.axis_size("fsdp")
    expert_count = lax.axis_size(AXES) * w_down.shape[1] // FF
    return 2 * block_rows * routes.shape[1] // expert_count


def local(tokens, norm_gain, routes, gate_probs, w_gate_up, w_down):
    block_rows = tokens.shape[0] * lax.axis_size("fsdp")
    dense = block_rows <= 2 * slot_capacity(tokens, routes, w_down)
    plan = every_row if dense and lax.axis_size("fsdp") % 2 == 0 else routed_rows
    return plan(tokens, norm_gain, routes, gate_probs, w_gate_up, w_down)


def solution(mesh):
    return jax.shard_map(
        local,
        mesh=mesh,
        in_specs=(
            P(AXES, None),
            P(),
            P(AXES, None),
            P(AXES, None),
            P(AXES, None, None),
            P(AXES, None, None),
        ),
        out_specs=P(AXES, None),
        check_vma=False,
    )
```

time: 95.3 us -> 52.8 us (0.55)
  blocking collectives: 65.7 us -> 32.6 us
  starting transfers between devices: 7.91 us -> 0.21 us
  other arithmetic: 2.24 us -> 4.56 us
  matrix products: 12.4 us -> 10.5 us
  waiting for transfers between devices: 4.35 us -> 2.59 us
    all_gather x3 -> x0, blocking collectives: 36.5 us -> none  [the longest x1 14 us: local(): lax.all_gather(normed, 'fsdp', axis=0, tiled=True)]
    all_to_all x0 -> x2, blocking collectives: none -> 32.6 us  [the longest x1 18.9 us: every_row(): lax.all_to_all(outgoing, AXES, 0, 0, axis_index_groups=same_core, tiled=T...]
    unnamed x1 -> x0, blocking collectives: 29.2 us -> none
    all_to_all x2 -> x0, starting transfers between devices: 7.91 us -> none  [the longest x1 4.19 us: local(): lax.all_to_all(result.reshape(incoming.shape), 'grp', split_axis=0, conca...]
    all_to_all x2 -> x0, waiting for transfers between devices: 4.35 us -> none  [the longest x1 4.35 us: local(): lax.all_to_all(result.reshape(incoming.shape), 'grp', split_axis=0, conca...]
    ppermute x0 -> x2, waiting for transfers between devices: none -> 2.59 us  [the longest x1 1.54 us: every_row(): other = lax.ppermute(own, AXES, partner)]
    dot_general x4 -> x2, matrix products: 12.4 us -> 10.5 us  [the longest x1 8.94 us: expert_mlp(): projected = jnp.dot(rows, w_gate_up[0], preferred_element_type=jnp.float32)]
    convert_element_type x1 -> x3, other arithmetic: 0.01 us -> 1.8 us  [the longest x1 0.83 us: rms_normed(): (as_float * lax.rsqrt(mean_square + 1e-06) * norm_gain).astype(jnp.bfloat16)]
  transfers between devices with their start and end apart: 2 -> 2, of which waited for: 1 -> 2; matrix products, arithmetic and copies ran while one was open for 1% -> 1% of each run, Pallas kernels for 0% -> 0%
where the time goes in v1:
time: 52.8 us; the launch traced here: 52.3 us
  blocking collectives  32.6 us (62%)
  matrix products  10.5 us (20%)
  other arithmetic  4.56 us (9%)
  waiting for transfers between devices  2.59 us (5%)
  local copies, waits for them, and re-layouts  1.67 us (3%)
    all_to_all x1, blocking collectives, every_row(): lax.all_to_all(outgoing, AXES, 0, 0, axis_index_groups=same_core, tiled=T...  18.9 us
    all_to_all x1, blocking collectives, every_row(): lax.all_to_all(chip_sum, AXES, 0, 0, axis_index_groups=same_core, tiled=T...  13.8 us
    dot_general x1, matrix products, expert_mlp(): projected = jnp.dot(rows, w_gate_up[0], preferred_element_type=jnp.float32)  8.94 us
    dot_general x1, matrix products, expert_mlp(): jnp.dot(hidden, w_down[0], preferred_element_type=jnp.float32)  1.56 us
    ppermute x1, waiting for transfers between devices, every_row(): other = lax.ppermute(own, AXES, partner)  1.54 us
  transfers between devices with their start and end apart: 2, of which 2 were waited for; matrix products, arithmetic and copies ran while one was open for 1% of the time, Pallas kernels for 0%

profile of v1, /device:TPU:0, one launch (start us, length us, event | category | flops | bytes accessed | tf_op | source)
XLA Modules:
  0.0 52.3 jit_solution(3209581076707684841)
XLA Ops:
  0.0 0.7 %convert_element_type.38 = bf16[2,8]{1,0:T(2,128)(2,1)S(1)} convert(s32[2,8]{1,0:T(2,128)} %param.8) | non-fusion elementwise | flops 16 | bytes 96 | tf_op jit(solution)/shard_map/convert_element_type | solution.py:39
  0.7 0.9 %fusion.17 = f32[2]{0:T(128)S(1)} fusion(bf16[2,4096]{1,0:T(2,128)(2,1)} %param.6), kind=kLoop, calls=%fused_computation.18 | loop fusion | flops 24574 | bytes 16392 | tf_op jit(solution)/shard_map/reduce_sum | solution.py:13
  1.6 0.8 %fusion.19 = bf16[2,4096]{1,0:T(2,128)(2,1)S(1)} fusion(bf16[2,4096]{1,0:T(2,128)(2,1)} %param.6, f32[2]{0:T(128)S(1)} %add_rsqrt_fusion, f32[4096]{0:T(1024)} %param.7), kind=kLoop, calls=%fused_computation.20 | loop fusion | flops 32768 | bytes 49160 | tf_op jit(solution)/shard_map/convert_element_type | solution.py:14
  2.4 0.8 %concatenate.6 = bf16[2,4224]{1,0:T(2,128)(2,1)S(1)} concatenate(bf16[2,4096]{1,0:T(2,128)(2,1)S(1)} %fusion.19, bf16[2,8]{1,0:T(2,128)(2,1)S(1)} %convert_element_type.38, bf16[2,8]{1,0:T(2,128)(2,1)} %param.9, bf16[2,112]{1,0:T(2,128)(2,1)S(1)} %broadcast_in_dim.7), dimensions={1} | concatenate | bytes 33792 | tf_op jit(solution)/shard_map/concatenate | solution.py:38
  3.1 0.1 broadcast_in_dim.8
  3.3 18.9 %all_to_all.10 = bf16[16,2,4224]{2,1,0:T(2,128)(2,1)S(1)} all-to-all(bf16[16,2,4224]{2,1,0:T(2,128)(2,1)S(1)} %broadcast_in_dim.8), channel_id=1, replica_groups={{0,2,4,6,8,10,12,14,16,18,20,22,24,26,28,30},{1,3,5,7,9,11,13,15,17,19,..., dimensions={0} | all-to-all | bytes 540672 | tf_op jit(solution)/shard_map/all_to_all | solution.py:42
  22.2 0.0 collective-permute-start
  22.2 1.5 %collective-permute-done = bf16[16,2,4224]{2,1,0:T(2,128)(2,1)S(1)} collective-permute-done((bf16[16,2,4224]{2,1,0:T(2,128)(2,1)S(1)}, bf16[16,2,4224]{2,1,0:T(2,128)(2,1)S(1)}, u32[]{:S(2)}, u32[]{:S(2)}) %collective-permute-start) | collective-permute-done | bytes 270368 | tf_op jit(solution)/shard_map/ppermute | solution.py:43
  23.7 0.7 %pad_maximum_fusion = bf16[32,2,4224]{2,1,0:T(2,128)(2,1)S(1)} fusion(bf16[16,2,4224]{2,1,0:T(2,128)(2,1)S(1)} %collective-permute-done, bf16[16,2,4224]{2,1,0:T(2,128)(2,1)S(1)} %all_to_all.10), kind=kLoop, calls=%fused_computation.7 | loop fusion | flops 270336 | bytes 1081344 | tf_op jit(solution)/shard_map/concatenate | solution.py:44
  24.4 0.2 reshape.21
  24.6 0.0 slice-start
  24.6 0.2 convert_reduce_fusion
  24.8 0.0 slice-start.1
  24.8 8.9 %fusion = f32[64,2048]{1,0:T(8,128)S(1)} fusion(bf16[1,4096,2048]{2,1,0:T(8,128)(2,1)} %param.10, bf16[64,4224]{1,0:T(8,128)(2,1)S(1)} %reshape.21), kind=kOutput, calls=%fused_computation | convolution fusion | flops 1073741824 | bytes 17825792 | tf_op jit(solution)/shard_map/dot_general | solution.py:19
  33.8 0.2 fusion.21
  34.0 0.0 slice-done
  34.0 1.6 %fusion.10 = f32[64,4096]{1,0:T(8,128)S(1)} fusion(bf16[1,1024,4096]{2,1,0:T(8,128)(2,1)S(1)} %bitcast.13, f32[64]{0:T(128)S(1)} %fusion.21, f32[64,2048]{1,0:T(8,128)S(1)} %fusion), kind=kOutput, calls=%fused_computation.6 | convolution fusion | flops 538050560 | bytes 9961728 | tf_op jit(solution)/shard_map/dot_general | solution.py:23
  35.6 0.2 convert_element_type.44
  35.8 0.2 collective-permute-start.1
  36.0 0.3 squeeze.12
  36.3 1.0 %collective-permute-done.1 = bf16[16,2,4096]{2,1,0:T(2,128)(2,1)S(1)} collective-permute-done((bf16[16,2,4096]{2,1,0:T(2,128)(2,1)S(1)}, bf16[16,2,4096]{2,1,0:T(2,128)(2,1)S(1)}, u32[]{:S(2)}, u32[]{:S(2)}) %collective-permute-start.1) | collective-permute-done | bytes 262176 | tf_op jit(solution)/shard_map/ppermute | solution.py:55
  37.4 0.3 add_convert_fusion
  37.7 13.8 %all_to_all.11 = bf16[16,2,4096]{2,1,0:T(2,128)(2,1)S(1)} all-to-all(bf16[16,2,4096]{2,1,0:T(2,128)(2,1)S(1)} %add_convert_fusion), channel_id=1, replica_groups={{0,2,4,6,8,10,12,14,16,18,20,22,24,26,28,30},{1,3,5,7,9,11,13,15,17,19,..., dimensions={0} | all-to-all | bytes 524288 | tf_op jit(solution)/shard_map/all_to_all | solution.py:57
  51.4 0.8 %reduce_sum.42 = bf16[2,4096]{1,0:T(2,128)(2,1)} reduce(bf16[16,2,4096]{2,1,0:T(2,128)(2,1)S(1)} %all_to_all.11, bf16[]{:T(256)} %constant.29.clone.1), dimensions={0}, to_apply=%region_3.4 | reduce | flops 122880 | bytes 278530 | tf_op jit(solution)/shard_map/reduce_sum | solution.py:58
  (6 shorter events, 0.1 us)
Async XLA Ops:
  22.2 1.5 %collective-permute-start = (bf16[16,2,4224]{2,1,0:T(2,128)(2,1)S(1)}, bf16[16,2,4224]{2,1,0:T(2,128)(2,1)S(1)}, u32[]{:S(2)}, u32[]{:S(2)}) collective-permute-start(bf16[16,2,4224]{2,1,0:T(2,128)(2,1)S(1)} %all_to_all.10), channel_id=1, source_target_pairs={{0,1},{1,0},{2,3},{3,2},{4,5},{5,4},{6,7},{7,6},{8,9},{9,8},{10,11... | collective-permute-start | bytes 811016 | tf_op jit(solution)/shard_map/ppermute | solution.py:43
  24.6 9.3 %slice-start = ((s8[8388608]{0:T(1024)(128)(4,1)}), s8[4194304]{0:T(1024)(128)(4,1)S(1)}, s32[]{:S(2)}) async-start(s8[8388608]{0:T(1024)(128)(4,1)} %bitcast.12), calls=%async_computation.2 | async-start | bytes 8388608
  24.8 9.2 %slice-start.1 = ((s8[8388608]{0:T(1024)(128)(4,1)}), s8[4194304]{0:T(1024)(128)(4,1)S(1)}, s32[]{:S(2)}) async-start(s8[8388608]{0:T(1024)(128)(4,1)} %bitcast.12), calls=%async_computation.3 | async-start | bytes 8388608
  35.8 1.6 %collective-permute-start.1 = (bf16[16,2,4096]{2,1,0:T(2,128)(2,1)S(1)}, bf16[16,2,4096]{2,1,0:T(2,128)(2,1)S(1)}, u32[]{:S(2)}, u32[]{:S(2)}) collective-permute-start(bf16[16,2,4096]{2,1,0:T(2,128)(2,1)S(1)} %convert_element_type.44), channel_id=1, source_target_pairs={{0,1},{1,0},{2,3},{3,2},{4,5},{5,4},{6,7},{7,6},{8,9},{9,8},{10,11... | collective-permute-start | bytes 786440 | tf_op jit(solution)/shard_map/ppermute | solution.py:55

commit v2 on v1

--- a/solution.py
+++ b/solution.py
@@ -1,11 +1,19 @@
 import jax
 import jax.numpy as jnp
 from jax import lax
+from jax.experimental import pallas as pl
+from jax.experimental.pallas import tpu as pltpu
 from jax.sharding import PartitionSpec as P
 
 FF = 1024
 LANES = 128
+SMALL_VMEM = 2 << 20
+MLP_VMEM = 24 << 20
 AXES = ("grp", "fsdp")
+
+
+def device_index():
+    return lax.axis_index("grp") * lax.axis_size("fsdp") + lax.axis_index("fsdp")
 
 
 def rms_normed(tokens, norm_gain):
@@ -23,38 +31,207 @@
     return jnp.dot(hidden, w_down[0], preferred_element_type=jnp.float32).astype(jnp.bfloat16)
 
 
+def row_payload(tokens, norm_gain, routes, gate_probs):
+    rows_dev, width = tokens.shape
+    top_count = routes.shape[1]
+    total = width + LANES * -(-2 * top_count // LANES)
+
+    def kernel(*refs):
+        sources, payload_ref, targets, sems = refs[:4], refs[4], refs[5:9], refs[9]
+        copies = [
+            pltpu.make_async_copy(source, target, sems.at[index])
+            for index, (source, target) in enumerate(zip(sources, targets))
+        ]
+        for copy in copies:
+            copy.start()
+        for copy in copies:
+            copy.wait()
+        tokens_ref, gain_ref, routes_ref, probs_ref = targets
+        as_float = tokens_ref[...].astype(jnp.float32)
+        mean_square = jnp.mean(as_float * as_float, axis=-1, keepdims=True)
+        scaled = as_float * lax.rsqrt(mean_square + 1e-06) * gain_ref[...]
+        payload_ref[:, :width] = scaled.astype(jnp.bfloat16)
+        control = jnp.concatenate(
+            [
+                routes_ref[...].astype(jnp.float32),
+                probs_ref[...].astype(jnp.float32),
+                jnp.zeros((rows_dev, total - width - 2 * top_count), jnp.float32),
+            ],
+            axis=1,
+        )
+        payload_ref[:, width:] = control.astype(jnp.bfloat16)
+
+    operands = (tokens, norm_gain.reshape(1, width), routes, gate_probs)
+    return pl.pallas_call(
+        kernel,
+        out_shape=jax.ShapeDtypeStruct((rows_dev, total), jnp.bfloat16),
+        in_specs=[pl.BlockSpec(memory_space=pltpu.HBM)] * 4,
+        out_specs=pl.BlockSpec(memory_space=pltpu.VMEM),
+        scratch_shapes=[pltpu.VMEM(o.shape, o.dtype) for o in operands]
+        + [pltpu.SemaphoreType.DMA((4,))],
+        compiler_params=pltpu.CompilerParams(vmem_limit_bytes=SMALL_VMEM),
+        name="row_payload",
+    )(*[pltpu.with_memory_space_constraint(o, pltpu.HBM) for o in operands])
+
+
+def load_rows(weight, first, count, chunk_count=8):
+    step = count // chunk_count
+
+    def kernel(source, target, sems):
+        copies = [
+            pltpu.make_async_copy(
+                source.at[0, pl.ds(first + chunk * step, step)],
+                target.at[pl.ds(chunk * step, step)],
+                sems.at[chunk],
+            )
+            for chunk in range(chunk_count)
+        ]
+        for copy in copies:
+            copy.start()
+        for copy in copies:
+            copy.wait()
+
+    shape = (count, weight.shape[2])
+    return pl.pallas_call(
+        kernel,
+        out_shape=pltpu.VMEM(shape, weight.dtype),
+        in_specs=[pl.BlockSpec(memory_space=pltpu.HBM)],
+        out_specs=pl.BlockSpec(memory_space=pltpu.VMEM),
+        scratch_shapes=[pltpu.SemaphoreType.DMA((chunk_count,))],
+        compiler_params=pltpu.CompilerParams(vmem_limit_bytes=SMALL_VMEM),
+        cost_estimate=pl.CostEstimate(
+            flops=0, transcendentals=0, bytes_accessed=2 * count * weight.shape[2]
+        ),
+        name="load_rows",
+    )(pltpu.with_memory_space_constraint(weight, pltpu.HBM))
+
+
+def stacked(pieces):
+    def kernel(*refs):
+        for index, ref in enumerate(refs[:-1]):
+            refs[-1][index] = ref[...]
+
+    vmem = pl.BlockSpec(memory_space=pltpu.VMEM)
+    return pl.pallas_call(
+        kernel,
+        out_shape=jax.ShapeDtypeStruct((len(pieces),) + pieces[0].shape, pieces[0].dtype),
+        in_specs=[vmem] * len(pieces),
+        out_specs=vmem,
+        compiler_params=pltpu.CompilerParams(vmem_limit_bytes=SMALL_VMEM),
+        name="stacked",
+    )(*pieces)
+
+
+def weighted_parts(own, other, gate_up_pieces, w_down, top_count):
+    hidden_dev, width = w_down.shape[1:]
+    blocks = list(own) + list(other)
+    block_rows = blocks[0].shape[0] * blocks[0].shape[1]
+    total = blocks[0].shape[2]
+    row_count = block_rows * len(blocks)
+    half = row_count // 2
+    piece_count = len(gate_up_pieces)
+    out_block = (half // blocks[0].shape[1], blocks[0].shape[1], width)
+
+    def kernel(*refs):
+        my_expert = device_index() // (FF // hidden_dev)
+        block_refs, refs = refs[: len(blocks)], refs[len(blocks) :]
+        piece_refs, refs = refs[:piece_count], refs[piece_count:]
+        down_hbm, own_out, other_out, rows_ref, down_ref, sem = refs
+        fetch = pltpu.make_async_copy(down_hbm.at[0], down_ref, sem)
+        fetch.start()
+        for index, source in enumerate(block_refs):
+            rows_ref[index * block_rows : (index + 1) * block_rows, :] = source[...].reshape(
+                block_rows, total
+            )
+        control = rows_ref[:, width:].astype(jnp.float32)
+        sent_routes = control[:, :top_count].astype(jnp.int32)
+        probs = control[:, top_count : 2 * top_count]
+        combine = probs / jnp.sum(probs, axis=-1, keepdims=True)
+        row_weight = jnp.sum(
+            jnp.where(sent_routes == my_expert, combine, 0.0), axis=-1, keepdims=True
+        )
+        projected, first = None, 0
+        for piece in piece_refs:
+            last = first + piece.shape[0]
+            term = jnp.dot(rows_ref[:, first:last], piece[...], preferred_element_type=jnp.float32)
+            projected, first = term if projected is None else projected + term, last
+        gate, up = projected[:, :hidden_dev], projected[:, hidden_dev:]
+        hidden = (jax.nn.silu(gate) * up).astype(jnp.bfloat16)
+        fetch.wait()
+        part = jnp.dot(hidden, down_ref[...], preferred_element_type=jnp.float32)
+        weighted = part.astype(jnp.bfloat16).astype(jnp.float32) * row_weight
+        own_out[...] = weighted[:half].reshape(out_block)
+        other_out[...] = weighted[half:].reshape(out_block).astype(jnp.bfloat16)
+
+    vmem = pl.BlockSpec(memory_space=pltpu.VMEM)
+    return pl.pallas_call(
+        kernel,
+        out_shape=[
+            jax.ShapeDtypeStruct(out_block, jnp.float32),
+            jax.ShapeDtypeStruct(out_block, jnp.bfloat16),
+        ],
+        in_specs=[vmem] * (len(blocks) + piece_count)
+        + [pl.BlockSpec(memory_space=pltpu.HBM)],
+        out_specs=[vmem] * 2,
+        scratch_shapes=[
+            pltpu.VMEM((row_count, total), jnp.bfloat16),
+            pltpu.VMEM(w_down.shape[1:], w_down.dtype),
+            pltpu.SemaphoreType.DMA,
+        ],
+        compiler_params=pltpu.CompilerParams(vmem_limit_bytes=MLP_VMEM),
+        name="weighted_parts",
+    )(
+        *blocks,
+        *[pltpu.with_memory_space_constraint(piece, pltpu.VMEM) for piece in gate_up_pieces],
+        pltpu.with_memory_space_constraint(w_down, pltpu.HBM),
+    )
+
+
+def chip_sum(own_part, partner_part):
+    pair_count = own_part.shape[0]
+
+    def kernel(own_ref, partner_ref, sum_ref):
+        my_chip = device_index() // 2
+        for chip in range(pair_count):
+            slot = jnp.bitwise_xor(my_chip, chip)
+            total = own_ref[slot] + partner_ref[slot].astype(jnp.float32)
+            sum_ref[chip] = total.astype(jnp.bfloat16)
+
+    vmem = pl.BlockSpec(memory_space=pltpu.VMEM)
+    return pl.pallas_call(
+        kernel,
+        out_shape=jax.ShapeDtypeStruct(own_part.shape, jnp.bfloat16),
+        in_specs=[vmem] * 2,
+        out_specs=vmem,
+        compiler_params=pltpu.CompilerParams(vmem_limit_bytes=SMALL_VMEM),
+        name="chip_sum",
+    )(own_part, partner_part)
+
+
+def exchanged(value, axis, flip):
+    size = lax.axis_size(axis)
+    return lax.ppermute(value, axis, [(d, d ^ flip) for d in range(size)])
+
+
 def every_row(tokens, norm_gain, routes, gate_probs, w_gate_up, w_down):
     device_count = lax.axis_size(AXES)
-    pair_count = device_count // 2
-    me = lax.axis_index(AXES)
-    my_expert = me // (FF // w_down.shape[1])
-    rows_dev, width = tokens.shape
-    top_count = routes.shape[1]
+    shard_count = lax.axis_size("fsdp")
+    group_count = lax.axis_size("grp")
     same_core = [[d for d in range(device_count) if d % 2 == k] for k in range(2)]
-    partner = [(d, d ^ 1) for d in range(device_count)]
-
-    normed = rms_normed(tokens, norm_gain)
-    padding = jnp.zeros((rows_dev, -2 * top_count % LANES), jnp.bfloat16)
-    payload = jnp.concatenate(
-        [normed, routes.astype(jnp.bfloat16), gate_probs, padding], axis=1
-    )
-    outgoing = jnp.broadcast_to(payload[None], (pair_count,) + payload.shape)
-    own = lax.all_to_all(outgoing, AXES, 0, 0, axis_index_groups=same_core, tiled=True)
-    other = lax.ppermute(own, AXES, partner)
-    rows = jnp.concatenate([own, other]).reshape(-1, payload.shape[1])
-
-    sent_routes = rows[:, width : width + top_count].astype(jnp.int32)
-    probs = rows[:, width + top_count : width + 2 * top_count].astype(jnp.float32)
-    combine = probs / jnp.sum(probs, axis=-1, keepdims=True)
-    row_weight = jnp.sum(jnp.where(sent_routes == my_expert, combine, 0.0), axis=-1)
-
-    part = expert_mlp(rows[:, :width], w_gate_up, w_down)
-    weighted = (part.astype(jnp.float32) * row_weight[:, None]).reshape(
-        2, pair_count, rows_dev, width
-    )
-    from_partner = lax.ppermute(weighted[1].astype(jnp.bfloat16), AXES, partner)
-    chip_sum = (weighted[0] + from_partner.astype(jnp.float32)).astype(jnp.bfloat16)
-    returned = lax.all_to_all(chip_sum, AXES, 0, 0, axis_index_groups=same_core, tiled=True)
+    depth = w_gate_up.shape[1] // 2
+
+    payload = row_payload(tokens, norm_gain, routes, gate_probs)
+    column = [payload] + [exchanged(payload, "fsdp", k) for k in range(2, shard_count, 2)]
+    column, first = lax.optimization_barrier((column, load_rows(w_gate_up, 0, depth)))
+    column = stacked(column)
+    plane = [exchanged(column, "grp", k) for k in range(1, group_count)]
+    plane, second = lax.optimization_barrier((plane, load_rows(w_gate_up, depth, depth)))
+    own = [column] + plane
+    other = [exchanged(block, "fsdp", 1) for block in own]
+    own_part, other_part = weighted_parts(own, other, [first, second], w_down, routes.shape[1])
+    from_partner = exchanged(other_part, "fsdp", 1)
+    summed = chip_sum(own_part, from_partner)
+    returned = lax.all_to_all(summed, AXES, 0, 0, axis_index_groups=same_core, tiled=True)
     return jnp.sum(returned.astype(jnp.float32), axis=0).astype(jnp.bfloat16)
 
 
@@ -113,7 +290,8 @@
 def local(tokens, norm_gain, routes, gate_probs, w_gate_up, w_down):
     block_rows = tokens.shape[0] * lax.axis_size("fsdp")
     dense = block_rows <= 2 * slot_capacity(tokens, routes, w_down)
-    plan = every_row if dense and lax.axis_size("fsdp") % 2 == 0 else routed_rows
+    paired = lax.axis_size("fsdp") > 1 and lax.axis_size(AXES) & (lax.axis_size(AXES) - 1) == 0
+    plan = every_row if dense and paired else routed_rows
     return plan(tokens, norm_gain, routes, gate_probs, w_gate_up, w_down)
 
 

time: 52.8 us -> 48.2 us (0.913)
  Pallas kernels: 0 us -> 16.1 us
  blocking collectives: 32.6 us -> 17.4 us
  matrix products: 10.5 us -> 0 us
  starting transfers between devices: 0.21 us -> 10.7 us
  other arithmetic: 4.56 us -> 0.83 us
  local copies, waits for them, and re-layouts: 1.67 us -> 0 us
    pallas_call x0 -> x6, Pallas kernels: none -> 16.1 us  [the longest x1 8.03 us: weighted_parts(): pl.pallas_call(kernel, out_shape=[jax.ShapeDtypeStruct(out_block, jnp.flo...]
    all_to_all x2 -> x1, blocking collectives: 32.6 us -> 17.4 us  [every_row(): lax.all_to_all(summed, AXES, 0, 0, axis_index_groups=same_core, tiled=True)]
    dot_general x2 -> x0, matrix products: 10.5 us -> none  [the longest x1 8.94 us: expert_mlp(): projected = jnp.dot(rows, w_gate_up[0], preferred_element_type=jnp.float32)]
    ppermute x2 -> x11, starting transfers between devices: 0.21 us -> 10.7 us  [exchanged(): return lax.ppermute(value, axis, [(d, d ^ flip) for d in range(size)])]
    convert_element_type x3 -> x0, other arithmetic: 1.8 us -> none  [the longest x1 0.83 us: rms_normed(): (as_float * lax.rsqrt(mean_square + 1e-06) * norm_gain).astype(jnp.bfloat16)]
    reduce_sum x3 -> x0, other arithmetic: 1.22 us -> none  [the longest x1 0.86 us: rms_normed(): mean_square = jnp.mean(as_float * as_float, axis=-1, keepdims=True)]
    concatenate x1 -> x0, local copies, waits for them, and re-layouts: 0.75 us -> none  [every_row(): jnp.concatenate([normed, routes.astype(jnp.bfloat16), gate_probs, padding...]
    concatenate x1 -> x0, other arithmetic: 0.7 us -> none  [every_row(): rows = jnp.concatenate([own, other]).reshape(-1, payload.shape[1])]
  transfers between devices with their start and end apart: 2 -> 11, of which waited for: 2 -> 7; matrix products, arithmetic and copies ran while one was open for 1% -> 0% of each run, Pallas kernels for 0% -> 14%
where the time goes in v2:
time: 48.2 us; the launch traced here: 47.9 us
  blocking collectives  17.4 us (36%)
  Pallas kernels  16.1 us (33%)
  starting transfers between devices  10.7 us (22%)
  waiting for transfers between devices  2.78 us (6%)
  other arithmetic  0.83 us (2%)
    all_to_all x1, blocking collectives, every_row(): lax.all_to_all(summed, AXES, 0, 0, axis_index_groups=same_core, tiled=True)  17.4 us
    ppermute x11, starting transfers between devices, exchanged(): return lax.ppermute(value, axis, [(d, d ^ flip) for d in range(size)])  10.7 us
    pallas_call x1, Pallas kernels, weighted_parts(): pl.pallas_call(kernel, out_shape=[jax.ShapeDtypeStruct(out_block, jnp.flo...  8.03 us
    pallas_call x2, Pallas kernels, load_rows(): pl.pallas_call(kernel, out_shape=pltpu.VMEM(shape, weight.dtype), in_spec...  6.94 us
    ppermute x11, waiting for transfers between devices, exchanged(): return lax.ppermute(value, axis, [(d, d ^ flip) for d in range(size)])  2.78 us
  transfers between devices with their start and end apart: 11, of which 7 were waited for; matrix products, arithmetic and copies ran while one was open for 0% of the time, Pallas kernels for 14%

profile of v2, /device:TPU:0, one launch (start us, length us, event | category | flops | bytes accessed | tf_op | source)
XLA Modules:
  0.0 47.9 jit_solution(6502979420377186849)
XLA Ops:
  0.0 0.9 %row_payload.1.refs_0_ = bf16[2,4224]{1,0:T(2,128)(2,1)S(1)} custom-call(bf16[2,4096]{1,0:T(2,128)(2,1)} %refs_0_.1, f32[1,4096]{1,0:T(1,128)} %bitcast.1, s32[2,8]{1,0:T(2,128)} %refs_2_.1, bf16[2,8]{1,0:T(2,128)(2,1)} %refs_3_.1), custom_call_target="tpu_custom_call" | custom-call | tf_op jit(solution)/shard_map/row_payload/pallas_call | solution.py:65
  0.9 5.1 %collective-permute-start.2 = (bf16[2,4224]{1,0:T(2,128)(2,1)S(1)}, bf16[2,4224]{1,0:T(2,128)(2,1)S(1)}, u32[]{:S(2)}, u32[]{:S(2)}) collective-permute-start(bf16[2,4224]{1,0:T(2,128)(2,1)S(1)} %row_payload.1.refs_0_), channel_id=1, source_target_pairs={{0,6},{1,7},{2,4},{3,5},{4,2},{5,3},{6,0},{7,1},{8,14},{9,15},{10,... | collective-permute-start | bytes 50696 | tf_op jit(solution)/shard_map/ppermute | solution.py:213
  6.0 0.6 %collective-permute-start = (bf16[2,4224]{1,0:T(2,128)(2,1)S(1)}, bf16[2,4224]{1,0:T(2,128)(2,1)S(1)}, u32[]{:S(2)}, u32[]{:S(2)}) collective-permute-start(bf16[2,4224]{1,0:T(2,128)(2,1)S(1)} %row_payload.1.refs_0_), channel_id=1, source_target_pairs={{0,2},{1,3},{2,0},{3,1},{4,6},{5,7},{6,4},{7,5},{8,10},{9,11},{10,... | collective-permute-start | bytes 50696 | tf_op jit(solution)/shard_map/ppermute | solution.py:213
  6.7 3.5 %load_rows.2.refs_8_ = bf16[2048,2048]{1,0:T(8,128)(2,1)S(1)} custom-call(bf16[1,4096,2048]{2,1,0:T(8,128)(2,1)} %source.3), custom_call_target="tpu_custom_call" | custom-call | bytes 8388608 | tf_op jit(solution)/shard_map/load_rows/pallas_call | solution.py:95
  10.2 0.5 %collective-permute-done.1.refs_2_ = bf16[2,4224]{1,0:T(2,128)(2,1)S(1)} collective-permute-done((bf16[2,4224]{1,0:T(2,128)(2,1)S(1)}, bf16[2,4224]{1,0:T(2,128)(2,1)S(1)}, u32[]{:S(2)}, u32[]{:S(2)}) %collective-permute-start.1) | collective-permute-done | bytes 16928 | tf_op jit(solution)/shard_map/ppermute | solution.py:213
  10.7 2.5 %collective-permute-start.5 = (bf16[4,2,4224]{2,1,0:T(2,128)(2,1)S(1)}, bf16[4,2,4224]{2,1,0:T(2,128)(2,1)S(1)}, u32[]{:S(2)}, u32[]{:S(2)}) collective-permute-start(bf16[4,2,4224]{2,1,0:T(2,128)(2,1)S(1)} %stacked.1.refs_0_), channel_id=1, source_target_pairs={{0,24},{8,16},{16,8},{24,0},{1,25},{9,17},{17,9},{25,1},{2,26},{10... | collective-permute-start | bytes 202760 | tf_op jit(solution)/shard_map/ppermute | solution.py:213
  13.2 0.5 %collective-permute-start.4 = (bf16[4,2,4224]{2,1,0:T(2,128)(2,1)S(1)}, bf16[4,2,4224]{2,1,0:T(2,128)(2,1)S(1)}, u32[]{:S(2)}, u32[]{:S(2)}) collective-permute-start(bf16[4,2,4224]{2,1,0:T(2,128)(2,1)S(1)} %stacked.1.refs_0_), channel_id=1, source_target_pairs={{0,16},{8,24},{16,0},{24,8},{1,17},{9,25},{17,1},{25,9},{2,18},{10... | collective-permute-start | bytes 202760 | tf_op jit(solution)/shard_map/ppermute | solution.py:213
  13.7 0.5 %collective-permute-start.3 = (bf16[4,2,4224]{2,1,0:T(2,128)(2,1)S(1)}, bf16[4,2,4224]{2,1,0:T(2,128)(2,1)S(1)}, u32[]{:S(2)}, u32[]{:S(2)}) collective-permute-start(bf16[4,2,4224]{2,1,0:T(2,128)(2,1)S(1)} %stacked.1.refs_0_), channel_id=1, source_target_pairs={{0,8},{8,0},{16,24},{24,16},{1,9},{9,1},{17,25},{25,17},{2,10},{10... | collective-permute-start | bytes 202760 | tf_op jit(solution)/shard_map/ppermute | solution.py:213
  14.2 3.5 %load_rows.3.refs_9_ = bf16[2048,2048]{1,0:T(8,128)(2,1)S(1)} custom-call(bf16[1,4096,2048]{2,1,0:T(8,128)(2,1)} %source.3), custom_call_target="tpu_custom_call" | custom-call | bytes 8388608 | tf_op jit(solution)/shard_map/load_rows/pallas_call | solution.py:95
  17.7 0.1 collective-permute-start.6
  17.8 0.2 collective-permute-done.3.refs_1_
  18.0 0.4 collective-permute-start.7
  18.4 0.1 collective-permute-start.8
  18.5 0.4 collective-permute-start.9
  18.9 0.2 collective-permute-done.6.refs_4_
  19.0 0.2 collective-permute-done.7.refs_5_
  19.3 0.4 collective-permute-done.8.refs_6_
  19.6 0.2 collective-permute-done.9.refs_7_
  19.8 8.0 %weighted_parts.1 = (f32[16,2,4096]{2,1,0:T(2,128)S(1)}, bf16[16,2,4096]{2,1,0:T(2,128)(2,1)S(1)}) custom-call(bf16[4,2,4224]{2,1,0:T(2,128)(2,1)S(1)} %stacked.1.refs_0_, bf16[4,2,4224]{2,1,0:T(2,128)(2,1)S(1)} %collective-permute-done.3.refs_1_, bf16[4,2,4224]{2,1,0:T(2,128)(2,1)S(1)} %collective-permute-done.4.refs_2_, ...), custom_call_target="tpu_custom_call" | custom-call | tf_op jit(solution)/shard_map/weighted_parts/pallas_call | solution.py:167
  27.8 0.4 collective-permute-start.10
  28.2 1.2 %collective-permute-done.10.partner_ref = bf16[16,2,4096]{2,1,0:T(2,128)(2,1)S(1)} collective-permute-done((bf16[16,2,4096]{2,1,0:T(2,128)(2,1)S(1)}, bf16[16,2,4096]{2,1,0:T(2,128)(2,1)S(1)}, u32[]{:S(2)}, u32[]{:S(2)}) %collective-permute-start.10) | collective-permute-done | bytes 262176 | tf_op jit(solution)/shard_map/ppermute | solution.py:213
  29.4 0.2 chip_sum.1
  29.7 17.4 %all_to_all.5 = bf16[16,2,4096]{2,1,0:T(2,128)(2,1)S(1)} all-to-all(bf16[16,2,4096]{2,1,0:T(2,128)(2,1)S(1)} %chip_sum.1), channel_id=1, replica_groups={{0,2,4,6,8,10,12,14,16,18,20,22,24,26,28,30},{1,3,5,7,9,11,13,15,17,19,..., dimensions={0} | all-to-all | bytes 524288 | tf_op jit(solution)/shard_map/all_to_all | solution.py:234
  47.1 0.8 %reduce_sum.12 = bf16[2,4096]{1,0:T(2,128)(2,1)} reduce(bf16[16,2,4096]{2,1,0:T(2,128)(2,1)S(1)} %all_to_all.5, bf16[]{:T(256)} %constant.2.clone.1), dimensions={0}, to_apply=%region_0.0 | reduce | flops 122880 | bytes 278530 | tf_op jit(solution)/shard_map/reduce_sum | solution.py:235
  (6 shorter events, 0.0 us)
Async XLA Ops:
  0.9 9.2 %collective-permute-start.2 = (bf16[2,4224]{1,0:T(2,128)(2,1)S(1)}, bf16[2,4224]{1,0:T(2,128)(2,1)S(1)}, u32[]{:S(2)}, u32[]{:S(2)}) collective-permute-start(bf16[2,4224]{1,0:T(2,128)(2,1)S(1)} %row_payload.1.refs_0_), channel_id=1, source_target_pairs={{0,6},{1,7},{2,4},{3,5},{4,2},{5,3},{6,0},{7,1},{8,14},{9,15},{10,... | collective-permute-start | bytes 50696 | tf_op jit(solution)/shard_map/ppermute | solution.py:213
  6.0 4.6 %collective-permute-start.1 = (bf16[2,4224]{1,0:T(2,128)(2,1)S(1)}, bf16[2,4224]{1,0:T(2,128)(2,1)S(1)}, u32[]{:S(2)}, u32[]{:S(2)}) collective-permute-start(bf16[2,4224]{1,0:T(2,128)(2,1)S(1)} %row_payload.1.refs_0_), channel_id=1, source_target_pairs={{0,4},{1,5},{2,6},{3,7},{4,0},{5,1},{6,2},{7,3},{8,12},{9,13},{10,... | collective-permute-start | bytes 50696 | tf_op jit(solution)/shard_map/ppermute | solution.py:213
  6.0 4.6 %collective-permute-start = (bf16[2,4224]{1,0:T(2,128)(2,1)S(1)}, bf16[2,4224]{1,0:T(2,128)(2,1)S(1)}, u32[]{:S(2)}, u32[]{:S(2)}) collective-permute-start(bf16[2,4224]{1,0:T(2,128)(2,1)S(1)} %row_payload.1.refs_0_), channel_id=1, source_target_pairs={{0,2},{1,3},{2,0},{3,1},{4,6},{5,7},{6,4},{7,5},{8,10},{9,11},{10,... | collective-permute-start | bytes 50696 | tf_op jit(solution)/shard_map/ppermute | solution.py:213
  10.7 7.1 %collective-permute-start.5 = (bf16[4,2,4224]{2,1,0:T(2,128)(2,1)S(1)}, bf16[4,2,4224]{2,1,0:T(2,128)(2,1)S(1)}, u32[]{:S(2)}, u32[]{:S(2)}) collective-permute-start(bf16[4,2,4224]{2,1,0:T(2,128)(2,1)S(1)} %stacked.1.refs_0_), channel_id=1, source_target_pairs={{0,24},{8,16},{16,8},{24,0},{1,25},{9,17},{17,9},{25,1},{2,26},{10... | collective-permute-start | bytes 202760 | tf_op jit(solution)/shard_map/ppermute | solution.py:213
  13.2 4.6 %collective-permute-start.4 = (bf16[4,2,4224]{2,1,0:T(2,128)(2,1)S(1)}, bf16[4,2,4224]{2,1,0:T(2,128)(2,1)S(1)}, u32[]{:S(2)}, u32[]{:S(2)}) collective-permute-start(bf16[4,2,4224]{2,1,0:T(2,128)(2,1)S(1)} %stacked.1.refs_0_), channel_id=1, source_target_pairs={{0,16},{8,24},{16,0},{24,8},{1,17},{9,25},{17,1},{25,9},{2,18},{10... | collective-permute-start | bytes 202760 | tf_op jit(solution)/shard_map/ppermute | solution.py:213
  13.7 4.3 %collective-permute-start.3 = (bf16[4,2,4224]{2,1,0:T(2,128)(2,1)S(1)}, bf16[4,2,4224]{2,1,0:T(2,128)(2,1)S(1)}, u32[]{:S(2)}, u32[]{:S(2)}) collective-permute-start(bf16[4,2,4224]{2,1,0:T(2,128)(2,1)S(1)} %stacked.1.refs_0_), channel_id=1, source_target_pairs={{0,8},{8,0},{16,24},{24,16},{1,9},{9,1},{17,25},{25,17},{2,10},{10... | collective-permute-start | bytes 202760 | tf_op jit(solution)/shard_map/ppermute | solution.py:213
  17.7 1.3 %collective-permute-start.6 = (bf16[4,2,4224]{2,1,0:T(2,128)(2,1)S(1)}, bf16[4,2,4224]{2,1,0:T(2,128)(2,1)S(1)}, u32[]{:S(2)}, u32[]{:S(2)}) collective-permute-start(bf16[4,2,4224]{2,1,0:T(2,128)(2,1)S(1)} %stacked.1.refs_0_), channel_id=1, source_target_pairs={{0,1},{1,0},{2,3},{3,2},{4,5},{5,4},{6,7},{7,6},{8,9},{9,8},{10,11... | collective-permute-start | bytes 202760 | tf_op jit(solution)/shard_map/ppermute | solution.py:213
  18.0 1.3 %collective-permute-start.7 = (bf16[4,2,4224]{2,1,0:T(2,128)(2,1)S(1)}, bf16[4,2,4224]{2,1,0:T(2,128)(2,1)S(1)}, u32[]{:S(2)}, u32[]{:S(2)}) collective-permute-start(bf16[4,2,4224]{2,1,0:T(2,128)(2,1)S(1)} %collective-permute-done.3.refs_1_), channel_id=1, source_target_pairs={{0,1},{1,0},{2,3},{3,2},{4,5},{5,4},{6,7},{7,6},{8,9},{9,8},{10,11... | collective-permute-start | bytes 202760 | tf_op jit(solution)/shard_map/ppermute | solution.py:213
  18.4 1.3 %collective-permute-start.8 = (bf16[4,2,4224]{2,1,0:T(2,128)(2,1)S(1)}, bf16[4,2,4224]{2,1,0:T(2,128)(2,1)S(1)}, u32[]{:S(2)}, u32[]{:S(2)}) collective-permute-start(bf16[4,2,4224]{2,1,0:T(2,128)(2,1)S(1)} %collective-permute-done.4.refs_2_), channel_id=1, source_target_pairs={{0,1},{1,0},{2,3},{3,2},{4,5},{5,4},{6,7},{7,6},{8,9},{9,8},{10,11... | collective-permute-start | bytes 202760 | tf_op jit(solution)/shard_map/ppermute | solution.py:213
  18.5 1.3 %collective-permute-start.9 = (bf16[4,2,4224]{2,1,0:T(2,128)(2,1)S(1)}, bf16[4,2,4224]{2,1,0:T(2,128)(2,1)S(1)}, u32[]{:S(2)}, u32[]{:S(2)}) collective-permute-start(bf16[4,2,4224]{2,1,0:T(2,128)(2,1)S(1)} %collective-permute-done.5.refs_3_), channel_id=1, source_target_pairs={{0,1},{1,0},{2,3},{3,2},{4,5},{5,4},{6,7},{7,6},{8,9},{9,8},{10,11... | collective-permute-start | bytes 202760 | tf_op jit(solution)/shard_map/ppermute | solution.py:213
  27.8 1.6 %collective-permute-start.10 = (bf16[16,2,4096]{2,1,0:T(2,128)(2,1)S(1)}, bf16[16,2,4096]{2,1,0:T(2,128)(2,1)S(1)}, u32[]{:S(2)}, u32[]{:S(2)}) collective-permute-start(bf16[16,2,4096]{2,1,0:T(2,128)(2,1)S(1)} %get-tuple-element.26), channel_id=1, source_target_pairs={{0,1},{1,0},{2,3},{3,2},{4,5},{5,4},{6,7},{7,6},{8,9},{9,8},{10,11... | collective-permute-start | bytes 786440 | tf_op jit(solution)/shard_map/ppermute | solution.py:213

commit v3 on v2

--- a/solution.py
+++ b/solution.py
@@ -1,3 +1,5 @@
+import math
+
 import jax
 import jax.numpy as jnp
 from jax import lax
@@ -9,6 +11,7 @@
 LANES = 128
 SMALL_VMEM = 2 << 20
 MLP_VMEM = 24 << 20
+MLP_TILE = 512
 AXES = ("grp", "fsdp")
 
 
@@ -130,13 +133,26 @@
     row_count = block_rows * len(blocks)
     half = row_count // 2
     piece_count = len(gate_up_pieces)
+    tile = math.gcd(math.gcd(hidden_dev, width), MLP_TILE)
     out_block = (half // blocks[0].shape[1], blocks[0].shape[1], width)
+
+    def projected(rows_ref, piece_refs, column):
+        sum_so_far, first = None, 0
+        for piece in piece_refs:
+            last = first + piece.shape[0]
+            term = jnp.dot(
+                rows_ref[:, first:last],
+                piece[:, pl.ds(column, tile)],
+                preferred_element_type=jnp.float32,
+            )
+            sum_so_far, first = term if sum_so_far is None else sum_so_far + term, last
+        return sum_so_far
 
     def kernel(*refs):
         my_expert = device_index() // (FF // hidden_dev)
         block_refs, refs = refs[: len(blocks)], refs[len(blocks) :]
         piece_refs, refs = refs[:piece_count], refs[piece_count:]
-        down_hbm, own_out, other_out, rows_ref, down_ref, sem = refs
+        down_hbm, own_out, other_out, rows_ref, hidden_ref, down_ref, sem = refs
         fetch = pltpu.make_async_copy(down_hbm.at[0], down_ref, sem)
         fetch.start()
         for index, source in enumerate(block_refs):
@@ -150,18 +166,24 @@
         row_weight = jnp.sum(
             jnp.where(sent_routes == my_expert, combine, 0.0), axis=-1, keepdims=True
         )
-        projected, first = None, 0
-        for piece in piece_refs:
-            last = first + piece.shape[0]
-            term = jnp.dot(rows_ref[:, first:last], piece[...], preferred_element_type=jnp.float32)
-            projected, first = term if projected is None else projected + term, last
-        gate, up = projected[:, :hidden_dev], projected[:, hidden_dev:]
-        hidden = (jax.nn.silu(gate) * up).astype(jnp.bfloat16)
+        @pl.loop(0, hidden_dev // tile)
+        def _(step):
+            column = pl.multiple_of(step * tile, tile)
+            gate = projected(rows_ref, piece_refs, column)
+            up = projected(rows_ref, piece_refs, pl.multiple_of(hidden_dev + column, tile))
+            hidden_ref[:, pl.ds(column, tile)] = (jax.nn.silu(gate) * up).astype(jnp.bfloat16)
+
         fetch.wait()
-        part = jnp.dot(hidden, down_ref[...], preferred_element_type=jnp.float32)
-        weighted = part.astype(jnp.bfloat16).astype(jnp.float32) * row_weight
-        own_out[...] = weighted[:half].reshape(out_block)
-        other_out[...] = weighted[half:].reshape(out_block).astype(jnp.bfloat16)
+        for column in range(0, width, tile):
+            columns = slice(column, column + tile)
+            part = jnp.dot(
+                hidden_ref[...], down_ref[:, columns], preferred_element_type=jnp.float32
+            )
+            weighted = part.astype(jnp.bfloat16).astype(jnp.float32) * row_weight
+            own_out[:, :, columns] = weighted[:half].reshape(out_block[:2] + (tile,))
+            other_out[:, :, columns] = (
+                weighted[half:].reshape(out_block[:2] + (tile,)).astype(jnp.bfloat16)
+            )
 
     vmem = pl.BlockSpec(memory_space=pltpu.VMEM)
     return pl.pallas_call(
@@ -175,6 +197,7 @@
         out_specs=[vmem] * 2,
         scratch_shapes=[
             pltpu.VMEM((row_count, total), jnp.bfloat16),
+            pltpu.VMEM((row_count, hidden_dev), jnp.bfloat16),
             pltpu.VMEM(w_down.shape[1:], w_down.dtype),
             pltpu.SemaphoreType.DMA,
         ],

time: 48.2 us -> 45.4 us (0.942)
  Pallas kernels: 16.1 us -> 13.3 us
    pallas_call x1, Pallas kernels: 8.03 us -> 5.23 us  [weighted_parts(): pl.pallas_call(kernel, out_shape=[jax.ShapeDtypeStruct(out_block, jnp.flo...]
  transfers between devices with their start and end apart: 11 -> 11, of which waited for: 7 -> 7; matrix products, arithmetic and copies ran while one was open for 0% -> 0% of each run, Pallas kernels for 14% -> 15%
where the time goes in v3:
time: 45.4 us; the launch traced here: 45.1 us
  blocking collectives  17.4 us (38%)
  Pallas kernels  13.3 us (29%)
  starting transfers between devices  10.7 us (24%)
  waiting for transfers between devices  2.78 us (6%)
  other arithmetic  0.83 us (2%)
    all_to_all x1, blocking collectives, every_row(): lax.all_to_all(summed, AXES, 0, 0, axis_index_groups=same_core, tiled=True)  17.4 us
    ppermute x11, starting transfers between devices, exchanged(): return lax.ppermute(value, axis, [(d, d ^ flip) for d in range(size)])  10.7 us
    pallas_call x2, Pallas kernels, load_rows(): pl.pallas_call(kernel, out_shape=pltpu.VMEM(shape, weight.dtype), in_spec...  6.94 us
    pallas_call x1, Pallas kernels, weighted_parts(): pl.pallas_call(kernel, out_shape=[jax.ShapeDtypeStruct(out_block, jnp.flo...  5.23 us
    ppermute x11, waiting for transfers between devices, exchanged(): return lax.ppermute(value, axis, [(d, d ^ flip) for d in range(size)])  2.78 us
    pallas_call x1, Pallas kernels, row_payload(): pl.pallas_call(kernel, out_shape=jax.ShapeDtypeStruct((rows_dev, total),...  0.91 us
  transfers between devices with their start and end apart: 11, of which 7 were waited for; matrix products, arithmetic and copies ran while one was open for 0% of the time, Pallas kernels for 15%

profile of v3, /device:TPU:0, one launch (start us, length us, event | category | flops | bytes accessed | tf_op | source)
XLA Modules:
  0.0 45.1 jit_solution(7354137982298308512)
XLA Ops:
  0.0 0.9 %row_payload.1.refs_0_ = bf16[2,4224]{1,0:T(2,128)(2,1)S(1)} custom-call(bf16[2,4096]{1,0:T(2,128)(2,1)} %refs_0_.1, f32[1,4096]{1,0:T(1,128)} %bitcast.1, s32[2,8]{1,0:T(2,128)} %refs_2_.1, bf16[2,8]{1,0:T(2,128)(2,1)} %refs_3_.1), custom_call_target="tpu_custom_call" | custom-call | tf_op jit(solution)/shard_map/row_payload/pallas_call | solution.py:68
  0.9 5.1 %collective-permute-start.2 = (bf16[2,4224]{1,0:T(2,128)(2,1)S(1)}, bf16[2,4224]{1,0:T(2,128)(2,1)S(1)}, u32[]{:S(2)}, u32[]{:S(2)}) collective-permute-start(bf16[2,4224]{1,0:T(2,128)(2,1)S(1)} %row_payload.1.refs_0_), channel_id=1, source_target_pairs={{0,6},{1,7},{2,4},{3,5},{4,2},{5,3},{6,0},{7,1},{8,14},{9,15},{10,... | collective-permute-start | bytes 50696 | tf_op jit(solution)/shard_map/ppermute | solution.py:236
  6.0 0.6 %collective-permute-start = (bf16[2,4224]{1,0:T(2,128)(2,1)S(1)}, bf16[2,4224]{1,0:T(2,128)(2,1)S(1)}, u32[]{:S(2)}, u32[]{:S(2)}) collective-permute-start(bf16[2,4224]{1,0:T(2,128)(2,1)S(1)} %row_payload.1.refs_0_), channel_id=1, source_target_pairs={{0,2},{1,3},{2,0},{3,1},{4,6},{5,7},{6,4},{7,5},{8,10},{9,11},{10,... | collective-permute-start | bytes 50696 | tf_op jit(solution)/shard_map/ppermute | solution.py:236
  6.7 3.5 %load_rows.2.refs_8_ = bf16[2048,2048]{1,0:T(8,128)(2,1)S(1)} custom-call(bf16[1,4096,2048]{2,1,0:T(8,128)(2,1)} %source.3), custom_call_target="tpu_custom_call" | custom-call | bytes 8388608 | tf_op jit(solution)/shard_map/load_rows/pallas_call | solution.py:98
  10.2 0.5 %collective-permute-done.1.refs_2_ = bf16[2,4224]{1,0:T(2,128)(2,1)S(1)} collective-permute-done((bf16[2,4224]{1,0:T(2,128)(2,1)S(1)}, bf16[2,4224]{1,0:T(2,128)(2,1)S(1)}, u32[]{:S(2)}, u32[]{:S(2)}) %collective-permute-start.1) | collective-permute-done | bytes 16928 | tf_op jit(solution)/shard_map/ppermute | solution.py:236
  10.7 2.5 %collective-permute-start.5 = (bf16[4,2,4224]{2,1,0:T(2,128)(2,1)S(1)}, bf16[4,2,4224]{2,1,0:T(2,128)(2,1)S(1)}, u32[]{:S(2)}, u32[]{:S(2)}) collective-permute-start(bf16[4,2,4224]{2,1,0:T(2,128)(2,1)S(1)} %stacked.1.refs_0_), channel_id=1, source_target_pairs={{0,24},{8,16},{16,8},{24,0},{1,25},{9,17},{17,9},{25,1},{2,26},{10... | collective-permute-start | bytes 202760 | tf_op jit(solution)/shard_map/ppermute | solution.py:236
  13.2 0.5 %collective-permute-start.4 = (bf16[4,2,4224]{2,1,0:T(2,128)(2,1)S(1)}, bf16[4,2,4224]{2,1,0:T(2,128)(2,1)S(1)}, u32[]{:S(2)}, u32[]{:S(2)}) collective-permute-start(bf16[4,2,4224]{2,1,0:T(2,128)(2,1)S(1)} %stacked.1.refs_0_), channel_id=1, source_target_pairs={{0,16},{8,24},{16,0},{24,8},{1,17},{9,25},{17,1},{25,9},{2,18},{10... | collective-permute-start | bytes 202760 | tf_op jit(solution)/shard_map/ppermute | solution.py:236
  13.7 0.5 %collective-permute-start.3 = (bf16[4,2,4224]{2,1,0:T(2,128)(2,1)S(1)}, bf16[4,2,4224]{2,1,0:T(2,128)(2,1)S(1)}, u32[]{:S(2)}, u32[]{:S(2)}) collective-permute-start(bf16[4,2,4224]{2,1,0:T(2,128)(2,1)S(1)} %stacked.1.refs_0_), channel_id=1, source_target_pairs={{0,8},{8,0},{16,24},{24,16},{1,9},{9,1},{17,25},{25,17},{2,10},{10... | collective-permute-start | bytes 202760 | tf_op jit(solution)/shard_map/ppermute | solution.py:236
  14.2 3.5 %load_rows.3.refs_9_ = bf16[2048,2048]{1,0:T(8,128)(2,1)S(1)} custom-call(bf16[1,4096,2048]{2,1,0:T(8,128)(2,1)} %source.3), custom_call_target="tpu_custom_call" | custom-call | bytes 8388608 | tf_op jit(solution)/shard_map/load_rows/pallas_call | solution.py:98
  17.7 0.1 collective-permute-start.6
  17.8 0.2 collective-permute-done.3.refs_1_
  18.0 0.4 collective-permute-start.7
  18.4 0.1 collective-permute-start.8
  18.5 0.4 collective-permute-start.9
  18.9 0.2 collective-permute-done.6.refs_4_
  19.0 0.2 collective-permute-done.7.refs_5_
  19.3 0.4 collective-permute-done.8.refs_6_
  19.6 0.2 collective-permute-done.9.refs_7_
  19.8 5.2 %weighted_parts.1 = (f32[16,2,4096]{2,1,0:T(2,128)S(1)}, bf16[16,2,4096]{2,1,0:T(2,128)(2,1)S(1)}) custom-call(bf16[4,2,4224]{2,1,0:T(2,128)(2,1)S(1)} %stacked.1.refs_0_, bf16[4,2,4224]{2,1,0:T(2,128)(2,1)S(1)} %collective-permute-done.3.refs_1_, bf16[4,2,4224]{2,1,0:T(2,128)(2,1)S(1)} %collective-permute-done.4.refs_2_, ...), custom_call_target="tpu_custom_call" | custom-call | tf_op jit(solution)/shard_map/weighted_parts/pallas_call | solution.py:189
  25.0 0.4 collective-permute-start.10
  25.5 1.2 %collective-permute-done.10.partner_ref = bf16[16,2,4096]{2,1,0:T(2,128)(2,1)S(1)} collective-permute-done((bf16[16,2,4096]{2,1,0:T(2,128)(2,1)S(1)}, bf16[16,2,4096]{2,1,0:T(2,128)(2,1)S(1)}, u32[]{:S(2)}, u32[]{:S(2)}) %collective-permute-start.10) | collective-permute-done | bytes 262176 | tf_op jit(solution)/shard_map/ppermute | solution.py:236
  26.6 0.2 chip_sum.1
  26.9 17.4 %all_to_all.5 = bf16[16,2,4096]{2,1,0:T(2,128)(2,1)S(1)} all-to-all(bf16[16,2,4096]{2,1,0:T(2,128)(2,1)S(1)} %chip_sum.1), channel_id=1, replica_groups={{0,2,4,6,8,10,12,14,16,18,20,22,24,26,28,30},{1,3,5,7,9,11,13,15,17,19,..., dimensions={0} | all-to-all | bytes 524288 | tf_op jit(solution)/shard_map/all_to_all | solution.py:257
  44.3 0.8 %reduce_sum.12 = bf16[2,4096]{1,0:T(2,128)(2,1)} reduce(bf16[16,2,4096]{2,1,0:T(2,128)(2,1)S(1)} %all_to_all.5, bf16[]{:T(256)} %constant.2.clone.1), dimensions={0}, to_apply=%region_0.0 | reduce | flops 122880 | bytes 278530 | tf_op jit(solution)/shard_map/reduce_sum | solution.py:258
  (6 shorter events, 0.0 us)
Async XLA Ops:
  0.9 9.2 %collective-permute-start.2 = (bf16[2,4224]{1,0:T(2,128)(2,1)S(1)}, bf16[2,4224]{1,0:T(2,128)(2,1)S(1)}, u32[]{:S(2)}, u32[]{:S(2)}) collective-permute-start(bf16[2,4224]{1,0:T(2,128)(2,1)S(1)} %row_payload.1.refs_0_), channel_id=1, source_target_pairs={{0,6},{1,7},{2,4},{3,5},{4,2},{5,3},{6,0},{7,1},{8,14},{9,15},{10,... | collective-permute-start | bytes 50696 | tf_op jit(solution)/shard_map/ppermute | solution.py:236
  6.0 4.6 %collective-permute-start.1 = (bf16[2,4224]{1,0:T(2,128)(2,1)S(1)}, bf16[2,4224]{1,0:T(2,128)(2,1)S(1)}, u32[]{:S(2)}, u32[]{:S(2)}) collective-permute-start(bf16[2,4224]{1,0:T(2,128)(2,1)S(1)} %row_payload.1.refs_0_), channel_id=1, source_target_pairs={{0,4},{1,5},{2,6},{3,7},{4,0},{5,1},{6,2},{7,3},{8,12},{9,13},{10,... | collective-permute-start | bytes 50696 | tf_op jit(solution)/shard_map/ppermute | solution.py:236
  6.0 4.6 %collective-permute-start = (bf16[2,4224]{1,0:T(2,128)(2,1)S(1)}, bf16[2,4224]{1,0:T(2,128)(2,1)S(1)}, u32[]{:S(2)}, u32[]{:S(2)}) collective-permute-start(bf16[2,4224]{1,0:T(2,128)(2,1)S(1)} %row_payload.1.refs_0_), channel_id=1, source_target_pairs={{0,2},{1,3},{2,0},{3,1},{4,6},{5,7},{6,4},{7,5},{8,10},{9,11},{10,... | collective-permute-start | bytes 50696 | tf_op jit(solution)/shard_map/ppermute | solution.py:236
  10.7 7.1 %collective-permute-start.5 = (bf16[4,2,4224]{2,1,0:T(2,128)(2,1)S(1)}, bf16[4,2,4224]{2,1,0:T(2,128)(2,1)S(1)}, u32[]{:S(2)}, u32[]{:S(2)}) collective-permute-start(bf16[4,2,4224]{2,1,0:T(2,128)(2,1)S(1)} %stacked.1.refs_0_), channel_id=1, source_target_pairs={{0,24},{8,16},{16,8},{24,0},{1,25},{9,17},{17,9},{25,1},{2,26},{10... | collective-permute-start | bytes 202760 | tf_op jit(solution)/shard_map/ppermute | solution.py:236
  13.2 4.6 %collective-permute-start.4 = (bf16[4,2,4224]{2,1,0:T(2,128)(2,1)S(1)}, bf16[4,2,4224]{2,1,0:T(2,128)(2,1)S(1)}, u32[]{:S(2)}, u32[]{:S(2)}) collective-permute-start(bf16[4,2,4224]{2,1,0:T(2,128)(2,1)S(1)} %stacked.1.refs_0_), channel_id=1, source_target_pairs={{0,16},{8,24},{16,0},{24,8},{1,17},{9,25},{17,1},{25,9},{2,18},{10... | collective-permute-start | bytes 202760 | tf_op jit(solution)/shard_map/ppermute | solution.py:236
  13.7 4.3 %collective-permute-start.3 = (bf16[4,2,4224]{2,1,0:T(2,128)(2,1)S(1)}, bf16[4,2,4224]{2,1,0:T(2,128)(2,1)S(1)}, u32[]{:S(2)}, u32[]{:S(2)}) collective-permute-start(bf16[4,2,4224]{2,1,0:T(2,128)(2,1)S(1)} %stacked.1.refs_0_), channel_id=1, source_target_pairs={{0,8},{8,0},{16,24},{24,16},{1,9},{9,1},{17,25},{25,17},{2,10},{10... | collective-permute-start | bytes 202760 | tf_op jit(solution)/shard_map/ppermute | solution.py:236
  17.7 1.3 %collective-permute-start.6 = (bf16[4,2,4224]{2,1,0:T(2,128)(2,1)S(1)}, bf16[4,2,4224]{2,1,0:T(2,128)(2,1)S(1)}, u32[]{:S(2)}, u32[]{:S(2)}) collective-permute-start(bf16[4,2,4224]{2,1,0:T(2,128)(2,1)S(1)} %stacked.1.refs_0_), channel_id=1, source_target_pairs={{0,1},{1,0},{2,3},{3,2},{4,5},{5,4},{6,7},{7,6},{8,9},{9,8},{10,11... | collective-permute-start | bytes 202760 | tf_op jit(solution)/shard_map/ppermute | solution.py:236
  18.0 1.3 %collective-permute-start.7 = (bf16[4,2,4224]{2,1,0:T(2,128)(2,1)S(1)}, bf16[4,2,4224]{2,1,0:T(2,128)(2,1)S(1)}, u32[]{:S(2)}, u32[]{:S(2)}) collective-permute-start(bf16[4,2,4224]{2,1,0:T(2,128)(2,1)S(1)} %collective-permute-done.3.refs_1_), channel_id=1, source_target_pairs={{0,1},{1,0},{2,3},{3,2},{4,5},{5,4},{6,7},{7,6},{8,9},{9,8},{10,11... | collective-permute-start | bytes 202760 | tf_op jit(solution)/shard_map/ppermute | solution.py:236
  18.4 1.3 %collective-permute-start.8 = (bf16[4,2,4224]{2,1,0:T(2,128)(2,1)S(1)}, bf16[4,2,4224]{2,1,0:T(2,128)(2,1)S(1)}, u32[]{:S(2)}, u32[]{:S(2)}) collective-permute-start(bf16[4,2,4224]{2,1,0:T(2,128)(2,1)S(1)} %collective-permute-done.4.refs_2_), channel_id=1, source_target_pairs={{0,1},{1,0},{2,3},{3,2},{4,5},{5,4},{6,7},{7,6},{8,9},{9,8},{10,11... | collective-permute-start | bytes 202760 | tf_op jit(solution)/shard_map/ppermute | solution.py:236
  18.5 1.3 %collective-permute-start.9 = (bf16[4,2,4224]{2,1,0:T(2,128)(2,1)S(1)}, bf16[4,2,4224]{2,1,0:T(2,128)(2,1)S(1)}, u32[]{:S(2)}, u32[]{:S(2)}) collective-permute-start(bf16[4,2,4224]{2,1,0:T(2,128)(2,1)S(1)} %collective-permute-done.5.refs_3_), channel_id=1, source_target_pairs={{0,1},{1,0},{2,3},{3,2},{4,5},{5,4},{6,7},{7,6},{8,9},{9,8},{10,11... | collective-permute-start | bytes 202760 | tf_op jit(solution)/shard_map/ppermute | solution.py:236
  25.0 1.6 %collective-permute-start.10 = (bf16[16,2,4096]{2,1,0:T(2,128)(2,1)S(1)}, bf16[16,2,4096]{2,1,0:T(2,128)(2,1)S(1)}, u32[]{:S(2)}, u32[]{:S(2)}) collective-permute-start(bf16[16,2,4096]{2,1,0:T(2,128)(2,1)S(1)} %get-tuple-element.26), channel_id=1, source_target_pairs={{0,1},{1,0},{2,3},{3,2},{4,5},{5,4},{6,7},{7,6},{8,9},{9,8},{10,11... | collective-permute-start | bytes 786440 | tf_op jit(solution)/shard_map/ppermute | solution.py:236

commit v4 on v3

--- a/solution.py
+++ b/solution.py
@@ -12,6 +12,7 @@
 SMALL_VMEM = 2 << 20
 MLP_VMEM = 24 << 20
 MLP_TILE = 512
+PREFETCH_WINDOW = pl.CostEstimate(flops=64 << 30, transcendentals=0, bytes_accessed=256 << 20)
 AXES = ("grp", "fsdp")
 
 
@@ -77,38 +78,6 @@
     )(*[pltpu.with_memory_space_constraint(o, pltpu.HBM) for o in operands])
 
 
-def load_rows(weight, first, count, chunk_count=8):
-    step = count // chunk_count
-
-    def kernel(source, target, sems):
-        copies = [
-            pltpu.make_async_copy(
-                source.at[0, pl.ds(first + chunk * step, step)],
-                target.at[pl.ds(chunk * step, step)],
-                sems.at[chunk],
-            )
-            for chunk in range(chunk_count)
-        ]
-        for copy in copies:
-            copy.start()
-        for copy in copies:
-            copy.wait()
-
-    shape = (count, weight.shape[2])
-    return pl.pallas_call(
-        kernel,
-        out_shape=pltpu.VMEM(shape, weight.dtype),
-        in_specs=[pl.BlockSpec(memory_space=pltpu.HBM)],
-        out_specs=pl.BlockSpec(memory_space=pltpu.VMEM),
-        scratch_shapes=[pltpu.SemaphoreType.DMA((chunk_count,))],
-        compiler_params=pltpu.CompilerParams(vmem_limit_bytes=SMALL_VMEM),
-        cost_estimate=pl.CostEstimate(
-            flops=0, transcendentals=0, bytes_accessed=2 * count * weight.shape[2]
-        ),
-        name="load_rows",
-    )(pltpu.with_memory_space_constraint(weight, pltpu.HBM))
-
-
 def stacked(pieces):
     def kernel(*refs):
         for index, ref in enumerate(refs[:-1]):
@@ -121,6 +90,7 @@
         in_specs=[vmem] * len(pieces),
         out_specs=vmem,
         compiler_params=pltpu.CompilerParams(vmem_limit_bytes=SMALL_VMEM),
+        cost_estimate=PREFETCH_WINDOW,
         name="stacked",
     )(*pieces)
 
@@ -241,17 +211,14 @@
     shard_count = lax.axis_size("fsdp")
     group_count = lax.axis_size("grp")
     same_core = [[d for d in range(device_count) if d % 2 == k] for k in range(2)]
-    depth = w_gate_up.shape[1] // 2
 
     payload = row_payload(tokens, norm_gain, routes, gate_probs)
     column = [payload] + [exchanged(payload, "fsdp", k) for k in range(2, shard_count, 2)]
-    column, first = lax.optimization_barrier((column, load_rows(w_gate_up, 0, depth)))
     column = stacked(column)
     plane = [exchanged(column, "grp", k) for k in range(1, group_count)]
-    plane, second = lax.optimization_barrier((plane, load_rows(w_gate_up, depth, depth)))
     own = [column] + plane
     other = [exchanged(block, "fsdp", 1) for block in own]
-    own_part, other_part = weighted_parts(own, other, [first, second], w_down, routes.shape[1])
+    own_part, other_part = weighted_parts(own, other, [w_gate_up[0]], w_down, routes.shape[1])
     from_partner = exchanged(other_part, "fsdp", 1)
     summed = chip_sum(own_part, from_partner)
     returned = lax.all_to_all(summed, AXES, 0, 0, axis_index_groups=same_core, tiled=True)

time: 45.4 us -> 42.5 us (0.936)
  waiting for transfers between devices: 2.78 us -> 10.4 us
  Pallas kernels: 13.3 us -> 6.52 us
  blocking collectives: 17.4 us -> 15 us
  starting transfers between devices: 10.7 us -> 9.55 us
    ppermute x11, waiting for transfers between devices: 2.78 us -> 10.4 us  [exchanged(): return lax.ppermute(value, axis, [(d, d ^ flip) for d in range(size)])]
    pallas_call x2 -> x0, Pallas kernels: 6.94 us -> none  [load_rows(): pl.pallas_call(kernel, out_shape=pltpu.VMEM(shape, weight.dtype), in_spec...]
    all_to_all x1, blocking collectives: 17.4 us -> 15 us  [every_row(): lax.all_to_all(summed, AXES, 0, 0, axis_index_groups=same_core, tiled=True)]
    ppermute x11, starting transfers between devices: 10.7 us -> 9.55 us  [exchanged(): return lax.ppermute(value, axis, [(d, d ^ flip) for d in range(size)])]
  transfers between devices with their start and end apart: 11 -> 11, of which waited for: 7 -> 8; matrix products, arithmetic and copies ran while one was open for 0% -> 0% of each run, Pallas kernels for 15% -> 0%
where the time goes in v4:
time: 42.5 us; the launch traced here: 42.4 us
  blocking collectives  15 us (35%)
  waiting for transfers between devices  10.4 us (24%)
  starting transfers between devices  9.55 us (22%)
  Pallas kernels  6.52 us (15%)
  other arithmetic  0.83 us (2%)
    all_to_all x1, blocking collectives, every_row(): lax.all_to_all(summed, AXES, 0, 0, axis_index_groups=same_core, tiled=True)  15 us
    ppermute x11, waiting for transfers between devices, exchanged(): return lax.ppermute(value, axis, [(d, d ^ flip) for d in range(size)])  10.4 us
    ppermute x11, starting transfers between devices, exchanged(): return lax.ppermute(value, axis, [(d, d ^ flip) for d in range(size)])  9.55 us
    pallas_call x1, Pallas kernels, weighted_parts(): pl.pallas_call(kernel, out_shape=[jax.ShapeDtypeStruct(out_block, jnp.flo...  5.22 us
    pallas_call x1, Pallas kernels, row_payload(): pl.pallas_call(kernel, out_shape=jax.ShapeDtypeStruct((rows_dev, total),...  1.06 us
  transfers between devices with their start and end apart: 11, of which 8 were waited for; matrix products, arithmetic and copies ran while one was open for 0% of the time, Pallas kernels for 0%

profile of v4, /device:TPU:0, one launch (start us, length us, event | category | flops | bytes accessed | tf_op | source)
XLA Modules:
  0.0 42.4 jit_solution(5496065699716811450)
XLA Ops:
  0.0 1.1 %row_payload.1.refs_0_ = bf16[2,4224]{1,0:T(2,128)(2,1)S(1)} custom-call(bf16[2,4096]{1,0:T(2,128)(2,1)} %refs_0_.1, f32[1,4096]{1,0:T(1,128)} %bitcast.5, s32[2,8]{1,0:T(2,128)} %refs_2_.1, bf16[2,8]{1,0:T(2,128)(2,1)} %refs_3_.1), custom_call_target="tpu_custom_call" | custom-call | tf_op jit(solution)/shard_map/row_payload/pallas_call | solution.py:69
  1.1 0.0 slice-start.1
  1.1 0.0 slice-start.2
  1.1 0.0 slice-start.3
  1.1 5.1 %collective-permute-start.2 = (bf16[2,4224]{1,0:T(2,128)(2,1)S(1)}, bf16[2,4224]{1,0:T(2,128)(2,1)S(1)}, u32[]{:S(2)}, u32[]{:S(2)}) collective-permute-start(bf16[2,4224]{1,0:T(2,128)(2,1)S(1)} %row_payload.1.refs_0_), channel_id=1, source_target_pairs={{0,6},{1,7},{2,4},{3,5},{4,2},{5,3},{6,0},{7,1},{8,14},{9,15},{10,... | collective-permute-start | bytes 50696 | tf_op jit(solution)/shard_map/ppermute | solution.py:206
  6.2 0.6 %collective-permute-start = (bf16[2,4224]{1,0:T(2,128)(2,1)S(1)}, bf16[2,4224]{1,0:T(2,128)(2,1)S(1)}, u32[]{:S(2)}, u32[]{:S(2)}) collective-permute-start(bf16[2,4224]{1,0:T(2,128)(2,1)S(1)} %row_payload.1.refs_0_), channel_id=1, source_target_pairs={{0,2},{1,3},{2,0},{3,1},{4,6},{5,7},{6,4},{7,5},{8,10},{9,11},{10,... | collective-permute-start | bytes 50696 | tf_op jit(solution)/shard_map/ppermute | solution.py:206
  6.9 1.1 %collective-permute-done.2.refs_3_ = bf16[2,4224]{1,0:T(2,128)(2,1)S(1)} collective-permute-done((bf16[2,4224]{1,0:T(2,128)(2,1)S(1)}, bf16[2,4224]{1,0:T(2,128)(2,1)S(1)}, u32[]{:S(2)}, u32[]{:S(2)}) %collective-permute-start.2) | collective-permute-done | bytes 16928 | tf_op jit(solution)/shard_map/ppermute | solution.py:206
  7.9 2.9 %collective-permute-done.1.refs_2_ = bf16[2,4224]{1,0:T(2,128)(2,1)S(1)} collective-permute-done((bf16[2,4224]{1,0:T(2,128)(2,1)S(1)}, bf16[2,4224]{1,0:T(2,128)(2,1)S(1)}, u32[]{:S(2)}, u32[]{:S(2)}) %collective-permute-start.1) | collective-permute-done | bytes 16928 | tf_op jit(solution)/shard_map/ppermute | solution.py:206
  10.9 2.5 %collective-permute-start.5 = (bf16[4,2,4224]{2,1,0:T(2,128)(2,1)S(1)}, bf16[4,2,4224]{2,1,0:T(2,128)(2,1)S(1)}, u32[]{:S(2)}, u32[]{:S(2)}) collective-permute-start(bf16[4,2,4224]{2,1,0:T(2,128)(2,1)S(1)} %stacked.1.refs_0_), channel_id=1, source_target_pairs={{0,24},{8,16},{16,8},{24,0},{1,25},{9,17},{17,9},{25,1},{2,26},{10... | collective-permute-start | bytes 202760 | tf_op jit(solution)/shard_map/ppermute | solution.py:206
  13.4 0.5 %collective-permute-start.4 = (bf16[4,2,4224]{2,1,0:T(2,128)(2,1)S(1)}, bf16[4,2,4224]{2,1,0:T(2,128)(2,1)S(1)}, u32[]{:S(2)}, u32[]{:S(2)}) collective-permute-start(bf16[4,2,4224]{2,1,0:T(2,128)(2,1)S(1)} %stacked.1.refs_0_), channel_id=1, source_target_pairs={{0,16},{8,24},{16,0},{24,8},{1,17},{9,25},{17,1},{25,9},{2,18},{10... | collective-permute-start | bytes 202760 | tf_op jit(solution)/shard_map/ppermute | solution.py:206
  13.9 0.5 %collective-permute-start.3 = (bf16[4,2,4224]{2,1,0:T(2,128)(2,1)S(1)}, bf16[4,2,4224]{2,1,0:T(2,128)(2,1)S(1)}, u32[]{:S(2)}, u32[]{:S(2)}) collective-permute-start(bf16[4,2,4224]{2,1,0:T(2,128)(2,1)S(1)} %stacked.1.refs_0_), channel_id=1, source_target_pairs={{0,8},{8,0},{16,24},{24,16},{1,9},{9,1},{17,25},{25,17},{2,10},{10... | collective-permute-start | bytes 202760 | tf_op jit(solution)/shard_map/ppermute | solution.py:206
  14.4 2.3 %collective-permute-done.5.refs_3_ = bf16[4,2,4224]{2,1,0:T(2,128)(2,1)S(1)} collective-permute-done((bf16[4,2,4224]{2,1,0:T(2,128)(2,1)S(1)}, bf16[4,2,4224]{2,1,0:T(2,128)(2,1)S(1)}, u32[]{:S(2)}, u32[]{:S(2)}) %collective-permute-start.5) | collective-permute-done | bytes 67616 | tf_op jit(solution)/shard_map/ppermute | solution.py:206
  16.7 0.0 collective-permute-start.9
  16.7 0.9 %collective-permute-done.4.refs_2_ = bf16[4,2,4224]{2,1,0:T(2,128)(2,1)S(1)} collective-permute-done((bf16[4,2,4224]{2,1,0:T(2,128)(2,1)S(1)}, bf16[4,2,4224]{2,1,0:T(2,128)(2,1)S(1)}, u32[]{:S(2)}, u32[]{:S(2)}) %collective-permute-start.4) | collective-permute-done | bytes 67616 | tf_op jit(solution)/shard_map/ppermute | solution.py:206
  17.7 0.5 %collective-permute-done.3.refs_1_ = bf16[4,2,4224]{2,1,0:T(2,128)(2,1)S(1)} collective-permute-done((bf16[4,2,4224]{2,1,0:T(2,128)(2,1)S(1)}, bf16[4,2,4224]{2,1,0:T(2,128)(2,1)S(1)}, u32[]{:S(2)}, u32[]{:S(2)}) %collective-permute-start.3) | collective-permute-done | bytes 67616 | tf_op jit(solution)/shard_map/ppermute | solution.py:206
  18.2 0.0 collective-permute-start.7
  18.2 0.7 %collective-permute-done.8.refs_6_ = bf16[4,2,4224]{2,1,0:T(2,128)(2,1)S(1)} collective-permute-done((bf16[4,2,4224]{2,1,0:T(2,128)(2,1)S(1)}, bf16[4,2,4224]{2,1,0:T(2,128)(2,1)S(1)}, u32[]{:S(2)}, u32[]{:S(2)}) %collective-permute-start.8) | collective-permute-done | bytes 67616 | tf_op jit(solution)/shard_map/ppermute | solution.py:206
  18.9 0.5 %collective-permute-done.7.refs_5_ = bf16[4,2,4224]{2,1,0:T(2,128)(2,1)S(1)} collective-permute-done((bf16[4,2,4224]{2,1,0:T(2,128)(2,1)S(1)}, bf16[4,2,4224]{2,1,0:T(2,128)(2,1)S(1)}, u32[]{:S(2)}, u32[]{:S(2)}) %collective-permute-start.7) | collective-permute-done | bytes 67616 | tf_op jit(solution)/shard_map/ppermute | solution.py:206
  19.5 5.2 %weighted_parts.1 = (f32[16,2,4096]{2,1,0:T(2,128)S(1)}, bf16[16,2,4096]{2,1,0:T(2,128)(2,1)S(1)}) custom-call(bf16[4,2,4224]{2,1,0:T(2,128)(2,1)S(1)} %stacked.1.refs_0_, bf16[4,2,4224]{2,1,0:T(2,128)(2,1)S(1)} %collective-permute-done.3.refs_1_, bf16[4,2,4224]{2,1,0:T(2,128)(2,1)S(1)} %collective-permute-done.4.refs_2_, ...), custom_call_target="tpu_custom_call" | custom-call | tf_op jit(solution)/shard_map/weighted_parts/pallas_call | solution.py:159
  24.7 0.2 collective-permute-start.10
  24.9 1.4 %collective-permute-done.10.partner_ref = bf16[16,2,4096]{2,1,0:T(2,128)(2,1)S(1)} collective-permute-done((bf16[16,2,4096]{2,1,0:T(2,128)(2,1)S(1)}, bf16[16,2,4096]{2,1,0:T(2,128)(2,1)S(1)}, u32[]{:S(2)}, u32[]{:S(2)}) %collective-permute-start.10) | collective-permute-done | bytes 262176 | tf_op jit(solution)/shard_map/ppermute | solution.py:206
  26.3 0.2 chip_sum.1
  26.5 15.0 %all_to_all.5 = bf16[16,2,4096]{2,1,0:T(2,128)(2,1)S(1)} all-to-all(bf16[16,2,4096]{2,1,0:T(2,128)(2,1)S(1)} %chip_sum.1), channel_id=1, replica_groups={{0,2,4,6,8,10,12,14,16,18,20,22,24,26,28,30},{1,3,5,7,9,11,13,15,17,19,..., dimensions={0} | all-to-all | bytes 524288 | tf_op jit(solution)/shard_map/all_to_all | solution.py:224
  41.5 0.8 %reduce_sum.12 = bf16[2,4096]{1,0:T(2,128)(2,1)} reduce(bf16[16,2,4096]{2,1,0:T(2,128)(2,1)S(1)} %all_to_all.5, bf16[]{:T(256)} %constant.2.clone.1), dimensions={0}, to_apply=%region_0.0 | reduce | flops 122880 | bytes 278530 | tf_op jit(solution)/shard_map/reduce_sum | solution.py:225
  (13 shorter events, 0.0 us)
Async XLA Ops:
  0.0 19.4 %slice-start = ((s8[16777216]{0:T(1024)(128)(4,1)}), s8[4194304]{0:T(1024)(128)(4,1)S(1)}, s32[]{:S(2)}) async-start(s8[16777216]{0:T(1024)(128)(4,1)} %bitcast.2), calls=%async_computation.1 | async-start | bytes 8388608
  1.1 18.4 %slice-start.1 = ((s8[16777216]{0:T(1024)(128)(4,1)}), s8[4194304]{0:T(1024)(128)(4,1)S(1)}, s32[]{:S(2)}) async-start(s8[16777216]{0:T(1024)(128)(4,1)} %bitcast.2), calls=%async_computation.2 | async-start | bytes 8388608
  1.1 18.4 %slice-start.2 = ((s8[16777216]{0:T(1024)(128)(4,1)}), s8[4194304]{0:T(1024)(128)(4,1)S(1)}, s32[]{:S(2)}) async-start(s8[16777216]{0:T(1024)(128)(4,1)} %bitcast.2), calls=%async_computation.3 | async-start | bytes 8388608
  1.1 18.4 %slice-start.3 = ((s8[16777216]{0:T(1024)(128)(4,1)}), s8[4194304]{0:T(1024)(128)(4,1)S(1)}, s32[]{:S(2)}) async-start(s8[16777216]{0:T(1024)(128)(4,1)} %bitcast.2), calls=%async_computation.4 | async-start | bytes 8388608
  1.1 6.8 %collective-permute-start.2 = (bf16[2,4224]{1,0:T(2,128)(2,1)S(1)}, bf16[2,4224]{1,0:T(2,128)(2,1)S(1)}, u32[]{:S(2)}, u32[]{:S(2)}) collective-permute-start(bf16[2,4224]{1,0:T(2,128)(2,1)S(1)} %row_payload.1.refs_0_), channel_id=1, source_target_pairs={{0,6},{1,7},{2,4},{3,5},{4,2},{5,3},{6,0},{7,1},{8,14},{9,15},{10,... | collective-permute-start | bytes 50696 | tf_op jit(solution)/shard_map/ppermute | solution.py:206
  6.2 4.6 %collective-permute-start.1 = (bf16[2,4224]{1,0:T(2,128)(2,1)S(1)}, bf16[2,4224]{1,0:T(2,128)(2,1)S(1)}, u32[]{:S(2)}, u32[]{:S(2)}) collective-permute-start(bf16[2,4224]{1,0:T(2,128)(2,1)S(1)} %row_payload.1.refs_0_), channel_id=1, source_target_pairs={{0,4},{1,5},{2,6},{3,7},{4,0},{5,1},{6,2},{7,3},{8,12},{9,13},{10,... | collective-permute-start | bytes 50696 | tf_op jit(solution)/shard_map/ppermute | solution.py:206
  6.2 4.6 %collective-permute-start = (bf16[2,4224]{1,0:T(2,128)(2,1)S(1)}, bf16[2,4224]{1,0:T(2,128)(2,1)S(1)}, u32[]{:S(2)}, u32[]{:S(2)}) collective-permute-start(bf16[2,4224]{1,0:T(2,128)(2,1)S(1)} %row_payload.1.refs_0_), channel_id=1, source_target_pairs={{0,2},{1,3},{2,0},{3,1},{4,6},{5,7},{6,4},{7,5},{8,10},{9,11},{10,... | collective-permute-start | bytes 50696 | tf_op jit(solution)/shard_map/ppermute | solution.py:206
  10.9 5.9 %collective-permute-start.5 = (bf16[4,2,4224]{2,1,0:T(2,128)(2,1)S(1)}, bf16[4,2,4224]{2,1,0:T(2,128)(2,1)S(1)}, u32[]{:S(2)}, u32[]{:S(2)}) collective-permute-start(bf16[4,2,4224]{2,1,0:T(2,128)(2,1)S(1)} %stacked.1.refs_0_), channel_id=1, source_target_pairs={{0,24},{8,16},{16,8},{24,0},{1,25},{9,17},{17,9},{25,1},{2,26},{10... | collective-permute-start | bytes 202760 | tf_op jit(solution)/shard_map/ppermute | solution.py:206
  13.4 4.3 %collective-permute-start.4 = (bf16[4,2,4224]{2,1,0:T(2,128)(2,1)S(1)}, bf16[4,2,4224]{2,1,0:T(2,128)(2,1)S(1)}, u32[]{:S(2)}, u32[]{:S(2)}) collective-permute-start(bf16[4,2,4224]{2,1,0:T(2,128)(2,1)S(1)} %stacked.1.refs_0_), channel_id=1, source_target_pairs={{0,16},{8,24},{16,0},{24,8},{1,17},{9,25},{17,1},{25,9},{2,18},{10... | collective-permute-start | bytes 202760 | tf_op jit(solution)/shard_map/ppermute | solution.py:206
  13.9 4.3 %collective-permute-start.3 = (bf16[4,2,4224]{2,1,0:T(2,128)(2,1)S(1)}, bf16[4,2,4224]{2,1,0:T(2,128)(2,1)S(1)}, u32[]{:S(2)}, u32[]{:S(2)}) collective-permute-start(bf16[4,2,4224]{2,1,0:T(2,128)(2,1)S(1)} %stacked.1.refs_0_), channel_id=1, source_target_pairs={{0,8},{8,0},{16,24},{24,16},{1,9},{9,1},{17,25},{25,17},{2,10},{10... | collective-permute-start | bytes 202760 | tf_op jit(solution)/shard_map/ppermute | solution.py:206
  14.4 3.8 %collective-permute-start.6 = (bf16[4,2,4224]{2,1,0:T(2,128)(2,1)S(1)}, bf16[4,2,4224]{2,1,0:T(2,128)(2,1)S(1)}, u32[]{:S(2)}, u32[]{:S(2)}) collective-permute-start(bf16[4,2,4224]{2,1,0:T(2,128)(2,1)S(1)} %stacked.1.refs_0_), channel_id=1, source_target_pairs={{0,1},{1,0},{2,3},{3,2},{4,5},{5,4},{6,7},{7,6},{8,9},{9,8},{10,11... | collective-permute-start | bytes 202760 | tf_op jit(solution)/shard_map/ppermute | solution.py:206
  16.7 1.5 %collective-permute-start.9 = (bf16[4,2,4224]{2,1,0:T(2,128)(2,1)S(1)}, bf16[4,2,4224]{2,1,0:T(2,128)(2,1)S(1)}, u32[]{:S(2)}, u32[]{:S(2)}) collective-permute-start(bf16[4,2,4224]{2,1,0:T(2,128)(2,1)S(1)} %collective-permute-done.5.refs_3_), channel_id=1, source_target_pairs={{0,1},{1,0},{2,3},{3,2},{4,5},{5,4},{6,7},{7,6},{8,9},{9,8},{10,11... | collective-permute-start | bytes 202760 | tf_op jit(solution)/shard_map/ppermute | solution.py:206
  17.7 1.3 %collective-permute-start.8 = (bf16[4,2,4224]{2,1,0:T(2,128)(2,1)S(1)}, bf16[4,2,4224]{2,1,0:T(2,128)(2,1)S(1)}, u32[]{:S(2)}, u32[]{:S(2)}) collective-permute-start(bf16[4,2,4224]{2,1,0:T(2,128)(2,1)S(1)} %collective-permute-done.4.refs_2_), channel_id=1, source_target_pairs={{0,1},{1,0},{2,3},{3,2},{4,5},{5,4},{6,7},{7,6},{8,9},{9,8},{10,11... | collective-permute-start | bytes 202760 | tf_op jit(solution)/shard_map/ppermute | solution.py:206
  18.2 1.3 %collective-permute-start.7 = (bf16[4,2,4224]{2,1,0:T(2,128)(2,1)S(1)}, bf16[4,2,4224]{2,1,0:T(2,128)(2,1)S(1)}, u32[]{:S(2)}, u32[]{:S(2)}) collective-permute-start(bf16[4,2,4224]{2,1,0:T(2,128)(2,1)S(1)} %collective-permute-done.3.refs_1_), channel_id=1, source_target_pairs={{0,1},{1,0},{2,3},{3,2},{4,5},{5,4},{6,7},{7,6},{8,9},{9,8},{10,11... | collective-permute-start | bytes 202760 | tf_op jit(solution)/shard_map/ppermute | solution.py:206
  24.7 1.6 %collective-permute-start.10 = (bf16[16,2,4096]{2,1,0:T(2,128)(2,1)S(1)}, bf16[16,2,4096]{2,1,0:T(2,128)(2,1)S(1)}, u32[]{:S(2)}, u32[]{:S(2)}) collective-permute-start(bf16[16,2,4096]{2,1,0:T(2,128)(2,1)S(1)} %get-tuple-element.8), channel_id=1, source_target_pairs={{0,1},{1,0},{2,3},{3,2},{4,5},{5,4},{6,7},{7,6},{8,9},{9,8},{10,11... | collective-permute-start | bytes 786440 | tf_op jit(solution)/shard_map/ppermute | solution.py:206

commit v5 on v4

--- a/solution.py
+++ b/solution.py
@@ -101,10 +101,10 @@
     block_rows = blocks[0].shape[0] * blocks[0].shape[1]
     total = blocks[0].shape[2]
     row_count = block_rows * len(blocks)
-    half = row_count // 2
+    half = width // 2
     piece_count = len(gate_up_pieces)
-    tile = math.gcd(math.gcd(hidden_dev, width), MLP_TILE)
-    out_block = (half // blocks[0].shape[1], blocks[0].shape[1], width)
+    tile = math.gcd(math.gcd(hidden_dev, half), MLP_TILE)
+    out_block = (row_count // blocks[0].shape[1], blocks[0].shape[1], half)
 
     def projected(rows_ref, piece_refs, column):
         sum_so_far, first = None, 0
@@ -144,16 +144,18 @@
             hidden_ref[:, pl.ds(column, tile)] = (jax.nn.silu(gate) * up).astype(jnp.bfloat16)
 
         fetch.wait()
-        for column in range(0, width, tile):
-            columns = slice(column, column + tile)
-            part = jnp.dot(
-                hidden_ref[...], down_ref[:, columns], preferred_element_type=jnp.float32
-            )
-            weighted = part.astype(jnp.bfloat16).astype(jnp.float32) * row_weight
-            own_out[:, :, columns] = weighted[:half].reshape(out_block[:2] + (tile,))
-            other_out[:, :, columns] = (
-                weighted[half:].reshape(out_block[:2] + (tile,)).astype(jnp.bfloat16)
-            )
+        core = lax.rem(lax.axis_index("fsdp"), 2)
+        for out, first in ((own_out, core * half), (other_out, (1 - core) * half)):
+            for column in range(0, half, tile):
+                part = jnp.dot(
+                    hidden_ref[...],
+                    down_ref[:, pl.ds(pl.multiple_of(first + column, tile), tile)],
+                    preferred_element_type=jnp.float32,
+                )
+                weighted = part.astype(jnp.bfloat16).astype(jnp.float32) * row_weight
+                out[:, :, column : column + tile] = weighted.reshape(
+                    out_block[:2] + (tile,)
+                ).astype(out.dtype)
 
     vmem = pl.BlockSpec(memory_space=pltpu.VMEM)
     return pl.pallas_call(
@@ -181,14 +183,17 @@
 
 
 def chip_sum(own_part, partner_part):
-    pair_count = own_part.shape[0]
+    pair_count = own_part.shape[0] // 2
 
     def kernel(own_ref, partner_ref, sum_ref):
-        my_chip = device_index() // 2
+        me = device_index()
+        core = lax.rem(me, 2)
         for chip in range(pair_count):
-            slot = jnp.bitwise_xor(my_chip, chip)
-            total = own_ref[slot] + partner_ref[slot].astype(jnp.float32)
-            sum_ref[chip] = total.astype(jnp.bfloat16)
+            same = jnp.bitwise_xor(me // 2, chip)
+            flip = pair_count + same
+            for mine, theirs, place in ((same, flip, core), (flip, same, 1 - core)):
+                total = own_ref[mine] + partner_ref[theirs].astype(jnp.float32)
+                sum_ref[2 * chip + place] = total.astype(jnp.bfloat16)
 
     vmem = pl.BlockSpec(memory_space=pltpu.VMEM)
     return pl.pallas_call(
@@ -201,16 +206,35 @@
     )(own_part, partner_part)
 
 
+def row_sum(returned):
+    device_count, rows_dev, half = returned.shape
+
+    def kernel(returned_ref, out_ref):
+        for core in range(2):
+            total = returned_ref[core].astype(jnp.float32)
+            for device in range(core + 2, device_count, 2):
+                total += returned_ref[device].astype(jnp.float32)
+            out_ref[:, core * half : (core + 1) * half] = total.astype(jnp.bfloat16)
+
+    vmem = pl.BlockSpec(memory_space=pltpu.VMEM)
+    return pl.pallas_call(
+        kernel,
+        out_shape=jax.ShapeDtypeStruct((rows_dev, 2 * half), jnp.bfloat16),
+        in_specs=[vmem],
+        out_specs=vmem,
+        compiler_params=pltpu.CompilerParams(vmem_limit_bytes=SMALL_VMEM),
+        name="row_sum",
+    )(returned)
+
+
 def exchanged(value, axis, flip):
     size = lax.axis_size(axis)
     return lax.ppermute(value, axis, [(d, d ^ flip) for d in range(size)])
 
 
 def every_row(tokens, norm_gain, routes, gate_probs, w_gate_up, w_down):
-    device_count = lax.axis_size(AXES)
     shard_count = lax.axis_size("fsdp")
     group_count = lax.axis_size("grp")
-    same_core = [[d for d in range(device_count) if d % 2 == k] for k in range(2)]
 
     payload = row_payload(tokens, norm_gain, routes, gate_probs)
     column = [payload] + [exchanged(payload, "fsdp", k) for k in range(2, shard_count, 2)]
@@ -221,8 +245,7 @@
     own_part, other_part = weighted_parts(own, other, [w_gate_up[0]], w_down, routes.shape[1])
     from_partner = exchanged(other_part, "fsdp", 1)
     summed = chip_sum(own_part, from_partner)
-    returned = lax.all_to_all(summed, AXES, 0, 0, axis_index_groups=same_core, tiled=True)
-    return jnp.sum(returned.astype(jnp.float32), axis=0).astype(jnp.bfloat16)
+    return row_sum(lax.all_to_all(summed, AXES, 0, 0, tiled=True))
 
 
 def routed_rows(tokens, norm_gain, routes, gate_probs, w_gate_up, w_down):

time: 42.5 us -> 40.9 us (0.962)
  blocking collectives: 15 us -> 13.5 us
  other arithmetic: 0.83 us -> 0.01 us
  Pallas kernels: 6.52 us -> 7.22 us
    all_to_all x1, blocking collectives: 15 us -> 13.5 us  [every_row(): return row_sum(lax.all_to_all(summed, AXES, 0, 0, tiled=True))]
    reduce_sum x1 -> x0, other arithmetic: 0.83 us -> none  [every_row(): return jnp.sum(returned.astype(jnp.float32), axis=0).astype(jnp.bfloat16)]
    pallas_call x0 -> x1, Pallas kernels: none -> 0.66 us  [row_sum(): pl.pallas_call(kernel, out_shape=jax.ShapeDtypeStruct((rows_dev, 2 * half...]
where the time goes in v5:
time: 40.9 us; the launch traced here: 40.7 us
  blocking collectives  13.5 us (33%)
  waiting for transfers between devices  10.4 us (25%)
  starting transfers between devices  9.55 us (23%)
  Pallas kernels  7.22 us (18%)
    all_to_all x1, blocking collectives, every_row(): return row_sum(lax.all_to_all(summed, AXES, 0, 0, tiled=True))  13.5 us
    ppermute x11, waiting for transfers between devices, exchanged(): return lax.ppermute(value, axis, [(d, d ^ flip) for d in range(size)])  10.4 us
    ppermute x11, starting transfers between devices, exchanged(): return lax.ppermute(value, axis, [(d, d ^ flip) for d in range(size)])  9.55 us
    pallas_call x1, Pallas kernels, weighted_parts(): pl.pallas_call(kernel, out_shape=[jax.ShapeDtypeStruct(out_block, jnp.flo...  5.26 us
    pallas_call x1, Pallas kernels, row_payload(): pl.pallas_call(kernel, out_shape=jax.ShapeDtypeStruct((rows_dev, total),...  1.06 us
  transfers between devices with their start and end apart: 11, of which 8 were waited for; matrix products, arithmetic and copies ran while one was open for 0% of the time, Pallas kernels for 0%

profile of v5, /device:TPU:0, one launch (start us, length us, event | category | flops | bytes accessed | tf_op | source)
XLA Modules:
  0.0 40.7 jit_solution(158736134442617734)
XLA Ops:
  0.0 1.1 %row_payload.1.refs_0_ = bf16[2,4224]{1,0:T(2,128)(2,1)S(1)} custom-call(bf16[2,4096]{1,0:T(2,128)(2,1)} %refs_0_.1, f32[1,4096]{1,0:T(1,128)} %bitcast.5, s32[2,8]{1,0:T(2,128)} %refs_2_.1, bf16[2,8]{1,0:T(2,128)(2,1)} %refs_3_.1), custom_call_target="tpu_custom_call" | custom-call | tf_op jit(solution)/shard_map/row_payload/pallas_call | solution.py:69
  1.1 0.0 slice-start.1
  1.1 0.0 slice-start.2
  1.1 5.1 %collective-permute-start.2 = (bf16[2,4224]{1,0:T(2,128)(2,1)S(1)}, bf16[2,4224]{1,0:T(2,128)(2,1)S(1)}, u32[]{:S(2)}, u32[]{:S(2)}) collective-permute-start(bf16[2,4224]{1,0:T(2,128)(2,1)S(1)} %row_payload.1.refs_0_), channel_id=1, source_target_pairs={{0,6},{1,7},{2,4},{3,5},{4,2},{5,3},{6,0},{7,1},{8,14},{9,15},{10,... | collective-permute-start | bytes 50696 | tf_op jit(solution)/shard_map/ppermute | solution.py:232
  6.2 0.6 %collective-permute-start = (bf16[2,4224]{1,0:T(2,128)(2,1)S(1)}, bf16[2,4224]{1,0:T(2,128)(2,1)S(1)}, u32[]{:S(2)}, u32[]{:S(2)}) collective-permute-start(bf16[2,4224]{1,0:T(2,128)(2,1)S(1)} %row_payload.1.refs_0_), channel_id=1, source_target_pairs={{0,2},{1,3},{2,0},{3,1},{4,6},{5,7},{6,4},{7,5},{8,10},{9,11},{10,... | collective-permute-start | bytes 50696 | tf_op jit(solution)/shard_map/ppermute | solution.py:232
  6.9 1.1 %collective-permute-done.2.refs_3_ = bf16[2,4224]{1,0:T(2,128)(2,1)S(1)} collective-permute-done((bf16[2,4224]{1,0:T(2,128)(2,1)S(1)}, bf16[2,4224]{1,0:T(2,128)(2,1)S(1)}, u32[]{:S(2)}, u32[]{:S(2)}) %collective-permute-start.2) | collective-permute-done | bytes 16928 | tf_op jit(solution)/shard_map/ppermute | solution.py:232
  7.9 2.9 %collective-permute-done.1.refs_2_ = bf16[2,4224]{1,0:T(2,128)(2,1)S(1)} collective-permute-done((bf16[2,4224]{1,0:T(2,128)(2,1)S(1)}, bf16[2,4224]{1,0:T(2,128)(2,1)S(1)}, u32[]{:S(2)}, u32[]{:S(2)}) %collective-permute-start.1) | collective-permute-done | bytes 16928 | tf_op jit(solution)/shard_map/ppermute | solution.py:232
  10.9 0.0 collective-permute-done.refs_1_
  10.9 2.5 %collective-permute-start.5 = (bf16[4,2,4224]{2,1,0:T(2,128)(2,1)S(1)}, bf16[4,2,4224]{2,1,0:T(2,128)(2,1)S(1)}, u32[]{:S(2)}, u32[]{:S(2)}) collective-permute-start(bf16[4,2,4224]{2,1,0:T(2,128)(2,1)S(1)} %stacked.1.refs_0_), channel_id=1, source_target_pairs={{0,24},{8,16},{16,8},{24,0},{1,25},{9,17},{17,9},{25,1},{2,26},{10... | collective-permute-start | bytes 202760 | tf_op jit(solution)/shard_map/ppermute | solution.py:232
  13.4 0.5 %collective-permute-start.4 = (bf16[4,2,4224]{2,1,0:T(2,128)(2,1)S(1)}, bf16[4,2,4224]{2,1,0:T(2,128)(2,1)S(1)}, u32[]{:S(2)}, u32[]{:S(2)}) collective-permute-start(bf16[4,2,4224]{2,1,0:T(2,128)(2,1)S(1)} %stacked.1.refs_0_), channel_id=1, source_target_pairs={{0,16},{8,24},{16,0},{24,8},{1,17},{9,25},{17,1},{25,9},{2,18},{10... | collective-permute-start | bytes 202760 | tf_op jit(solution)/shard_map/ppermute | solution.py:232
  13.9 0.5 %collective-permute-start.3 = (bf16[4,2,4224]{2,1,0:T(2,128)(2,1)S(1)}, bf16[4,2,4224]{2,1,0:T(2,128)(2,1)S(1)}, u32[]{:S(2)}, u32[]{:S(2)}) collective-permute-start(bf16[4,2,4224]{2,1,0:T(2,128)(2,1)S(1)} %stacked.1.refs_0_), channel_id=1, source_target_pairs={{0,8},{8,0},{16,24},{24,16},{1,9},{9,1},{17,25},{25,17},{2,10},{10... | collective-permute-start | bytes 202760 | tf_op jit(solution)/shard_map/ppermute | solution.py:232
  14.4 0.0 collective-permute-start.6
  14.4 2.3 %collective-permute-done.5.refs_3_ = bf16[4,2,4224]{2,1,0:T(2,128)(2,1)S(1)} collective-permute-done((bf16[4,2,4224]{2,1,0:T(2,128)(2,1)S(1)}, bf16[4,2,4224]{2,1,0:T(2,128)(2,1)S(1)}, u32[]{:S(2)}, u32[]{:S(2)}) %collective-permute-start.5) | collective-permute-done | bytes 67616 | tf_op jit(solution)/shard_map/ppermute | solution.py:232
  16.7 0.9 %collective-permute-done.4.refs_2_ = bf16[4,2,4224]{2,1,0:T(2,128)(2,1)S(1)} collective-permute-done((bf16[4,2,4224]{2,1,0:T(2,128)(2,1)S(1)}, bf16[4,2,4224]{2,1,0:T(2,128)(2,1)S(1)}, u32[]{:S(2)}, u32[]{:S(2)}) %collective-permute-start.4) | collective-permute-done | bytes 67616 | tf_op jit(solution)/shard_map/ppermute | solution.py:232
  17.7 0.5 %collective-permute-done.3.refs_1_ = bf16[4,2,4224]{2,1,0:T(2,128)(2,1)S(1)} collective-permute-done((bf16[4,2,4224]{2,1,0:T(2,128)(2,1)S(1)}, bf16[4,2,4224]{2,1,0:T(2,128)(2,1)S(1)}, u32[]{:S(2)}, u32[]{:S(2)}) %collective-permute-start.3) | collective-permute-done | bytes 67616 | tf_op jit(solution)/shard_map/ppermute | solution.py:232
  18.2 0.0 collective-permute-start.7
  18.2 0.7 %collective-permute-done.8.refs_6_ = bf16[4,2,4224]{2,1,0:T(2,128)(2,1)S(1)} collective-permute-done((bf16[4,2,4224]{2,1,0:T(2,128)(2,1)S(1)}, bf16[4,2,4224]{2,1,0:T(2,128)(2,1)S(1)}, u32[]{:S(2)}, u32[]{:S(2)}) %collective-permute-start.8) | collective-permute-done | bytes 67616 | tf_op jit(solution)/shard_map/ppermute | solution.py:232
  18.9 0.5 %collective-permute-done.7.refs_5_ = bf16[4,2,4224]{2,1,0:T(2,128)(2,1)S(1)} collective-permute-done((bf16[4,2,4224]{2,1,0:T(2,128)(2,1)S(1)}, bf16[4,2,4224]{2,1,0:T(2,128)(2,1)S(1)}, u32[]{:S(2)}, u32[]{:S(2)}) %collective-permute-start.7) | collective-permute-done | bytes 67616 | tf_op jit(solution)/shard_map/ppermute | solution.py:232
  19.5 5.3 %weighted_parts.1 = (f32[32,2,2048]{2,1,0:T(2,128)S(1)}, bf16[32,2,2048]{2,1,0:T(2,128)(2,1)S(1)}) custom-call(bf16[4,2,4224]{2,1,0:T(2,128)(2,1)S(1)} %stacked.1.refs_0_, bf16[4,2,4224]{2,1,0:T(2,128)(2,1)S(1)} %collective-permute-done.3.refs_1_, bf16[4,2,4224]{2,1,0:T(2,128)(2,1)S(1)} %collective-permute-done.4.refs_2_, ...), custom_call_target="tpu_custom_call" | custom-call | tf_op jit(solution)/shard_map/weighted_parts/pallas_call | solution.py:161
  24.7 0.2 collective-permute-start.10
  25.0 1.4 %collective-permute-done.10.partner_ref = bf16[32,2,2048]{2,1,0:T(2,128)(2,1)S(1)} collective-permute-done((bf16[32,2,2048]{2,1,0:T(2,128)(2,1)S(1)}, bf16[32,2,2048]{2,1,0:T(2,128)(2,1)S(1)}, u32[]{:S(2)}, u32[]{:S(2)}) %collective-permute-start.10) | collective-permute-done | bytes 262176 | tf_op jit(solution)/shard_map/ppermute | solution.py:232
  26.3 0.2 chip_sum.1
  26.6 13.5 %all_to_all.5.returned_ref = bf16[32,2,2048]{2,1,0:T(2,128)(2,1)S(1)} all-to-all(bf16[32,2,2048]{2,1,0:T(2,128)(2,1)S(1)} %chip_sum.1), channel_id=1, replica_groups=mesh['grp'=4,'fsdp'=8] {'grp','fsdp'}, dimensions={0} | all-to-all | bytes 524288 | tf_op jit(solution)/shard_map/all_to_all | solution.py:248
  40.0 0.7 %row_sum.1 = bf16[2,4096]{1,0:T(2,128)(2,1)} custom-call(bf16[32,2,2048]{2,1,0:T(2,128)(2,1)S(1)} %all_to_all.5.returned_ref), custom_call_target="tpu_custom_call" | custom-call | tf_op jit(solution)/shard_map/row_sum/pallas_call | solution.py:220
  (13 shorter events, 0.0 us)
Async XLA Ops:
  0.0 19.4 %slice-start = ((s8[16777216]{0:T(1024)(128)(4,1)}), s8[4194304]{0:T(1024)(128)(4,1)S(1)}, s32[]{:S(2)}) async-start(s8[16777216]{0:T(1024)(128)(4,1)} %bitcast.2), calls=%async_computation.1 | async-start | bytes 8388608
  1.1 18.4 %slice-start.1 = ((s8[16777216]{0:T(1024)(128)(4,1)}), s8[4194304]{0:T(1024)(128)(4,1)S(1)}, s32[]{:S(2)}) async-start(s8[16777216]{0:T(1024)(128)(4,1)} %bitcast.2), calls=%async_computation.2 | async-start | bytes 8388608
  1.1 18.4 %slice-start.2 = ((s8[16777216]{0:T(1024)(128)(4,1)}), s8[4194304]{0:T(1024)(128)(4,1)S(1)}, s32[]{:S(2)}) async-start(s8[16777216]{0:T(1024)(128)(4,1)} %bitcast.2), calls=%async_computation.3 | async-start | bytes 8388608
  1.1 18.4 %slice-start.3 = ((s8[16777216]{0:T(1024)(128)(4,1)}), s8[4194304]{0:T(1024)(128)(4,1)S(1)}, s32[]{:S(2)}) async-start(s8[16777216]{0:T(1024)(128)(4,1)} %bitcast.2), calls=%async_computation.4 | async-start | bytes 8388608
  1.1 6.8 %collective-permute-start.2 = (bf16[2,4224]{1,0:T(2,128)(2,1)S(1)}, bf16[2,4224]{1,0:T(2,128)(2,1)S(1)}, u32[]{:S(2)}, u32[]{:S(2)}) collective-permute-start(bf16[2,4224]{1,0:T(2,128)(2,1)S(1)} %row_payload.1.refs_0_), channel_id=1, source_target_pairs={{0,6},{1,7},{2,4},{3,5},{4,2},{5,3},{6,0},{7,1},{8,14},{9,15},{10,... | collective-permute-start | bytes 50696 | tf_op jit(solution)/shard_map/ppermute | solution.py:232
  6.2 4.6 %collective-permute-start.1 = (bf16[2,4224]{1,0:T(2,128)(2,1)S(1)}, bf16[2,4224]{1,0:T(2,128)(2,1)S(1)}, u32[]{:S(2)}, u32[]{:S(2)}) collective-permute-start(bf16[2,4224]{1,0:T(2,128)(2,1)S(1)} %row_payload.1.refs_0_), channel_id=1, source_target_pairs={{0,4},{1,5},{2,6},{3,7},{4,0},{5,1},{6,2},{7,3},{8,12},{9,13},{10,... | collective-permute-start | bytes 50696 | tf_op jit(solution)/shard_map/ppermute | solution.py:232
  6.2 4.6 %collective-permute-start = (bf16[2,4224]{1,0:T(2,128)(2,1)S(1)}, bf16[2,4224]{1,0:T(2,128)(2,1)S(1)}, u32[]{:S(2)}, u32[]{:S(2)}) collective-permute-start(bf16[2,4224]{1,0:T(2,128)(2,1)S(1)} %row_payload.1.refs_0_), channel_id=1, source_target_pairs={{0,2},{1,3},{2,0},{3,1},{4,6},{5,7},{6,4},{7,5},{8,10},{9,11},{10,... | collective-permute-start | bytes 50696 | tf_op jit(solution)/shard_map/ppermute | solution.py:232
  10.9 5.9 %collective-permute-start.5 = (bf16[4,2,4224]{2,1,0:T(2,128)(2,1)S(1)}, bf16[4,2,4224]{2,1,0:T(2,128)(2,1)S(1)}, u32[]{:S(2)}, u32[]{:S(2)}) collective-permute-start(bf16[4,2,4224]{2,1,0:T(2,128)(2,1)S(1)} %stacked.1.refs_0_), channel_id=1, source_target_pairs={{0,24},{8,16},{16,8},{24,0},{1,25},{9,17},{17,9},{25,1},{2,26},{10... | collective-permute-start | bytes 202760 | tf_op jit(solution)/shard_map/ppermute | solution.py:232
  13.4 4.3 %collective-permute-start.4 = (bf16[4,2,4224]{2,1,0:T(2,128)(2,1)S(1)}, bf16[4,2,4224]{2,1,0:T(2,128)(2,1)S(1)}, u32[]{:S(2)}, u32[]{:S(2)}) collective-permute-start(bf16[4,2,4224]{2,1,0:T(2,128)(2,1)S(1)} %stacked.1.refs_0_), channel_id=1, source_target_pairs={{0,16},{8,24},{16,0},{24,8},{1,17},{9,25},{17,1},{25,9},{2,18},{10... | collective-permute-start | bytes 202760 | tf_op jit(solution)/shard_map/ppermute | solution.py:232
  13.9 4.3 %collective-permute-start.3 = (bf16[4,2,4224]{2,1,0:T(2,128)(2,1)S(1)}, bf16[4,2,4224]{2,1,0:T(2,128)(2,1)S(1)}, u32[]{:S(2)}, u32[]{:S(2)}) collective-permute-start(bf16[4,2,4224]{2,1,0:T(2,128)(2,1)S(1)} %stacked.1.refs_0_), channel_id=1, source_target_pairs={{0,8},{8,0},{16,24},{24,16},{1,9},{9,1},{17,25},{25,17},{2,10},{10... | collective-permute-start | bytes 202760 | tf_op jit(solution)/shard_map/ppermute | solution.py:232
  14.4 3.8 %collective-permute-start.6 = (bf16[4,2,4224]{2,1,0:T(2,128)(2,1)S(1)}, bf16[4,2,4224]{2,1,0:T(2,128)(2,1)S(1)}, u32[]{:S(2)}, u32[]{:S(2)}) collective-permute-start(bf16[4,2,4224]{2,1,0:T(2,128)(2,1)S(1)} %stacked.1.refs_0_), channel_id=1, source_target_pairs={{0,1},{1,0},{2,3},{3,2},{4,5},{5,4},{6,7},{7,6},{8,9},{9,8},{10,11... | collective-permute-start | bytes 202760 | tf_op jit(solution)/shard_map/ppermute | solution.py:232
  16.7 1.5 %collective-permute-start.9 = (bf16[4,2,4224]{2,1,0:T(2,128)(2,1)S(1)}, bf16[4,2,4224]{2,1,0:T(2,128)(2,1)S(1)}, u32[]{:S(2)}, u32[]{:S(2)}) collective-permute-start(bf16[4,2,4224]{2,1,0:T(2,128)(2,1)S(1)} %collective-permute-done.5.refs_3_), channel_id=1, source_target_pairs={{0,1},{1,0},{2,3},{3,2},{4,5},{5,4},{6,7},{7,6},{8,9},{9,8},{10,11... | collective-permute-start | bytes 202760 | tf_op jit(solution)/shard_map/ppermute | solution.py:232
  17.7 1.3 %collective-permute-start.8 = (bf16[4,2,4224]{2,1,0:T(2,128)(2,1)S(1)}, bf16[4,2,4224]{2,1,0:T(2,128)(2,1)S(1)}, u32[]{:S(2)}, u32[]{:S(2)}) collective-permute-start(bf16[4,2,4224]{2,1,0:T(2,128)(2,1)S(1)} %collective-permute-done.4.refs_2_), channel_id=1, source_target_pairs={{0,1},{1,0},{2,3},{3,2},{4,5},{5,4},{6,7},{7,6},{8,9},{9,8},{10,11... | collective-permute-start | bytes 202760 | tf_op jit(solution)/shard_map/ppermute | solution.py:232
  18.2 1.3 %collective-permute-start.7 = (bf16[4,2,4224]{2,1,0:T(2,128)(2,1)S(1)}, bf16[4,2,4224]{2,1,0:T(2,128)(2,1)S(1)}, u32[]{:S(2)}, u32[]{:S(2)}) collective-permute-start(bf16[4,2,4224]{2,1,0:T(2,128)(2,1)S(1)} %collective-permute-done.3.refs_1_), channel_id=1, source_target_pairs={{0,1},{1,0},{2,3},{3,2},{4,5},{5,4},{6,7},{7,6},{8,9},{9,8},{10,11... | collective-permute-start | bytes 202760 | tf_op jit(solution)/shard_map/ppermute | solution.py:232
  24.7 1.6 %collective-permute-start.10 = (bf16[32,2,2048]{2,1,0:T(2,128)(2,1)S(1)}, bf16[32,2,2048]{2,1,0:T(2,128)(2,1)S(1)}, u32[]{:S(2)}, u32[]{:S(2)}) collective-permute-start(bf16[32,2,2048]{2,1,0:T(2,128)(2,1)S(1)} %get-tuple-element.8), channel_id=1, source_target_pairs={{0,1},{1,0},{2,3},{3,2},{4,5},{5,4},{6,7},{7,6},{8,9},{9,8},{10,11... | collective-permute-start | bytes 786440 | tf_op jit(solution)/shard_map/ppermute | solution.py:232

commit v6 on v5

--- a/solution.py
+++ b/solution.py
@@ -122,9 +122,18 @@
         my_expert = device_index() // (FF // hidden_dev)
         block_refs, refs = refs[: len(blocks)], refs[len(blocks) :]
         piece_refs, refs = refs[:piece_count], refs[piece_count:]
-        down_hbm, own_out, other_out, rows_ref, hidden_ref, down_ref, sem = refs
-        fetch = pltpu.make_async_copy(down_hbm.at[0], down_ref, sem)
-        fetch.start()
+        down_hbm, other_out, hidden_ref, weight_out, down_own, rows_ref, down_ref, sems = refs
+        core = lax.rem(lax.axis_index("fsdp"), 2)
+        fetches = [
+            pltpu.make_async_copy(
+                down_hbm.at[0, :, pl.ds(pl.multiple_of(place * half, half), half)],
+                target,
+                sems.at[index],
+            )
+            for index, (place, target) in enumerate(((1 - core, down_ref), (core, down_own)))
+        ]
+        for fetch in fetches:
+            fetch.start()
         for index, source in enumerate(block_refs):
             rows_ref[index * block_rows : (index + 1) * block_rows, :] = source[...].reshape(
                 block_rows, total
@@ -143,35 +152,27 @@
             up = projected(rows_ref, piece_refs, pl.multiple_of(hidden_dev + column, tile))
             hidden_ref[:, pl.ds(column, tile)] = (jax.nn.silu(gate) * up).astype(jnp.bfloat16)
 
-        fetch.wait()
-        core = lax.rem(lax.axis_index("fsdp"), 2)
-        for out, first in ((own_out, core * half), (other_out, (1 - core) * half)):
-            for column in range(0, half, tile):
-                part = jnp.dot(
-                    hidden_ref[...],
-                    down_ref[:, pl.ds(pl.multiple_of(first + column, tile), tile)],
-                    preferred_element_type=jnp.float32,
-                )
-                weighted = part.astype(jnp.bfloat16).astype(jnp.float32) * row_weight
-                out[:, :, column : column + tile] = weighted.reshape(
-                    out_block[:2] + (tile,)
-                ).astype(out.dtype)
+        for fetch in fetches:
+            fetch.wait()
+        weight_out[...] = jnp.broadcast_to(row_weight, weight_out.shape)
+        weighted_columns(hidden_ref, down_ref, row_weight, other_out, tile)
 
     vmem = pl.BlockSpec(memory_space=pltpu.VMEM)
     return pl.pallas_call(
         kernel,
         out_shape=[
-            jax.ShapeDtypeStruct(out_block, jnp.float32),
             jax.ShapeDtypeStruct(out_block, jnp.bfloat16),
+            jax.ShapeDtypeStruct((row_count, hidden_dev), jnp.bfloat16),
+            jax.ShapeDtypeStruct((row_count, LANES), jnp.float32),
+            pltpu.VMEM((hidden_dev, half), w_down.dtype),
         ],
         in_specs=[vmem] * (len(blocks) + piece_count)
         + [pl.BlockSpec(memory_space=pltpu.HBM)],
-        out_specs=[vmem] * 2,
+        out_specs=[vmem] * 4,
         scratch_shapes=[
             pltpu.VMEM((row_count, total), jnp.bfloat16),
-            pltpu.VMEM((row_count, hidden_dev), jnp.bfloat16),
-            pltpu.VMEM(w_down.shape[1:], w_down.dtype),
-            pltpu.SemaphoreType.DMA,
+            pltpu.VMEM((hidden_dev, half), w_down.dtype),
+            pltpu.SemaphoreType.DMA((2,)),
         ],
         compiler_params=pltpu.CompilerParams(vmem_limit_bytes=MLP_VMEM),
         name="weighted_parts",
@@ -180,6 +181,34 @@
         *[pltpu.with_memory_space_constraint(piece, pltpu.VMEM) for piece in gate_up_pieces],
         pltpu.with_memory_space_constraint(w_down, pltpu.HBM),
     )
+
+
+def weighted_columns(hidden_ref, down_ref, row_weight, out, tile):
+    for column in range(0, down_ref.shape[1], tile):
+        columns = slice(column, column + tile)
+        part = jnp.dot(hidden_ref[...], down_ref[:, columns], preferred_element_type=jnp.float32)
+        weighted = part.astype(jnp.bfloat16).astype(jnp.float32) * row_weight
+        out[:, :, columns] = weighted.reshape(out.shape[:2] + (tile,)).astype(out.dtype)
+
+
+def own_columns(hidden, weight, down_own, out_block):
+    tile = math.gcd(out_block[2], MLP_TILE)
+
+    def kernel(hidden_ref, weight_ref, down_ref, out):
+        weighted_columns(hidden_ref, down_ref, weight_ref[:, :1], out, tile)
+
+    vmem = pl.BlockSpec(memory_space=pltpu.VMEM)
+    return pl.pallas_call(
+        kernel,
+        out_shape=jax.ShapeDtypeStruct(out_block, jnp.float32),
+        in_specs=[vmem] * 3,
+        out_specs=vmem,
+        compiler_params=pltpu.CompilerParams(vmem_limit_bytes=MLP_VMEM),
+        cost_estimate=pl.CostEstimate(
+            flops=2 * hidden.shape[0] * down_own.size, transcendentals=0, bytes_accessed=down_own.nbytes
+        ),
+        name="own_columns",
+    )(hidden, weight, pltpu.with_memory_space_constraint(down_own, pltpu.VMEM))
 
 
 def chip_sum(own_part, partner_part):
@@ -242,8 +271,9 @@
     plane = [exchanged(column, "grp", k) for k in range(1, group_count)]
     own = [column] + plane
     other = [exchanged(block, "fsdp", 1) for block in own]
-    own_part, other_part = weighted_parts(own, other, [w_gate_up[0]], w_down, routes.shape[1])
+    other_part, hidden, weight, down_own = weighted_parts(own, other, [w_gate_up[0]], w_down, routes.shape[1])
     from_partner = exchanged(other_part, "fsdp", 1)
+    own_part = own_columns(hidden, weight, down_own, other_part.shape)
     summed = chip_sum(own_part, from_partner)
     return row_sum(lax.all_to_all(summed, AXES, 0, 0, tiled=True))
 

time: 40.9 us -> 40.2 us (0.983)
  waiting for transfers between devices: 10.4 us -> 9.49 us
    ppermute x11, waiting for transfers between devices: 10.4 us -> 9.49 us  [exchanged(): return lax.ppermute(value, axis, [(d, d ^ flip) for d in range(size)])]
    pallas_call x1 -> x2, Pallas kernels: 5.26 us -> 5.44 us  [the longest x1 4.55 us: weighted_parts(): pl.pallas_call(kernel, out_shape=[jax.ShapeDtypeStruct(out_block, jnp.bfl...]
  transfers between devices with their start and end apart: 11 -> 11, of which waited for: 8 -> 8; matrix products, arithmetic and copies ran while one was open for 0% -> 0% of each run, Pallas kernels for 0% -> 2%
where the time goes in v6:
time: 40.2 us; the launch traced here: 40 us
  blocking collectives  13.5 us (34%)
  starting transfers between devices  9.54 us (24%)
  waiting for transfers between devices  9.49 us (24%)
  Pallas kernels  7.4 us (18%)
    all_to_all x1, blocking collectives, every_row(): return row_sum(lax.all_to_all(summed, AXES, 0, 0, tiled=True))  13.5 us
    ppermute x11, starting transfers between devices, exchanged(): return lax.ppermute(value, axis, [(d, d ^ flip) for d in range(size)])  9.54 us
    ppermute x11, waiting for transfers between devices, exchanged(): return lax.ppermute(value, axis, [(d, d ^ flip) for d in range(size)])  9.49 us
    pallas_call x1, Pallas kernels, weighted_parts(): pl.pallas_call(kernel, out_shape=[jax.ShapeDtypeStruct(out_block, jnp.bfl...  4.55 us
    pallas_call x1, Pallas kernels, row_payload(): pl.pallas_call(kernel, out_shape=jax.ShapeDtypeStruct((rows_dev, total),...  1.06 us
    pallas_call x1, Pallas kernels, own_columns(): pl.pallas_call(kernel, out_shape=jax.ShapeDtypeStruct(out_block, jnp.floa...  0.88 us
  transfers between devices with their start and end apart: 11, of which 8 were waited for; matrix products, arithmetic and copies ran while one was open for 0% of the time, Pallas kernels for 2%

profile of v6, /device:TPU:0, one launch (start us, length us, event | category | flops | bytes accessed | tf_op | source)
XLA Modules:
  0.0 40.0 jit_solution(12665255990470168022)
XLA Ops:
  0.0 1.1 %row_payload.1.refs_0_ = bf16[2,4224]{1,0:T(2,128)(2,1)S(1)} custom-call(bf16[2,4096]{1,0:T(2,128)(2,1)} %refs_0_.1, f32[1,4096]{1,0:T(1,128)} %bitcast.5, s32[2,8]{1,0:T(2,128)} %refs_2_.1, bf16[2,8]{1,0:T(2,128)(2,1)} %refs_3_.1), custom_call_target="tpu_custom_call" | custom-call | tf_op jit(solution)/shard_map/row_payload/pallas_call | solution.py:69
  1.1 0.0 slice-start.1
  1.1 0.0 slice-start.2
  1.1 5.1 %collective-permute-start.2 = (bf16[2,4224]{1,0:T(2,128)(2,1)S(1)}, bf16[2,4224]{1,0:T(2,128)(2,1)S(1)}, u32[]{:S(2)}, u32[]{:S(2)}) collective-permute-start(bf16[2,4224]{1,0:T(2,128)(2,1)S(1)} %row_payload.1.refs_0_), channel_id=1, source_target_pairs={{0,6},{1,7},{2,4},{3,5},{4,2},{5,3},{6,0},{7,1},{8,14},{9,15},{10,... | collective-permute-start | bytes 50696 | tf_op jit(solution)/shard_map/ppermute | solution.py:261
  6.2 0.6 %collective-permute-start = (bf16[2,4224]{1,0:T(2,128)(2,1)S(1)}, bf16[2,4224]{1,0:T(2,128)(2,1)S(1)}, u32[]{:S(2)}, u32[]{:S(2)}) collective-permute-start(bf16[2,4224]{1,0:T(2,128)(2,1)S(1)} %row_payload.1.refs_0_), channel_id=1, source_target_pairs={{0,2},{1,3},{2,0},{3,1},{4,6},{5,7},{6,4},{7,5},{8,10},{9,11},{10,... | collective-permute-start | bytes 50696 | tf_op jit(solution)/shard_map/ppermute | solution.py:261
  6.9 1.1 %collective-permute-done.2.refs_3_ = bf16[2,4224]{1,0:T(2,128)(2,1)S(1)} collective-permute-done((bf16[2,4224]{1,0:T(2,128)(2,1)S(1)}, bf16[2,4224]{1,0:T(2,128)(2,1)S(1)}, u32[]{:S(2)}, u32[]{:S(2)}) %collective-permute-start.2) | collective-permute-done | bytes 16928 | tf_op jit(solution)/shard_map/ppermute | solution.py:261
  7.9 2.9 %collective-permute-done.1.refs_2_ = bf16[2,4224]{1,0:T(2,128)(2,1)S(1)} collective-permute-done((bf16[2,4224]{1,0:T(2,128)(2,1)S(1)}, bf16[2,4224]{1,0:T(2,128)(2,1)S(1)}, u32[]{:S(2)}, u32[]{:S(2)}) %collective-permute-start.1) | collective-permute-done | bytes 16928 | tf_op jit(solution)/shard_map/ppermute | solution.py:261
  10.9 0.0 collective-permute-done.refs_1_
  10.9 2.5 %collective-permute-start.5 = (bf16[4,2,4224]{2,1,0:T(2,128)(2,1)S(1)}, bf16[4,2,4224]{2,1,0:T(2,128)(2,1)S(1)}, u32[]{:S(2)}, u32[]{:S(2)}) collective-permute-start(bf16[4,2,4224]{2,1,0:T(2,128)(2,1)S(1)} %stacked.1.refs_0_), channel_id=1, source_target_pairs={{0,24},{8,16},{16,8},{24,0},{1,25},{9,17},{17,9},{25,1},{2,26},{10... | collective-permute-start | bytes 202760 | tf_op jit(solution)/shard_map/ppermute | solution.py:261
  13.4 0.5 %collective-permute-start.4 = (bf16[4,2,4224]{2,1,0:T(2,128)(2,1)S(1)}, bf16[4,2,4224]{2,1,0:T(2,128)(2,1)S(1)}, u32[]{:S(2)}, u32[]{:S(2)}) collective-permute-start(bf16[4,2,4224]{2,1,0:T(2,128)(2,1)S(1)} %stacked.1.refs_0_), channel_id=1, source_target_pairs={{0,16},{8,24},{16,0},{24,8},{1,17},{9,25},{17,1},{25,9},{2,18},{10... | collective-permute-start | bytes 202760 | tf_op jit(solution)/shard_map/ppermute | solution.py:261
  13.9 0.5 %collective-permute-start.3 = (bf16[4,2,4224]{2,1,0:T(2,128)(2,1)S(1)}, bf16[4,2,4224]{2,1,0:T(2,128)(2,1)S(1)}, u32[]{:S(2)}, u32[]{:S(2)}) collective-permute-start(bf16[4,2,4224]{2,1,0:T(2,128)(2,1)S(1)} %stacked.1.refs_0_), channel_id=1, source_target_pairs={{0,8},{8,0},{16,24},{24,16},{1,9},{9,1},{17,25},{25,17},{2,10},{10... | collective-permute-start | bytes 202760 | tf_op jit(solution)/shard_map/ppermute | solution.py:261
  14.4 2.3 %collective-permute-done.5.refs_3_ = bf16[4,2,4224]{2,1,0:T(2,128)(2,1)S(1)} collective-permute-done((bf16[4,2,4224]{2,1,0:T(2,128)(2,1)S(1)}, bf16[4,2,4224]{2,1,0:T(2,128)(2,1)S(1)}, u32[]{:S(2)}, u32[]{:S(2)}) %collective-permute-start.5) | collective-permute-done | bytes 67616 | tf_op jit(solution)/shard_map/ppermute | solution.py:261
  16.7 0.9 %collective-permute-done.4.refs_2_ = bf16[4,2,4224]{2,1,0:T(2,128)(2,1)S(1)} collective-permute-done((bf16[4,2,4224]{2,1,0:T(2,128)(2,1)S(1)}, bf16[4,2,4224]{2,1,0:T(2,128)(2,1)S(1)}, u32[]{:S(2)}, u32[]{:S(2)}) %collective-permute-start.4) | collective-permute-done | bytes 67616 | tf_op jit(solution)/shard_map/ppermute | solution.py:261
  17.7 0.5 %collective-permute-done.3.refs_1_ = bf16[4,2,4224]{2,1,0:T(2,128)(2,1)S(1)} collective-permute-done((bf16[4,2,4224]{2,1,0:T(2,128)(2,1)S(1)}, bf16[4,2,4224]{2,1,0:T(2,128)(2,1)S(1)}, u32[]{:S(2)}, u32[]{:S(2)}) %collective-permute-start.3) | collective-permute-done | bytes 67616 | tf_op jit(solution)/shard_map/ppermute | solution.py:261
  18.2 0.0 collective-permute-start.7
  18.2 0.7 %collective-permute-done.8.refs_6_ = bf16[4,2,4224]{2,1,0:T(2,128)(2,1)S(1)} collective-permute-done((bf16[4,2,4224]{2,1,0:T(2,128)(2,1)S(1)}, bf16[4,2,4224]{2,1,0:T(2,128)(2,1)S(1)}, u32[]{:S(2)}, u32[]{:S(2)}) %collective-permute-start.8) | collective-permute-done | bytes 67616 | tf_op jit(solution)/shard_map/ppermute | solution.py:261
  18.9 0.5 %collective-permute-done.7.refs_5_ = bf16[4,2,4224]{2,1,0:T(2,128)(2,1)S(1)} collective-permute-done((bf16[4,2,4224]{2,1,0:T(2,128)(2,1)S(1)}, bf16[4,2,4224]{2,1,0:T(2,128)(2,1)S(1)}, u32[]{:S(2)}, u32[]{:S(2)}) %collective-permute-start.7) | collective-permute-done | bytes 67616 | tf_op jit(solution)/shard_map/ppermute | solution.py:261
  19.5 4.6 %weighted_parts.1 = (bf16[32,2,2048]{2,1,0:T(2,128)(2,1)S(1)}, bf16[64,1024]{1,0:T(8,128)(2,1)S(1)}, f32[64,128]{1,0:T(8,128)S(1)}, bf16[1024,2048]{1,0:T(8,128)(2,1)S(1)}) custom-call(bf16[4,2,4224]{2,1,0:T(2,128)(2,1)S(1)} %stacked.1.refs_0_, bf16[4,2,4224]{2,1,0:T(2,128)(2,1)S(1)} %collective-permute-done.3.refs_1_, ...), custom_call_target="tpu_custom_call" | custom-call | tf_op jit(solution)/shard_map/weighted_parts/pallas_call | solution.py:161
  24.0 0.2 collective-permute-start.10
  24.2 0.9 %own_columns.1.own_ref = f32[32,2,2048]{2,1,0:T(2,128)S(1)} custom-call(bf16[64,1024]{1,0:T(8,128)(2,1)S(1)} %get-tuple-element.9.hidden_ref, f32[64,128]{1,0:T(8,128)S(1)} %get-tuple-element.10.weight_ref, bf16[1024,2048]{1,0:T(8,128)(2,1)S(1)} %get-tuple-element.11.down_ref), custom_call_target="tpu_custom_call" | custom-call | flops 268435456 | bytes 4194304 | tf_op jit(solution)/shard_map/own_columns/pallas_call | solution.py:201
  25.1 0.5 %collective-permute-done.10.partner_ref = bf16[32,2,2048]{2,1,0:T(2,128)(2,1)S(1)} collective-permute-done((bf16[32,2,2048]{2,1,0:T(2,128)(2,1)S(1)}, bf16[32,2,2048]{2,1,0:T(2,128)(2,1)S(1)}, u32[]{:S(2)}, u32[]{:S(2)}) %collective-permute-start.10) | collective-permute-done | bytes 262176 | tf_op jit(solution)/shard_map/ppermute | solution.py:261
  25.6 0.2 chip_sum.1
  25.9 13.5 %all_to_all.5.returned_ref = bf16[32,2,2048]{2,1,0:T(2,128)(2,1)S(1)} all-to-all(bf16[32,2,2048]{2,1,0:T(2,128)(2,1)S(1)} %chip_sum.1), channel_id=1, replica_groups=mesh['grp'=4,'fsdp'=8] {'grp','fsdp'}, dimensions={0} | all-to-all | bytes 524288 | tf_op jit(solution)/shard_map/all_to_all | solution.py:278
  39.3 0.7 %row_sum.1 = bf16[2,4096]{1,0:T(2,128)(2,1)} custom-call(bf16[32,2,2048]{2,1,0:T(2,128)(2,1)S(1)} %all_to_all.5.returned_ref), custom_call_target="tpu_custom_call" | custom-call | tf_op jit(solution)/shard_map/row_sum/pallas_call | solution.py:249
  (14 shorter events, 0.0 us)
Async XLA Ops:
  0.0 19.4 %slice-start = ((s8[16777216]{0:T(1024)(128)(4,1)}), s8[4194304]{0:T(1024)(128)(4,1)S(1)}, s32[]{:S(2)}) async-start(s8[16777216]{0:T(1024)(128)(4,1)} %bitcast.2), calls=%async_computation.1 | async-start | bytes 8388608
  1.1 18.4 %slice-start.1 = ((s8[16777216]{0:T(1024)(128)(4,1)}), s8[4194304]{0:T(1024)(128)(4,1)S(1)}, s32[]{:S(2)}) async-start(s8[16777216]{0:T(1024)(128)(4,1)} %bitcast.2), calls=%async_computation.2 | async-start | bytes 8388608
  1.1 18.4 %slice-start.2 = ((s8[16777216]{0:T(1024)(128)(4,1)}), s8[4194304]{0:T(1024)(128)(4,1)S(1)}, s32[]{:S(2)}) async-start(s8[16777216]{0:T(1024)(128)(4,1)} %bitcast.2), calls=%async_computation.3 | async-start | bytes 8388608
  1.1 18.4 %slice-start.3 = ((s8[16777216]{0:T(1024)(128)(4,1)}), s8[4194304]{0:T(1024)(128)(4,1)S(1)}, s32[]{:S(2)}) async-start(s8[16777216]{0:T(1024)(128)(4,1)} %bitcast.2), calls=%async_computation.4 | async-start | bytes 8388608
  1.1 6.8 %collective-permute-start.2 = (bf16[2,4224]{1,0:T(2,128)(2,1)S(1)}, bf16[2,4224]{1,0:T(2,128)(2,1)S(1)}, u32[]{:S(2)}, u32[]{:S(2)}) collective-permute-start(bf16[2,4224]{1,0:T(2,128)(2,1)S(1)} %row_payload.1.refs_0_), channel_id=1, source_target_pairs={{0,6},{1,7},{2,4},{3,5},{4,2},{5,3},{6,0},{7,1},{8,14},{9,15},{10,... | collective-permute-start | bytes 50696 | tf_op jit(solution)/shard_map/ppermute | solution.py:261
  6.2 4.6 %collective-permute-start.1 = (bf16[2,4224]{1,0:T(2,128)(2,1)S(1)}, bf16[2,4224]{1,0:T(2,128)(2,1)S(1)}, u32[]{:S(2)}, u32[]{:S(2)}) collective-permute-start(bf16[2,4224]{1,0:T(2,128)(2,1)S(1)} %row_payload.1.refs_0_), channel_id=1, source_target_pairs={{0,4},{1,5},{2,6},{3,7},{4,0},{5,1},{6,2},{7,3},{8,12},{9,13},{10,... | collective-permute-start | bytes 50696 | tf_op jit(solution)/shard_map/ppermute | solution.py:261
  6.2 4.6 %collective-permute-start = (bf16[2,4224]{1,0:T(2,128)(2,1)S(1)}, bf16[2,4224]{1,0:T(2,128)(2,1)S(1)}, u32[]{:S(2)}, u32[]{:S(2)}) collective-permute-start(bf16[2,4224]{1,0:T(2,128)(2,1)S(1)} %row_payload.1.refs_0_), channel_id=1, source_target_pairs={{0,2},{1,3},{2,0},{3,1},{4,6},{5,7},{6,4},{7,5},{8,10},{9,11},{10,... | collective-permute-start | bytes 50696 | tf_op jit(solution)/shard_map/ppermute | solution.py:261
  10.9 5.9 %collective-permute-start.5 = (bf16[4,2,4224]{2,1,0:T(2,128)(2,1)S(1)}, bf16[4,2,4224]{2,1,0:T(2,128)(2,1)S(1)}, u32[]{:S(2)}, u32[]{:S(2)}) collective-permute-start(bf16[4,2,4224]{2,1,0:T(2,128)(2,1)S(1)} %stacked.1.refs_0_), channel_id=1, source_target_pairs={{0,24},{8,16},{16,8},{24,0},{1,25},{9,17},{17,9},{25,1},{2,26},{10... | collective-permute-start | bytes 202760 | tf_op jit(solution)/shard_map/ppermute | solution.py:261
  13.4 4.3 %collective-permute-start.4 = (bf16[4,2,4224]{2,1,0:T(2,128)(2,1)S(1)}, bf16[4,2,4224]{2,1,0:T(2,128)(2,1)S(1)}, u32[]{:S(2)}, u32[]{:S(2)}) collective-permute-start(bf16[4,2,4224]{2,1,0:T(2,128)(2,1)S(1)} %stacked.1.refs_0_), channel_id=1, source_target_pairs={{0,16},{8,24},{16,0},{24,8},{1,17},{9,25},{17,1},{25,9},{2,18},{10... | collective-permute-start | bytes 202760 | tf_op jit(solution)/shard_map/ppermute | solution.py:261
  13.9 4.3 %collective-permute-start.3 = (bf16[4,2,4224]{2,1,0:T(2,128)(2,1)S(1)}, bf16[4,2,4224]{2,1,0:T(2,128)(2,1)S(1)}, u32[]{:S(2)}, u32[]{:S(2)}) collective-permute-start(bf16[4,2,4224]{2,1,0:T(2,128)(2,1)S(1)} %stacked.1.refs_0_), channel_id=1, source_target_pairs={{0,8},{8,0},{16,24},{24,16},{1,9},{9,1},{17,25},{25,17},{2,10},{10... | collective-permute-start | bytes 202760 | tf_op jit(solution)/shard_map/ppermute | solution.py:261
  14.4 3.8 %collective-permute-start.6 = (bf16[4,2,4224]{2,1,0:T(2,128)(2,1)S(1)}, bf16[4,2,4224]{2,1,0:T(2,128)(2,1)S(1)}, u32[]{:S(2)}, u32[]{:S(2)}) collective-permute-start(bf16[4,2,4224]{2,1,0:T(2,128)(2,1)S(1)} %stacked.1.refs_0_), channel_id=1, source_target_pairs={{0,1},{1,0},{2,3},{3,2},{4,5},{5,4},{6,7},{7,6},{8,9},{9,8},{10,11... | collective-permute-start | bytes 202760 | tf_op jit(solution)/shard_map/ppermute | solution.py:261
  16.7 1.5 %collective-permute-start.9 = (bf16[4,2,4224]{2,1,0:T(2,128)(2,1)S(1)}, bf16[4,2,4224]{2,1,0:T(2,128)(2,1)S(1)}, u32[]{:S(2)}, u32[]{:S(2)}) collective-permute-start(bf16[4,2,4224]{2,1,0:T(2,128)(2,1)S(1)} %collective-permute-done.5.refs_3_), channel_id=1, source_target_pairs={{0,1},{1,0},{2,3},{3,2},{4,5},{5,4},{6,7},{7,6},{8,9},{9,8},{10,11... | collective-permute-start | bytes 202760 | tf_op jit(solution)/shard_map/ppermute | solution.py:261
  17.7 1.3 %collective-permute-start.8 = (bf16[4,2,4224]{2,1,0:T(2,128)(2,1)S(1)}, bf16[4,2,4224]{2,1,0:T(2,128)(2,1)S(1)}, u32[]{:S(2)}, u32[]{:S(2)}) collective-permute-start(bf16[4,2,4224]{2,1,0:T(2,128)(2,1)S(1)} %collective-permute-done.4.refs_2_), channel_id=1, source_target_pairs={{0,1},{1,0},{2,3},{3,2},{4,5},{5,4},{6,7},{7,6},{8,9},{9,8},{10,11... | collective-permute-start | bytes 202760 | tf_op jit(solution)/shard_map/ppermute | solution.py:261
  18.2 1.3 %collective-permute-start.7 = (bf16[4,2,4224]{2,1,0:T(2,128)(2,1)S(1)}, bf16[4,2,4224]{2,1,0:T(2,128)(2,1)S(1)}, u32[]{:S(2)}, u32[]{:S(2)}) collective-permute-start(bf16[4,2,4224]{2,1,0:T(2,128)(2,1)S(1)} %collective-permute-done.3.refs_1_), channel_id=1, source_target_pairs={{0,1},{1,0},{2,3},{3,2},{4,5},{5,4},{6,7},{7,6},{8,9},{9,8},{10,11... | collective-permute-start | bytes 202760 | tf_op jit(solution)/shard_map/ppermute | solution.py:261
  24.0 1.6 %collective-permute-start.10 = (bf16[32,2,2048]{2,1,0:T(2,128)(2,1)S(1)}, bf16[32,2,2048]{2,1,0:T(2,128)(2,1)S(1)}, u32[]{:S(2)}, u32[]{:S(2)}) collective-permute-start(bf16[32,2,2048]{2,1,0:T(2,128)(2,1)S(1)} %get-tuple-element.12), channel_id=1, source_target_pairs={{0,1},{1,0},{2,3},{3,2},{4,5},{5,4},{6,7},{7,6},{8,9},{9,8},{10,11... | collective-permute-start | bytes 786440 | tf_op jit(solution)/shard_map/ppermute | solution.py:261

commit v7 on v6

--- a/solution.py
+++ b/solution.py
@@ -10,7 +10,7 @@
 FF = 1024
 LANES = 128
 SMALL_VMEM = 2 << 20
-MLP_VMEM = 24 << 20
+MLP_VMEM = 8 << 20
 MLP_TILE = 512
 PREFETCH_WINDOW = pl.CostEstimate(flops=64 << 30, transcendentals=0, bytes_accessed=256 << 20)
 AXES = ("grp", "fsdp")
@@ -96,7 +96,7 @@
 
 
 def weighted_parts(own, other, gate_up_pieces, w_down, top_count):
-    hidden_dev, width = w_down.shape[1:]
+    hidden_dev, width = w_down.shape
     blocks = list(own) + list(other)
     block_rows = blocks[0].shape[0] * blocks[0].shape[1]
     total = blocks[0].shape[2]
@@ -122,18 +122,8 @@
         my_expert = device_index() // (FF // hidden_dev)
         block_refs, refs = refs[: len(blocks)], refs[len(blocks) :]
         piece_refs, refs = refs[:piece_count], refs[piece_count:]
-        down_hbm, other_out, hidden_ref, weight_out, down_own, rows_ref, down_ref, sems = refs
+        down_ref, other_out, hidden_ref, weight_out, rows_ref = refs
         core = lax.rem(lax.axis_index("fsdp"), 2)
-        fetches = [
-            pltpu.make_async_copy(
-                down_hbm.at[0, :, pl.ds(pl.multiple_of(place * half, half), half)],
-                target,
-                sems.at[index],
-            )
-            for index, (place, target) in enumerate(((1 - core, down_ref), (core, down_own)))
-        ]
-        for fetch in fetches:
-            fetch.start()
         for index, source in enumerate(block_refs):
             rows_ref[index * block_rows : (index + 1) * block_rows, :] = source[...].reshape(
                 block_rows, total
@@ -145,17 +135,12 @@
         row_weight = jnp.sum(
             jnp.where(sent_routes == my_expert, combine, 0.0), axis=-1, keepdims=True
         )
-        @pl.loop(0, hidden_dev // tile)
-        def _(step):
-            column = pl.multiple_of(step * tile, tile)
+        for column in range(0, hidden_dev, tile):
             gate = projected(rows_ref, piece_refs, column)
-            up = projected(rows_ref, piece_refs, pl.multiple_of(hidden_dev + column, tile))
-            hidden_ref[:, pl.ds(column, tile)] = (jax.nn.silu(gate) * up).astype(jnp.bfloat16)
-
-        for fetch in fetches:
-            fetch.wait()
+            up = projected(rows_ref, piece_refs, hidden_dev + column)
+            hidden_ref[:, column : column + tile] = (jax.nn.silu(gate) * up).astype(jnp.bfloat16)
         weight_out[...] = jnp.broadcast_to(row_weight, weight_out.shape)
-        weighted_columns(hidden_ref, down_ref, row_weight, other_out, tile)
+        weighted_columns(hidden_ref, down_ref, (1 - core) * half, row_weight, other_out, tile)
 
     vmem = pl.BlockSpec(memory_space=pltpu.VMEM)
     return pl.pallas_call(
@@ -164,38 +149,36 @@
             jax.ShapeDtypeStruct(out_block, jnp.bfloat16),
             jax.ShapeDtypeStruct((row_count, hidden_dev), jnp.bfloat16),
             jax.ShapeDtypeStruct((row_count, LANES), jnp.float32),
-            pltpu.VMEM((hidden_dev, half), w_down.dtype),
         ],
-        in_specs=[vmem] * (len(blocks) + piece_count)
-        + [pl.BlockSpec(memory_space=pltpu.HBM)],
-        out_specs=[vmem] * 4,
+        in_specs=[vmem] * (len(blocks) + piece_count + 1),
+        out_specs=[vmem] * 3,
         scratch_shapes=[
             pltpu.VMEM((row_count, total), jnp.bfloat16),
-            pltpu.VMEM((hidden_dev, half), w_down.dtype),
-            pltpu.SemaphoreType.DMA((2,)),
         ],
         compiler_params=pltpu.CompilerParams(vmem_limit_bytes=MLP_VMEM),
         name="weighted_parts",
     )(
         *blocks,
         *[pltpu.with_memory_space_constraint(piece, pltpu.VMEM) for piece in gate_up_pieces],
-        pltpu.with_memory_space_constraint(w_down, pltpu.HBM),
-    )
-
-
-def weighted_columns(hidden_ref, down_ref, row_weight, out, tile):
-    for column in range(0, down_ref.shape[1], tile):
+        pltpu.with_memory_space_constraint(w_down, pltpu.VMEM),
+    )
+
+
+def weighted_columns(hidden_ref, down_ref, first, row_weight, out, tile):
+    for column in range(0, out.shape[2], tile):
         columns = slice(column, column + tile)
-        part = jnp.dot(hidden_ref[...], down_ref[:, columns], preferred_element_type=jnp.float32)
+        source = pl.ds(pl.multiple_of(first + column, tile), tile)
+        part = jnp.dot(hidden_ref[...], down_ref[:, source], preferred_element_type=jnp.float32)
         weighted = part.astype(jnp.bfloat16).astype(jnp.float32) * row_weight
         out[:, :, columns] = weighted.reshape(out.shape[:2] + (tile,)).astype(out.dtype)
 
 
-def own_columns(hidden, weight, down_own, out_block):
+def own_columns(hidden, weight, w_down, out_block):
     tile = math.gcd(out_block[2], MLP_TILE)
 
     def kernel(hidden_ref, weight_ref, down_ref, out):
-        weighted_columns(hidden_ref, down_ref, weight_ref[:, :1], out, tile)
+        first = lax.rem(lax.axis_index("fsdp"), 2) * out_block[2]
+        weighted_columns(hidden_ref, down_ref, first, weight_ref[:, :1], out, tile)
 
     vmem = pl.BlockSpec(memory_space=pltpu.VMEM)
     return pl.pallas_call(
@@ -205,10 +188,10 @@
         out_specs=vmem,
         compiler_params=pltpu.CompilerParams(vmem_limit_bytes=MLP_VMEM),
         cost_estimate=pl.CostEstimate(
-            flops=2 * hidden.shape[0] * down_own.size, transcendentals=0, bytes_accessed=down_own.nbytes
+            flops=hidden.shape[0] * w_down.size, transcendentals=0, bytes_accessed=w_down.nbytes // 2
         ),
         name="own_columns",
-    )(hidden, weight, pltpu.with_memory_space_constraint(down_own, pltpu.VMEM))
+    )(hidden, weight, pltpu.with_memory_space_constraint(w_down, pltpu.VMEM))
 
 
 def chip_sum(own_part, partner_part):
@@ -271,9 +254,9 @@
     plane = [exchanged(column, "grp", k) for k in range(1, group_count)]
     own = [column] + plane
     other = [exchanged(block, "fsdp", 1) for block in own]
-    other_part, hidden, weight, down_own = weighted_parts(own, other, [w_gate_up[0]], w_down, routes.shape[1])
+    other_part, hidden, weight = weighted_parts(own, other, [w_gate_up[0]], w_down[0], routes.shape[1])
     from_partner = exchanged(other_part, "fsdp", 1)
-    own_part = own_columns(hidden, weight, down_own, other_part.shape)
+    own_part = own_columns(hidden, weight, w_down[0], other_part.shape)
     summed = chip_sum(own_part, from_partner)
     return row_sum(lax.all_to_all(summed, AXES, 0, 0, tiled=True))
 

time: 40.2 us -> 39.6 us (0.985)
  Pallas kernels: 7.4 us -> 6.79 us
    pallas_call x1, Pallas kernels: 4.55 us -> 3.94 us  [weighted_parts(): pl.pallas_call(kernel, out_shape=[jax.ShapeDtypeStruct(out_block, jnp.bfl...]
where the time goes in v7:
time: 39.6 us; the launch traced here: 39.4 us
  blocking collectives  13.5 us (34%)
  starting transfers between devices  9.54 us (24%)
  waiting for transfers between devices  9.48 us (24%)
  Pallas kernels  6.79 us (17%)
    all_to_all x1, blocking collectives, every_row(): return row_sum(lax.all_to_all(summed, AXES, 0, 0, tiled=True))  13.5 us
    ppermute x11, starting transfers between devices, exchanged(): return lax.ppermute(value, axis, [(d, d ^ flip) for d in range(size)])  9.54 us
    ppermute x11, waiting for transfers between devices, exchanged(): return lax.ppermute(value, axis, [(d, d ^ flip) for d in range(size)])  9.48 us
    pallas_call x1, Pallas kernels, weighted_parts(): pl.pallas_call(kernel, out_shape=[jax.ShapeDtypeStruct(out_block, jnp.bfl...  3.94 us
    pallas_call x1, Pallas kernels, row_payload(): pl.pallas_call(kernel, out_shape=jax.ShapeDtypeStruct((rows_dev, total),...  1.06 us
    pallas_call x1, Pallas kernels, own_columns(): pl.pallas_call(kernel, out_shape=jax.ShapeDtypeStruct(out_block, jnp.floa...  0.88 us
  transfers between devices with their start and end apart: 11, of which 8 were waited for; matrix products, arithmetic and copies ran while one was open for 0% of the time, Pallas kernels for 2%

profile of v7, /device:TPU:0, one launch (start us, length us, event | category | flops | bytes accessed | tf_op | source)
XLA Modules:
  0.0 39.4 jit_solution(9151018768775482239)
XLA Ops:
  0.0 1.1 %row_payload.1.refs_0_ = bf16[2,4224]{1,0:T(2,128)(2,1)S(1)} custom-call(bf16[2,4096]{1,0:T(2,128)(2,1)} %refs_0_.1, f32[1,4096]{1,0:T(1,128)} %bitcast.10, s32[2,8]{1,0:T(2,128)} %refs_2_.1, bf16[2,8]{1,0:T(2,128)(2,1)} %refs_3_.1), custom_call_target="tpu_custom_call" | custom-call | tf_op jit(solution)/shard_map/row_payload/pallas_call | solution.py:69
  1.1 0.0 slice-start.1
  1.1 0.0 slice-start.3
  1.1 0.0 slice-start.5
  1.1 5.1 %collective-permute-start.2 = (bf16[2,4224]{1,0:T(2,128)(2,1)S(1)}, bf16[2,4224]{1,0:T(2,128)(2,1)S(1)}, u32[]{:S(2)}, u32[]{:S(2)}) collective-permute-start(bf16[2,4224]{1,0:T(2,128)(2,1)S(1)} %row_payload.1.refs_0_), channel_id=1, source_target_pairs={{0,6},{1,7},{2,4},{3,5},{4,2},{5,3},{6,0},{7,1},{8,14},{9,15},{10,... | collective-permute-start | bytes 50696 | tf_op jit(solution)/shard_map/ppermute | solution.py:244
  6.2 0.6 %collective-permute-start = (bf16[2,4224]{1,0:T(2,128)(2,1)S(1)}, bf16[2,4224]{1,0:T(2,128)(2,1)S(1)}, u32[]{:S(2)}, u32[]{:S(2)}) collective-permute-start(bf16[2,4224]{1,0:T(2,128)(2,1)S(1)} %row_payload.1.refs_0_), channel_id=1, source_target_pairs={{0,2},{1,3},{2,0},{3,1},{4,6},{5,7},{6,4},{7,5},{8,10},{9,11},{10,... | collective-permute-start | bytes 50696 | tf_op jit(solution)/shard_map/ppermute | solution.py:244
  6.9 1.1 %collective-permute-done.2.refs_3_ = bf16[2,4224]{1,0:T(2,128)(2,1)S(1)} collective-permute-done((bf16[2,4224]{1,0:T(2,128)(2,1)S(1)}, bf16[2,4224]{1,0:T(2,128)(2,1)S(1)}, u32[]{:S(2)}, u32[]{:S(2)}) %collective-permute-start.2) | collective-permute-done | bytes 16928 | tf_op jit(solution)/shard_map/ppermute | solution.py:244
  8.0 2.9 %collective-permute-done.1.refs_2_ = bf16[2,4224]{1,0:T(2,128)(2,1)S(1)} collective-permute-done((bf16[2,4224]{1,0:T(2,128)(2,1)S(1)}, bf16[2,4224]{1,0:T(2,128)(2,1)S(1)}, u32[]{:S(2)}, u32[]{:S(2)}) %collective-permute-start.1) | collective-permute-done | bytes 16928 | tf_op jit(solution)/shard_map/ppermute | solution.py:244
  10.9 2.5 %collective-permute-start.5 = (bf16[4,2,4224]{2,1,0:T(2,128)(2,1)S(1)}, bf16[4,2,4224]{2,1,0:T(2,128)(2,1)S(1)}, u32[]{:S(2)}, u32[]{:S(2)}) collective-permute-start(bf16[4,2,4224]{2,1,0:T(2,128)(2,1)S(1)} %stacked.1.refs_0_), channel_id=1, source_target_pairs={{0,24},{8,16},{16,8},{24,0},{1,25},{9,17},{17,9},{25,1},{2,26},{10... | collective-permute-start | bytes 202760 | tf_op jit(solution)/shard_map/ppermute | solution.py:244
  13.4 0.5 %collective-permute-start.4 = (bf16[4,2,4224]{2,1,0:T(2,128)(2,1)S(1)}, bf16[4,2,4224]{2,1,0:T(2,128)(2,1)S(1)}, u32[]{:S(2)}, u32[]{:S(2)}) collective-permute-start(bf16[4,2,4224]{2,1,0:T(2,128)(2,1)S(1)} %stacked.1.refs_0_), channel_id=1, source_target_pairs={{0,16},{8,24},{16,0},{24,8},{1,17},{9,25},{17,1},{25,9},{2,18},{10... | collective-permute-start | bytes 202760 | tf_op jit(solution)/shard_map/ppermute | solution.py:244
  13.9 0.5 %collective-permute-start.3 = (bf16[4,2,4224]{2,1,0:T(2,128)(2,1)S(1)}, bf16[4,2,4224]{2,1,0:T(2,128)(2,1)S(1)}, u32[]{:S(2)}, u32[]{:S(2)}) collective-permute-start(bf16[4,2,4224]{2,1,0:T(2,128)(2,1)S(1)} %stacked.1.refs_0_), channel_id=1, source_target_pairs={{0,8},{8,0},{16,24},{24,16},{1,9},{9,1},{17,25},{25,17},{2,10},{10... | collective-permute-start | bytes 202760 | tf_op jit(solution)/shard_map/ppermute | solution.py:244
  14.5 2.3 %collective-permute-done.5.refs_3_ = bf16[4,2,4224]{2,1,0:T(2,128)(2,1)S(1)} collective-permute-done((bf16[4,2,4224]{2,1,0:T(2,128)(2,1)S(1)}, bf16[4,2,4224]{2,1,0:T(2,128)(2,1)S(1)}, u32[]{:S(2)}, u32[]{:S(2)}) %collective-permute-start.5) | collective-permute-done | bytes 67616 | tf_op jit(solution)/shard_map/ppermute | solution.py:244
  16.8 0.9 %collective-permute-done.4.refs_2_ = bf16[4,2,4224]{2,1,0:T(2,128)(2,1)S(1)} collective-permute-done((bf16[4,2,4224]{2,1,0:T(2,128)(2,1)S(1)}, bf16[4,2,4224]{2,1,0:T(2,128)(2,1)S(1)}, u32[]{:S(2)}, u32[]{:S(2)}) %collective-permute-start.4) | collective-permute-done | bytes 67616 | tf_op jit(solution)/shard_map/ppermute | solution.py:244
  17.7 0.5 %collective-permute-done.3.refs_1_ = bf16[4,2,4224]{2,1,0:T(2,128)(2,1)S(1)} collective-permute-done((bf16[4,2,4224]{2,1,0:T(2,128)(2,1)S(1)}, bf16[4,2,4224]{2,1,0:T(2,128)(2,1)S(1)}, u32[]{:S(2)}, u32[]{:S(2)}) %collective-permute-start.3) | collective-permute-done | bytes 67616 | tf_op jit(solution)/shard_map/ppermute | solution.py:244
  18.2 0.0 collective-permute-start.7
  18.2 0.7 %collective-permute-done.8.refs_6_ = bf16[4,2,4224]{2,1,0:T(2,128)(2,1)S(1)} collective-permute-done((bf16[4,2,4224]{2,1,0:T(2,128)(2,1)S(1)}, bf16[4,2,4224]{2,1,0:T(2,128)(2,1)S(1)}, u32[]{:S(2)}, u32[]{:S(2)}) %collective-permute-start.8) | collective-permute-done | bytes 67616 | tf_op jit(solution)/shard_map/ppermute | solution.py:244
  19.0 0.5 %collective-permute-done.7.refs_5_ = bf16[4,2,4224]{2,1,0:T(2,128)(2,1)S(1)} collective-permute-done((bf16[4,2,4224]{2,1,0:T(2,128)(2,1)S(1)}, bf16[4,2,4224]{2,1,0:T(2,128)(2,1)S(1)}, u32[]{:S(2)}, u32[]{:S(2)}) %collective-permute-start.7) | collective-permute-done | bytes 67616 | tf_op jit(solution)/shard_map/ppermute | solution.py:244
  19.5 3.9 %weighted_parts.1 = (bf16[32,2,2048]{2,1,0:T(2,128)(2,1)S(1)}, bf16[64,1024]{1,0:T(8,128)(2,1)S(1)}, f32[64,128]{1,0:T(8,128)S(1)}) custom-call(bf16[4,2,4224]{2,1,0:T(2,128)(2,1)S(1)} %stacked.1.refs_0_, bf16[4,2,4224]{2,1,0:T(2,128)(2,1)S(1)} %collective-permute-done.3.refs_1_, bf16[4,2,4224]{2,1,0:T(2,128)(2,1)S(1)} %collective-permute-done.4.refs_2_, ...), custom_call_target="tpu_custom_call" | custom-call | tf_op jit(solution)/shard_map/weighted_parts/pallas_call | solution.py:146
  23.5 0.2 collective-permute-start.10
  23.7 0.9 %own_columns.1.own_ref = f32[32,2,2048]{2,1,0:T(2,128)S(1)} custom-call(bf16[64,1024]{1,0:T(8,128)(2,1)S(1)} %get-tuple-element.8.hidden_ref, f32[64,128]{1,0:T(8,128)S(1)} %get-tuple-element.9.weight_ref, bf16[1024,4096]{1,0:T(8,128)(2,1)S(1)} %bitcast.6), custom_call_target="tpu_custom_call" | custom-call | flops 268435456 | bytes 4194304 | tf_op jit(solution)/shard_map/own_columns/pallas_call | solution.py:184
  24.6 0.5 %collective-permute-done.10.partner_ref = bf16[32,2,2048]{2,1,0:T(2,128)(2,1)S(1)} collective-permute-done((bf16[32,2,2048]{2,1,0:T(2,128)(2,1)S(1)}, bf16[32,2,2048]{2,1,0:T(2,128)(2,1)S(1)}, u32[]{:S(2)}, u32[]{:S(2)}) %collective-permute-start.10) | collective-permute-done | bytes 262176 | tf_op jit(solution)/shard_map/ppermute | solution.py:244
  25.1 0.2 chip_sum.1
  25.3 13.5 %all_to_all.5.returned_ref = bf16[32,2,2048]{2,1,0:T(2,128)(2,1)S(1)} all-to-all(bf16[32,2,2048]{2,1,0:T(2,128)(2,1)S(1)} %chip_sum.1), channel_id=1, replica_groups=mesh['grp'=4,'fsdp'=8] {'grp','fsdp'}, dimensions={0} | all-to-all | bytes 524288 | tf_op jit(solution)/shard_map/all_to_all | solution.py:261
  38.8 0.7 %row_sum.1 = bf16[2,4096]{1,0:T(2,128)(2,1)} custom-call(bf16[32,2,2048]{2,1,0:T(2,128)(2,1)S(1)} %all_to_all.5.returned_ref), custom_call_target="tpu_custom_call" | custom-call | tf_op jit(solution)/shard_map/row_sum/pallas_call | solution.py:232
  (19 shorter events, 0.0 us)
Async XLA Ops:
  0.0 19.5 %slice-start = ((s8[8388608]{0:T(1024)(128)(4,1)}), s8[4194304]{0:T(1024)(128)(4,1)S(1)}, s32[]{:S(2)}) async-start(s8[8388608]{0:T(1024)(128)(4,1)} %bitcast.3), calls=%async_computation.1 | async-start | bytes 8388608
  0.0 19.5 %slice-start.2 = ((s8[16777216]{0:T(1024)(128)(4,1)}), s8[4194304]{0:T(1024)(128)(4,1)S(1)}, s32[]{:S(2)}) async-start(s8[16777216]{0:T(1024)(128)(4,1)} %bitcast.7), calls=%async_computation.3 | async-start | bytes 8388608
  1.1 18.4 %slice-start.1 = ((s8[8388608]{0:T(1024)(128)(4,1)}), s8[4194304]{0:T(1024)(128)(4,1)S(1)}, s32[]{:S(2)}) async-start(s8[8388608]{0:T(1024)(128)(4,1)} %bitcast.3), calls=%async_computation.2 | async-start | bytes 8388608
  1.1 18.4 %slice-start.3 = ((s8[16777216]{0:T(1024)(128)(4,1)}), s8[4194304]{0:T(1024)(128)(4,1)S(1)}, s32[]{:S(2)}) async-start(s8[16777216]{0:T(1024)(128)(4,1)} %bitcast.7), calls=%async_computation.4 | async-start | bytes 8388608
  1.1 18.4 %slice-start.4 = ((s8[16777216]{0:T(1024)(128)(4,1)}), s8[4194304]{0:T(1024)(128)(4,1)S(1)}, s32[]{:S(2)}) async-start(s8[16777216]{0:T(1024)(128)(4,1)} %bitcast.7), calls=%async_computation.5 | async-start | bytes 8388608
  1.1 18.4 %slice-start.5 = ((s8[16777216]{0:T(1024)(128)(4,1)}), s8[4194304]{0:T(1024)(128)(4,1)S(1)}, s32[]{:S(2)}) async-start(s8[16777216]{0:T(1024)(128)(4,1)} %bitcast.7), calls=%async_computation.6 | async-start | bytes 8388608
  1.1 6.8 %collective-permute-start.2 = (bf16[2,4224]{1,0:T(2,128)(2,1)S(1)}, bf16[2,4224]{1,0:T(2,128)(2,1)S(1)}, u32[]{:S(2)}, u32[]{:S(2)}) collective-permute-start(bf16[2,4224]{1,0:T(2,128)(2,1)S(1)} %row_payload.1.refs_0_), channel_id=1, source_target_pairs={{0,6},{1,7},{2,4},{3,5},{4,2},{5,3},{6,0},{7,1},{8,14},{9,15},{10,... | collective-permute-start | bytes 50696 | tf_op jit(solution)/shard_map/ppermute | solution.py:244
  6.2 4.6 %collective-permute-start.1 = (bf16[2,4224]{1,0:T(2,128)(2,1)S(1)}, bf16[2,4224]{1,0:T(2,128)(2,1)S(1)}, u32[]{:S(2)}, u32[]{:S(2)}) collective-permute-start(bf16[2,4224]{1,0:T(2,128)(2,1)S(1)} %row_payload.1.refs_0_), channel_id=1, source_target_pairs={{0,4},{1,5},{2,6},{3,7},{4,0},{5,1},{6,2},{7,3},{8,12},{9,13},{10,... | collective-permute-start | bytes 50696 | tf_op jit(solution)/shard_map/ppermute | solution.py:244
  6.2 4.6 %collective-permute-start = (bf16[2,4224]{1,0:T(2,128)(2,1)S(1)}, bf16[2,4224]{1,0:T(2,128)(2,1)S(1)}, u32[]{:S(2)}, u32[]{:S(2)}) collective-permute-start(bf16[2,4224]{1,0:T(2,128)(2,1)S(1)} %row_payload.1.refs_0_), channel_id=1, source_target_pairs={{0,2},{1,3},{2,0},{3,1},{4,6},{5,7},{6,4},{7,5},{8,10},{9,11},{10,... | collective-permute-start | bytes 50696 | tf_op jit(solution)/shard_map/ppermute | solution.py:244
  10.9 5.9 %collective-permute-start.5 = (bf16[4,2,4224]{2,1,0:T(2,128)(2,1)S(1)}, bf16[4,2,4224]{2,1,0:T(2,128)(2,1)S(1)}, u32[]{:S(2)}, u32[]{:S(2)}) collective-permute-start(bf16[4,2,4224]{2,1,0:T(2,128)(2,1)S(1)} %stacked.1.refs_0_), channel_id=1, source_target_pairs={{0,24},{8,16},{16,8},{24,0},{1,25},{9,17},{17,9},{25,1},{2,26},{10... | collective-permute-start | bytes 202760 | tf_op jit(solution)/shard_map/ppermute | solution.py:244
  13.4 4.3 %collective-permute-start.4 = (bf16[4,2,4224]{2,1,0:T(2,128)(2,1)S(1)}, bf16[4,2,4224]{2,1,0:T(2,128)(2,1)S(1)}, u32[]{:S(2)}, u32[]{:S(2)}) collective-permute-start(bf16[4,2,4224]{2,1,0:T(2,128)(2,1)S(1)} %stacked.1.refs_0_), channel_id=1, source_target_pairs={{0,16},{8,24},{16,0},{24,8},{1,17},{9,25},{17,1},{25,9},{2,18},{10... | collective-permute-start | bytes 202760 | tf_op jit(solution)/shard_map/ppermute | solution.py:244
  13.9 4.3 %collective-permute-start.3 = (bf16[4,2,4224]{2,1,0:T(2,128)(2,1)S(1)}, bf16[4,2,4224]{2,1,0:T(2,128)(2,1)S(1)}, u32[]{:S(2)}, u32[]{:S(2)}) collective-permute-start(bf16[4,2,4224]{2,1,0:T(2,128)(2,1)S(1)} %stacked.1.refs_0_), channel_id=1, source_target_pairs={{0,8},{8,0},{16,24},{24,16},{1,9},{9,1},{17,25},{25,17},{2,10},{10... | collective-permute-start | bytes 202760 | tf_op jit(solution)/shard_map/ppermute | solution.py:244
  14.4 3.8 %collective-permute-start.6 = (bf16[4,2,4224]{2,1,0:T(2,128)(2,1)S(1)}, bf16[4,2,4224]{2,1,0:T(2,128)(2,1)S(1)}, u32[]{:S(2)}, u32[]{:S(2)}) collective-permute-start(bf16[4,2,4224]{2,1,0:T(2,128)(2,1)S(1)} %stacked.1.refs_0_), channel_id=1, source_target_pairs={{0,1},{1,0},{2,3},{3,2},{4,5},{5,4},{6,7},{7,6},{8,9},{9,8},{10,11... | collective-permute-start | bytes 202760 | tf_op jit(solution)/shard_map/ppermute | solution.py:244
  16.8 1.5 %collective-permute-start.9 = (bf16[4,2,4224]{2,1,0:T(2,128)(2,1)S(1)}, bf16[4,2,4224]{2,1,0:T(2,128)(2,1)S(1)}, u32[]{:S(2)}, u32[]{:S(2)}) collective-permute-start(bf16[4,2,4224]{2,1,0:T(2,128)(2,1)S(1)} %collective-permute-done.5.refs_3_), channel_id=1, source_target_pairs={{0,1},{1,0},{2,3},{3,2},{4,5},{5,4},{6,7},{7,6},{8,9},{9,8},{10,11... | collective-permute-start | bytes 202760 | tf_op jit(solution)/shard_map/ppermute | solution.py:244
  17.7 1.3 %collective-permute-start.8 = (bf16[4,2,4224]{2,1,0:T(2,128)(2,1)S(1)}, bf16[4,2,4224]{2,1,0:T(2,128)(2,1)S(1)}, u32[]{:S(2)}, u32[]{:S(2)}) collective-permute-start(bf16[4,2,4224]{2,1,0:T(2,128)(2,1)S(1)} %collective-permute-done.4.refs_2_), channel_id=1, source_target_pairs={{0,1},{1,0},{2,3},{3,2},{4,5},{5,4},{6,7},{7,6},{8,9},{9,8},{10,11... | collective-permute-start | bytes 202760 | tf_op jit(solution)/shard_map/ppermute | solution.py:244
  18.2 1.3 %collective-permute-start.7 = (bf16[4,2,4224]{2,1,0:T(2,128)(2,1)S(1)}, bf16[4,2,4224]{2,1,0:T(2,128)(2,1)S(1)}, u32[]{:S(2)}, u32[]{:S(2)}) collective-permute-start(bf16[4,2,4224]{2,1,0:T(2,128)(2,1)S(1)} %collective-permute-done.3.refs_1_), channel_id=1, source_target_pairs={{0,1},{1,0},{2,3},{3,2},{4,5},{5,4},{6,7},{7,6},{8,9},{9,8},{10,11... | collective-permute-start | bytes 202760 | tf_op jit(solution)/shard_map/ppermute | solution.py:244
  23.5 1.6 %collective-permute-start.10 = (bf16[32,2,2048]{2,1,0:T(2,128)(2,1)S(1)}, bf16[32,2,2048]{2,1,0:T(2,128)(2,1)S(1)}, u32[]{:S(2)}, u32[]{:S(2)}) collective-permute-start(bf16[32,2,2048]{2,1,0:T(2,128)(2,1)S(1)} %get-tuple-element.10), channel_id=1, source_target_pairs={{0,1},{1,0},{2,3},{3,2},{4,5},{5,4},{6,7},{7,6},{8,9},{9,8},{10,11... | collective-permute-start | bytes 786440 | tf_op jit(solution)/shard_map/ppermute | solution.py:244

commit v8 on v7

--- a/solution.py
+++ b/solution.py
@@ -11,7 +11,7 @@
 LANES = 128
 SMALL_VMEM = 2 << 20
 MLP_VMEM = 8 << 20
-MLP_TILE = 512
+MLP_TILE = 1024
 PREFETCH_WINDOW = pl.CostEstimate(flops=64 << 30, transcendentals=0, bytes_accessed=256 << 20)
 AXES = ("grp", "fsdp")
 

time: 39.6 us -> 39.6 us (level)
  no operation moved by 1% of the time
where the time goes in v8:
time: 39.6 us; the launch traced here: 39.5 us
  blocking collectives  13.5 us (34%)
  starting transfers between devices  9.55 us (24%)
  waiting for transfers between devices  9.48 us (24%)
  Pallas kernels  6.81 us (17%)
    all_to_all x1, blocking collectives, every_row(): return row_sum(lax.all_to_all(summed, AXES, 0, 0, tiled=True))  13.5 us
    ppermute x11, starting transfers between devices, exchanged(): return lax.ppermute(value, axis, [(d, d ^ flip) for d in range(size)])  9.55 us
    ppermute x11, waiting for transfers between devices, exchanged(): return lax.ppermute(value, axis, [(d, d ^ flip) for d in range(size)])  9.48 us
    pallas_call x1, Pallas kernels, weighted_parts(): pl.pallas_call(kernel, out_shape=[jax.ShapeDtypeStruct(out_block, jnp.bfl...  3.95 us
    pallas_call x1, Pallas kernels, row_payload(): pl.pallas_call(kernel, out_shape=jax.ShapeDtypeStruct((rows_dev, total),...  1.06 us
    pallas_call x1, Pallas kernels, own_columns(): pl.pallas_call(kernel, out_shape=jax.ShapeDtypeStruct(out_block, jnp.floa...  0.88 us
  transfers between devices with their start and end apart: 11, of which 8 were waited for; matrix products, arithmetic and copies ran while one was open for 0% of the time, Pallas kernels for 2%

profile of v8, /device:TPU:0, one launch (start us, length us, event | category | flops | bytes accessed | tf_op | source)
XLA Modules:
  0.0 39.5 jit_solution(17985848264103503412)
XLA Ops:
  0.0 1.1 %row_payload.1.refs_0_ = bf16[2,4224]{1,0:T(2,128)(2,1)S(1)} custom-call(bf16[2,4096]{1,0:T(2,128)(2,1)} %refs_0_.1, f32[1,4096]{1,0:T(1,128)} %bitcast.10, s32[2,8]{1,0:T(2,128)} %refs_2_.1, bf16[2,8]{1,0:T(2,128)(2,1)} %refs_3_.1), custom_call_target="tpu_custom_call" | custom-call | tf_op jit(solution)/shard_map/row_payload/pallas_call | solution.py:69
  1.1 0.0 slice-start.1
  1.1 0.0 slice-start.3
  1.1 0.0 slice-start.5
  1.1 5.1 %collective-permute-start.2 = (bf16[2,4224]{1,0:T(2,128)(2,1)S(1)}, bf16[2,4224]{1,0:T(2,128)(2,1)S(1)}, u32[]{:S(2)}, u32[]{:S(2)}) collective-permute-start(bf16[2,4224]{1,0:T(2,128)(2,1)S(1)} %row_payload.1.refs_0_), channel_id=1, source_target_pairs={{0,6},{1,7},{2,4},{3,5},{4,2},{5,3},{6,0},{7,1},{8,14},{9,15},{10,... | collective-permute-start | bytes 50696 | tf_op jit(solution)/shard_map/ppermute | solution.py:244
  6.2 0.6 %collective-permute-start = (bf16[2,4224]{1,0:T(2,128)(2,1)S(1)}, bf16[2,4224]{1,0:T(2,128)(2,1)S(1)}, u32[]{:S(2)}, u32[]{:S(2)}) collective-permute-start(bf16[2,4224]{1,0:T(2,128)(2,1)S(1)} %row_payload.1.refs_0_), channel_id=1, source_target_pairs={{0,2},{1,3},{2,0},{3,1},{4,6},{5,7},{6,4},{7,5},{8,10},{9,11},{10,... | collective-permute-start | bytes 50696 | tf_op jit(solution)/shard_map/ppermute | solution.py:244
  6.9 1.1 %collective-permute-done.2.refs_3_ = bf16[2,4224]{1,0:T(2,128)(2,1)S(1)} collective-permute-done((bf16[2,4224]{1,0:T(2,128)(2,1)S(1)}, bf16[2,4224]{1,0:T(2,128)(2,1)S(1)}, u32[]{:S(2)}, u32[]{:S(2)}) %collective-permute-start.2) | collective-permute-done | bytes 16928 | tf_op jit(solution)/shard_map/ppermute | solution.py:244
  8.0 2.9 %collective-permute-done.1.refs_2_ = bf16[2,4224]{1,0:T(2,128)(2,1)S(1)} collective-permute-done((bf16[2,4224]{1,0:T(2,128)(2,1)S(1)}, bf16[2,4224]{1,0:T(2,128)(2,1)S(1)}, u32[]{:S(2)}, u32[]{:S(2)}) %collective-permute-start.1) | collective-permute-done | bytes 16928 | tf_op jit(solution)/shard_map/ppermute | solution.py:244
  10.9 2.5 %collective-permute-start.5 = (bf16[4,2,4224]{2,1,0:T(2,128)(2,1)S(1)}, bf16[4,2,4224]{2,1,0:T(2,128)(2,1)S(1)}, u32[]{:S(2)}, u32[]{:S(2)}) collective-permute-start(bf16[4,2,4224]{2,1,0:T(2,128)(2,1)S(1)} %stacked.1.refs_0_), channel_id=1, source_target_pairs={{0,24},{8,16},{16,8},{24,0},{1,25},{9,17},{17,9},{25,1},{2,26},{10... | collective-permute-start | bytes 202760 | tf_op jit(solution)/shard_map/ppermute | solution.py:244
  13.4 0.5 %collective-permute-start.4 = (bf16[4,2,4224]{2,1,0:T(2,128)(2,1)S(1)}, bf16[4,2,4224]{2,1,0:T(2,128)(2,1)S(1)}, u32[]{:S(2)}, u32[]{:S(2)}) collective-permute-start(bf16[4,2,4224]{2,1,0:T(2,128)(2,1)S(1)} %stacked.1.refs_0_), channel_id=1, source_target_pairs={{0,16},{8,24},{16,0},{24,8},{1,17},{9,25},{17,1},{25,9},{2,18},{10... | collective-permute-start | bytes 202760 | tf_op jit(solution)/shard_map/ppermute | solution.py:244
  13.9 0.5 %collective-permute-start.3 = (bf16[4,2,4224]{2,1,0:T(2,128)(2,1)S(1)}, bf16[4,2,4224]{2,1,0:T(2,128)(2,1)S(1)}, u32[]{:S(2)}, u32[]{:S(2)}) collective-permute-start(bf16[4,2,4224]{2,1,0:T(2,128)(2,1)S(1)} %stacked.1.refs_0_), channel_id=1, source_target_pairs={{0,8},{8,0},{16,24},{24,16},{1,9},{9,1},{17,25},{25,17},{2,10},{10... | collective-permute-start | bytes 202760 | tf_op jit(solution)/shard_map/ppermute | solution.py:244
  14.5 2.3 %collective-permute-done.5.refs_3_ = bf16[4,2,4224]{2,1,0:T(2,128)(2,1)S(1)} collective-permute-done((bf16[4,2,4224]{2,1,0:T(2,128)(2,1)S(1)}, bf16[4,2,4224]{2,1,0:T(2,128)(2,1)S(1)}, u32[]{:S(2)}, u32[]{:S(2)}) %collective-permute-start.5) | collective-permute-done | bytes 67616 | tf_op jit(solution)/shard_map/ppermute | solution.py:244
  16.8 0.9 %collective-permute-done.4.refs_2_ = bf16[4,2,4224]{2,1,0:T(2,128)(2,1)S(1)} collective-permute-done((bf16[4,2,4224]{2,1,0:T(2,128)(2,1)S(1)}, bf16[4,2,4224]{2,1,0:T(2,128)(2,1)S(1)}, u32[]{:S(2)}, u32[]{:S(2)}) %collective-permute-start.4) | collective-permute-done | bytes 67616 | tf_op jit(solution)/shard_map/ppermute | solution.py:244
  17.7 0.5 %collective-permute-done.3.refs_1_ = bf16[4,2,4224]{2,1,0:T(2,128)(2,1)S(1)} collective-permute-done((bf16[4,2,4224]{2,1,0:T(2,128)(2,1)S(1)}, bf16[4,2,4224]{2,1,0:T(2,128)(2,1)S(1)}, u32[]{:S(2)}, u32[]{:S(2)}) %collective-permute-start.3) | collective-permute-done | bytes 67616 | tf_op jit(solution)/shard_map/ppermute | solution.py:244
  18.2 0.0 collective-permute-start.7
  18.2 0.7 %collective-permute-done.8.refs_6_ = bf16[4,2,4224]{2,1,0:T(2,128)(2,1)S(1)} collective-permute-done((bf16[4,2,4224]{2,1,0:T(2,128)(2,1)S(1)}, bf16[4,2,4224]{2,1,0:T(2,128)(2,1)S(1)}, u32[]{:S(2)}, u32[]{:S(2)}) %collective-permute-start.8) | collective-permute-done | bytes 67616 | tf_op jit(solution)/shard_map/ppermute | solution.py:244
  19.0 0.5 %collective-permute-done.7.refs_5_ = bf16[4,2,4224]{2,1,0:T(2,128)(2,1)S(1)} collective-permute-done((bf16[4,2,4224]{2,1,0:T(2,128)(2,1)S(1)}, bf16[4,2,4224]{2,1,0:T(2,128)(2,1)S(1)}, u32[]{:S(2)}, u32[]{:S(2)}) %collective-permute-start.7) | collective-permute-done | bytes 67616 | tf_op jit(solution)/shard_map/ppermute | solution.py:244
  19.5 4.0 %weighted_parts.1 = (bf16[32,2,2048]{2,1,0:T(2,128)(2,1)S(1)}, bf16[64,1024]{1,0:T(8,128)(2,1)S(1)}, f32[64,128]{1,0:T(8,128)S(1)}) custom-call(bf16[4,2,4224]{2,1,0:T(2,128)(2,1)S(1)} %stacked.1.refs_0_, bf16[4,2,4224]{2,1,0:T(2,128)(2,1)S(1)} %collective-permute-done.3.refs_1_, bf16[4,2,4224]{2,1,0:T(2,128)(2,1)S(1)} %collective-permute-done.4.refs_2_, ...), custom_call_target="tpu_custom_call" | custom-call | tf_op jit(solution)/shard_map/weighted_parts/pallas_call | solution.py:146
  23.5 0.2 collective-permute-start.10
  23.7 0.9 %own_columns.1.own_ref = f32[32,2,2048]{2,1,0:T(2,128)S(1)} custom-call(bf16[64,1024]{1,0:T(8,128)(2,1)S(1)} %get-tuple-element.8.hidden_ref, f32[64,128]{1,0:T(8,128)S(1)} %get-tuple-element.9.weight_ref, bf16[1024,4096]{1,0:T(8,128)(2,1)S(1)} %bitcast.6), custom_call_target="tpu_custom_call" | custom-call | flops 268435456 | bytes 4194304 | tf_op jit(solution)/shard_map/own_columns/pallas_call | solution.py:184
  24.6 0.5 %collective-permute-done.10.partner_ref = bf16[32,2,2048]{2,1,0:T(2,128)(2,1)S(1)} collective-permute-done((bf16[32,2,2048]{2,1,0:T(2,128)(2,1)S(1)}, bf16[32,2,2048]{2,1,0:T(2,128)(2,1)S(1)}, u32[]{:S(2)}, u32[]{:S(2)}) %collective-permute-start.10) | collective-permute-done | bytes 262176 | tf_op jit(solution)/shard_map/ppermute | solution.py:244
  25.1 0.2 chip_sum.1
  25.3 13.5 %all_to_all.5.returned_ref = bf16[32,2,2048]{2,1,0:T(2,128)(2,1)S(1)} all-to-all(bf16[32,2,2048]{2,1,0:T(2,128)(2,1)S(1)} %chip_sum.1), channel_id=1, replica_groups=mesh['grp'=4,'fsdp'=8] {'grp','fsdp'}, dimensions={0} | all-to-all | bytes 524288 | tf_op jit(solution)/shard_map/all_to_all | solution.py:261
  38.8 0.7 %row_sum.1 = bf16[2,4096]{1,0:T(2,128)(2,1)} custom-call(bf16[32,2,2048]{2,1,0:T(2,128)(2,1)S(1)} %all_to_all.5.returned_ref), custom_call_target="tpu_custom_call" | custom-call | tf_op jit(solution)/shard_map/row_sum/pallas_call | solution.py:232
  (19 shorter events, 0.0 us)
Async XLA Ops:
  0.0 19.5 %slice-start = ((s8[8388608]{0:T(1024)(128)(4,1)}), s8[4194304]{0:T(1024)(128)(4,1)S(1)}, s32[]{:S(2)}) async-start(s8[8388608]{0:T(1024)(128)(4,1)} %bitcast.3), calls=%async_computation.1 | async-start | bytes 8388608
  0.0 19.5 %slice-start.2 = ((s8[16777216]{0:T(1024)(128)(4,1)}), s8[4194304]{0:T(1024)(128)(4,1)S(1)}, s32[]{:S(2)}) async-start(s8[16777216]{0:T(1024)(128)(4,1)} %bitcast.7), calls=%async_computation.3 | async-start | bytes 8388608
  1.1 18.4 %slice-start.1 = ((s8[8388608]{0:T(1024)(128)(4,1)}), s8[4194304]{0:T(1024)(128)(4,1)S(1)}, s32[]{:S(2)}) async-start(s8[8388608]{0:T(1024)(128)(4,1)} %bitcast.3), calls=%async_computation.2 | async-start | bytes 8388608
  1.1 18.4 %slice-start.3 = ((s8[16777216]{0:T(1024)(128)(4,1)}), s8[4194304]{0:T(1024)(128)(4,1)S(1)}, s32[]{:S(2)}) async-start(s8[16777216]{0:T(1024)(128)(4,1)} %bitcast.7), calls=%async_computation.4 | async-start | bytes 8388608
  1.1 18.4 %slice-start.4 = ((s8[16777216]{0:T(1024)(128)(4,1)}), s8[4194304]{0:T(1024)(128)(4,1)S(1)}, s32[]{:S(2)}) async-start(s8[16777216]{0:T(1024)(128)(4,1)} %bitcast.7), calls=%async_computation.5 | async-start | bytes 8388608
  1.1 18.4 %slice-start.5 = ((s8[16777216]{0:T(1024)(128)(4,1)}), s8[4194304]{0:T(1024)(128)(4,1)S(1)}, s32[]{:S(2)}) async-start(s8[16777216]{0:T(1024)(128)(4,1)} %bitcast.7), calls=%async_computation.6 | async-start | bytes 8388608
  1.1 6.8 %collective-permute-start.2 = (bf16[2,4224]{1,0:T(2,128)(2,1)S(1)}, bf16[2,4224]{1,0:T(2,128)(2,1)S(1)}, u32[]{:S(2)}, u32[]{:S(2)}) collective-permute-start(bf16[2,4224]{1,0:T(2,128)(2,1)S(1)} %row_payload.1.refs_0_), channel_id=1, source_target_pairs={{0,6},{1,7},{2,4},{3,5},{4,2},{5,3},{6,0},{7,1},{8,14},{9,15},{10,... | collective-permute-start | bytes 50696 | tf_op jit(solution)/shard_map/ppermute | solution.py:244
  6.2 4.6 %collective-permute-start.1 = (bf16[2,4224]{1,0:T(2,128)(2,1)S(1)}, bf16[2,4224]{1,0:T(2,128)(2,1)S(1)}, u32[]{:S(2)}, u32[]{:S(2)}) collective-permute-start(bf16[2,4224]{1,0:T(2,128)(2,1)S(1)} %row_payload.1.refs_0_), channel_id=1, source_target_pairs={{0,4},{1,5},{2,6},{3,7},{4,0},{5,1},{6,2},{7,3},{8,12},{9,13},{10,... | collective-permute-start | bytes 50696 | tf_op jit(solution)/shard_map/ppermute | solution.py:244
  6.2 4.6 %collective-permute-start = (bf16[2,4224]{1,0:T(2,128)(2,1)S(1)}, bf16[2,4224]{1,0:T(2,128)(2,1)S(1)}, u32[]{:S(2)}, u32[]{:S(2)}) collective-permute-start(bf16[2,4224]{1,0:T(2,128)(2,1)S(1)} %row_payload.1.refs_0_), channel_id=1, source_target_pairs={{0,2},{1,3},{2,0},{3,1},{4,6},{5,7},{6,4},{7,5},{8,10},{9,11},{10,... | collective-permute-start | bytes 50696 | tf_op jit(solution)/shard_map/ppermute | solution.py:244
  10.9 5.9 %collective-permute-start.5 = (bf16[4,2,4224]{2,1,0:T(2,128)(2,1)S(1)}, bf16[4,2,4224]{2,1,0:T(2,128)(2,1)S(1)}, u32[]{:S(2)}, u32[]{:S(2)}) collective-permute-start(bf16[4,2,4224]{2,1,0:T(2,128)(2,1)S(1)} %stacked.1.refs_0_), channel_id=1, source_target_pairs={{0,24},{8,16},{16,8},{24,0},{1,25},{9,17},{17,9},{25,1},{2,26},{10... | collective-permute-start | bytes 202760 | tf_op jit(solution)/shard_map/ppermute | solution.py:244
  13.4 4.3 %collective-permute-start.4 = (bf16[4,2,4224]{2,1,0:T(2,128)(2,1)S(1)}, bf16[4,2,4224]{2,1,0:T(2,128)(2,1)S(1)}, u32[]{:S(2)}, u32[]{:S(2)}) collective-permute-start(bf16[4,2,4224]{2,1,0:T(2,128)(2,1)S(1)} %stacked.1.refs_0_), channel_id=1, source_target_pairs={{0,16},{8,24},{16,0},{24,8},{1,17},{9,25},{17,1},{25,9},{2,18},{10... | collective-permute-start | bytes 202760 | tf_op jit(solution)/shard_map/ppermute | solution.py:244
  13.9 4.3 %collective-permute-start.3 = (bf16[4,2,4224]{2,1,0:T(2,128)(2,1)S(1)}, bf16[4,2,4224]{2,1,0:T(2,128)(2,1)S(1)}, u32[]{:S(2)}, u32[]{:S(2)}) collective-permute-start(bf16[4,2,4224]{2,1,0:T(2,128)(2,1)S(1)} %stacked.1.refs_0_), channel_id=1, source_target_pairs={{0,8},{8,0},{16,24},{24,16},{1,9},{9,1},{17,25},{25,17},{2,10},{10... | collective-permute-start | bytes 202760 | tf_op jit(solution)/shard_map/ppermute | solution.py:244
  14.4 3.8 %collective-permute-start.6 = (bf16[4,2,4224]{2,1,0:T(2,128)(2,1)S(1)}, bf16[4,2,4224]{2,1,0:T(2,128)(2,1)S(1)}, u32[]{:S(2)}, u32[]{:S(2)}) collective-permute-start(bf16[4,2,4224]{2,1,0:T(2,128)(2,1)S(1)} %stacked.1.refs_0_), channel_id=1, source_target_pairs={{0,1},{1,0},{2,3},{3,2},{4,5},{5,4},{6,7},{7,6},{8,9},{9,8},{10,11... | collective-permute-start | bytes 202760 | tf_op jit(solution)/shard_map/ppermute | solution.py:244
  16.8 1.5 %collective-permute-start.9 = (bf16[4,2,4224]{2,1,0:T(2,128)(2,1)S(1)}, bf16[4,2,4224]{2,1,0:T(2,128)(2,1)S(1)}, u32[]{:S(2)}, u32[]{:S(2)}) collective-permute-start(bf16[4,2,4224]{2,1,0:T(2,128)(2,1)S(1)} %collective-permute-done.5.refs_3_), channel_id=1, source_target_pairs={{0,1},{1,0},{2,3},{3,2},{4,5},{5,4},{6,7},{7,6},{8,9},{9,8},{10,11... | collective-permute-start | bytes 202760 | tf_op jit(solution)/shard_map/ppermute | solution.py:244
  17.7 1.3 %collective-permute-start.8 = (bf16[4,2,4224]{2,1,0:T(2,128)(2,1)S(1)}, bf16[4,2,4224]{2,1,0:T(2,128)(2,1)S(1)}, u32[]{:S(2)}, u32[]{:S(2)}) collective-permute-start(bf16[4,2,4224]{2,1,0:T(2,128)(2,1)S(1)} %collective-permute-done.4.refs_2_), channel_id=1, source_target_pairs={{0,1},{1,0},{2,3},{3,2},{4,5},{5,4},{6,7},{7,6},{8,9},{9,8},{10,11... | collective-permute-start | bytes 202760 | tf_op jit(solution)/shard_map/ppermute | solution.py:244
  18.2 1.3 %collective-permute-start.7 = (bf16[4,2,4224]{2,1,0:T(2,128)(2,1)S(1)}, bf16[4,2,4224]{2,1,0:T(2,128)(2,1)S(1)}, u32[]{:S(2)}, u32[]{:S(2)}) collective-permute-start(bf16[4,2,4224]{2,1,0:T(2,128)(2,1)S(1)} %collective-permute-done.3.refs_1_), channel_id=1, source_target_pairs={{0,1},{1,0},{2,3},{3,2},{4,5},{5,4},{6,7},{7,6},{8,9},{9,8},{10,11... | collective-permute-start | bytes 202760 | tf_op jit(solution)/shard_map/ppermute | solution.py:244
  23.5 1.6 %collective-permute-start.10 = (bf16[32,2,2048]{2,1,0:T(2,128)(2,1)S(1)}, bf16[32,2,2048]{2,1,0:T(2,128)(2,1)S(1)}, u32[]{:S(2)}, u32[]{:S(2)}) collective-permute-start(bf16[32,2,2048]{2,1,0:T(2,128)(2,1)S(1)} %get-tuple-element.10), channel_id=1, source_target_pairs={{0,1},{1,0},{2,3},{3,2},{4,5},{5,4},{6,7},{7,6},{8,9},{9,8},{10,11... | collective-permute-start | bytes 786440 | tf_op jit(solution)/shard_map/ppermute | solution.py:244
